TPU v7x, 32 devices: a whole 2x2x4 slice. The times are simulated.
32 devices in a mesh: lat: 8 (over y, x, core), chan: 4 (over z).
Axes of the slice: x: 2, y: 2, z: 4, core: 2. Of those that a mesh axis runs over, the one named last changes fastest.
Arguments:
- signal: bfloat16 [384, 384, 1440], P('lat', 'chan'), may hold values from -6 to 6
- spectral_filter: float32 [384, 2, 384], replicated, may hold values from -4 to 4
- channel_mix: bfloat16 [2, 384, 384], replicated, may hold values from -0.21875 to 0.21875
Outputs:
- output: bfloat16 [384, 384, 1440], P('lat', 'chan')
All inputs are finite; a program needn't handle non-finite values.
Results may differ from a plain program's by a relative error of at most 0.01.
Values may be sent and summed in bfloat16 or wider, within the bound.
No kernel may reach another device: no remote copies, remote signals or barrier semaphores. Data moves between devices by JAX's collectives and lax.ppermute only.
A program may use at most 192 MiB of HBM per device.

v0:
```python
import math

import jax
import jax.numpy as jnp
from jax import lax
from jax.sharding import PartitionSpec as P

LB = 128


def fourier_tables(orders, lon_count):
    cells = jnp.arange(lon_count, dtype=jnp.int32)
    phase = orders[:, None] * cells[None, :] % lon_count
    angle = phase.astype(jnp.float32) * (2.0 * math.pi / lon_count)
    forward = jnp.stack([jnp.cos(angle), -jnp.sin(angle)], 0)
    factor = jnp.where(orders == 0, 1.0, 2.0).astype(jnp.float32)[None, :, None]
    return (forward.astype(jnp.bfloat16), (forward * factor).astype(jnp.bfloat16))


def latitude_terms(lat_index, lat_total, lon_count):
    theta = (lat_index.astype(jnp.float32) + 0.5) * (math.pi / lat_total)
    weight = jnp.sin(theta) * (2.0 * math.pi * math.pi / (lat_total * lon_count))
    return (jnp.cos(theta), jnp.log(jnp.sin(theta)), weight)


def seed_logs(orders, log_sine):
    order_f = orders.astype(jnp.float32)[:, None]
    base_term = 0.5 * jnp.log((2.0 * order_f + 1.0) / (4.0 * math.pi))
    ratio_term = 0.5 * (
        jax.scipy.special.gammaln(order_f + 0.5)
        - jax.scipy.special.gammaln(order_f + 1.0)
        - 0.5 * math.log(math.pi)
    )
    return base_term + ratio_term + order_f * log_sine[None, :]


def legendre_rows(recursion, orders, log_seeds, first_degree, row_count, cosine):
    order_f = orders.astype(jnp.float32)[:, None]

    def advance(carried, degree):
        previous, earlier, log_scale = carried
        degree_f = degree.astype(jnp.float32)
        degree_gap = degree_f * degree_f - order_f * order_f
        coeff_a = jnp.sqrt((4.0 * degree_f * degree_f - 1.0) / jnp.maximum(degree_gap, 1.0))
        below_sq = (degree_f - 1.0) * (degree_f - 1.0)
        coeff_b = jnp.sqrt(jnp.maximum(below_sq - order_f * order_f, 0.0) / (4.0 * below_sq - 1.0))
        grown = coeff_a * (cosine[None, :] * previous - coeff_b * earlier)
        at_start = degree_f == order_f
        is_above = degree_f > order_f
        fresh_value = jnp.where(at_start, 1.0, jnp.where(is_above, grown, 0.0))
        log_scale = jnp.where(at_start, log_seeds, log_scale)
        scaled_value = fresh_value * jnp.exp(log_scale)
        rescale = jnp.where(degree_f >= order_f, jnp.abs(fresh_value) + jnp.abs(previous), 1.0)
        return (
            (fresh_value / rescale, previous / rescale, log_scale + jnp.log(rescale)),
            scaled_value,
        )

    degrees_here = first_degree + jnp.arange(row_count, dtype=jnp.int32)
    carried, values = lax.scan(advance, recursion, degrees_here, unroll=8)
    return (carried, jnp.moveaxis(values, 0, 1))


def apply_filter(coefficients, gains):
    real_part = coefficients[..., 0, :] * gains[:, 0, :] - coefficients[..., 1, :] * gains[:, 1, :]
    imag_part = coefficients[..., 0, :] * gains[:, 1, :] + coefficients[..., 1, :] * gains[:, 0, :]
    return jnp.stack([real_part, imag_part], -2)


def mix_table(channel_mix):
    real_w = channel_mix[0]
    imag_w = channel_mix[1]
    return jnp.stack([jnp.stack([real_w, imag_w], 1), jnp.stack([-imag_w, real_w], 1)], 0)


def build_legendre(orders, log_sine, cosine, first_block, degrees, lat_total):
    slot_count = orders.shape[0]
    log_seeds = seed_logs(orders, log_sine)
    zero_state = jnp.zeros((slot_count, lat_total), jnp.float32)
    empty_table = jnp.zeros((slot_count, degrees, lat_total), jnp.bfloat16)

    def build_advance_block(block_index, carried):
        recursion, legendre = carried
        recursion, block_rows = legendre_rows(
            recursion, orders, log_seeds, block_index * LB, LB, cosine
        )
        legendre = lax.dynamic_update_slice_in_dim(
            legendre, block_rows.astype(jnp.bfloat16), block_index * LB, 1
        )
        return (recursion, legendre)

    start_carry = ((zero_state, zero_state, zero_state), empty_table)
    return lax.fori_loop(first_block, degrees // LB, build_advance_block, start_carry)[1]


def analyse_rows(legendre, fourier_part, first_block, degrees):
    slot_count = legendre.shape[0]
    channel_count = fourier_part.shape[3]
    empty_sum = jnp.zeros((slot_count, degrees, 2, channel_count), jnp.float32)

    def analyse_advance_block(block_index, summed):
        block_rows = lax.dynamic_slice_in_dim(legendre, block_index * LB, LB, 1)
        partial_sum = jnp.einsum(
            "glj,gjtc->gltc", block_rows, fourier_part, preferred_element_type=jnp.float32
        )
        return lax.dynamic_update_slice_in_dim(summed, partial_sum, block_index * LB, 1)

    return lax.fori_loop(first_block, degrees // LB, analyse_advance_block, empty_sum)


def synthesise_rows(legendre, mixed_part, first_block, degrees):
    slot_count, _, lat_total = legendre.shape
    channel_count = mixed_part.shape[3]
    empty_sum = jnp.zeros((slot_count, lat_total, 2, channel_count), jnp.float32)

    def synthesise_advance_block(block_index, summed):
        block_rows = lax.dynamic_slice_in_dim(legendre, block_index * LB, LB, 1)
        block_values = lax.dynamic_slice_in_dim(mixed_part, block_index * LB, LB, 1)
        return summed + jnp.einsum(
            "glj,gltc->gjtc", block_rows, block_values, preferred_element_type=jnp.float32
        )

    return lax.fori_loop(first_block, degrees // LB, synthesise_advance_block, empty_sum)


def on_device(signal, spectral_filter, channel_mix):
    lat_count = lax.axis_size("lat")
    chan_count = lax.axis_size("chan")
    lat_rows, quarter, lon_count = signal.shape
    lat_total = lat_rows * lat_count
    degrees = spectral_filter.shape[0]
    full_channels = channel_mix.shape[1]
    per_dev = degrees // lat_count
    sub_count = per_dev // chan_count
    lat_index = lax.axis_index("lat")
    chan_index = lax.axis_index("chan")
    every_slot = jnp.arange(degrees, dtype=jnp.int32)
    dest_dev = every_slot // per_dev
    slot_index = every_slot % per_dev
    own_slots = chan_index * sub_count + jnp.arange(sub_count, dtype=jnp.int32)
    orders_all = dest_dev * per_dev + slot_index
    orders_own = lat_index * per_dev + own_slots
    trig, synth = fourier_tables(orders_all, lon_count)
    own_rows = lat_index * lat_rows + jnp.arange(lat_rows, dtype=jnp.int32)
    _, _, own_weight = latitude_terms(own_rows, lat_total, lon_count)
    spectrum = jnp.einsum("acn,tkn->katc", signal, trig, preferred_element_type=jnp.float32)
    spectrum = (spectrum * own_weight[None, :, None, None]).astype(jnp.bfloat16)
    fourier = lax.all_to_all(
        lax.all_to_all(spectrum, "lat", split_axis=0, concat_axis=1, tiled=True),
        "chan",
        split_axis=0,
        concat_axis=3,
        tiled=True,
    )
    cosine, log_sine, _ = latitude_terms(
        jnp.arange(lat_total, dtype=jnp.int32), lat_total, lon_count
    )
    slot_total = orders_own.shape[0]
    first_end = slot_total // 2
    bounds = [(0, first_end), (first_end, slot_total)]
    tables = []
    first_blocks = []
    filtered_parts = []
    for start_slot, end_slot in bounds:
        group_orders = orders_own[start_slot:end_slot]
        first_block = jnp.min(group_orders) // LB
        legendre = build_legendre(group_orders, log_sine, cosine, first_block, degrees, lat_total)
        fourier_part = fourier[start_slot:end_slot]
        coefficients = analyse_rows(legendre, fourier_part, first_block, degrees)
        filtered_parts.append(apply_filter(coefficients, spectral_filter).astype(jnp.bfloat16))
        tables.append(legendre)
        first_blocks.append(first_block)
    filtered = jnp.concatenate(filtered_parts, 0)
    kernel = mix_table(channel_mix)
    flat_kernel = kernel.reshape(2 * full_channels, 2 * full_channels)
    mixed = jnp.dot(
        filtered.reshape(slot_total * degrees, 2 * full_channels),
        flat_kernel,
        preferred_element_type=jnp.float32,
    )
    mixed = mixed.astype(jnp.bfloat16).reshape(slot_total, degrees, 2, full_channels)
    back_parts = []
    for group_index in range(len(bounds)):
        start_slot, end_slot = bounds[group_index]
        mixed_part = mixed[start_slot:end_slot]
        back_parts.append(
            synthesise_rows(tables[group_index], mixed_part, first_blocks[group_index], degrees)
        )
    back = jnp.concatenate(back_parts, 0).astype(jnp.bfloat16)
    back = lax.all_to_all(back, "chan", split_axis=3, concat_axis=0, tiled=True)
    returned = lax.all_to_all(back, "lat", split_axis=1, concat_axis=0, tiled=True)
    output = jnp.einsum("katc,tkn->acn", returned, synth, preferred_element_type=jnp.float32)
    return output.astype(jnp.bfloat16)


def solution(mesh):
    return jax.shard_map(
        on_device,
        mesh=mesh,
        in_specs=(P("lat", "chan", None), P(), P()),
        out_specs=P("lat", "chan", None),
        check_vma=False,
    )
```

profile of v0, /device:TPU:8, one launch (start us, length us, event | category | flops | bytes accessed | tf_op | source)
XLA Modules:
  0.0 1339.6 jit_solution(16196962002320569169)
XLA Ops:
  0.0 10.2 fusion.40
  10.3 17.6 %fusion.27 = bf16[384,48,2,96]{0,3,1,2:T(8,128)(2,1)} fusion(f32[48]{0:T(128)S(1)} %sine_multiply_fusion, bf16[48,96,1440]{2,1,0:T(8,128)(2,1)} %param.19, f32[1,384,1440]{1,2,0:T(8,128)} %get-tuple-element.1470, f32[1,384,1440]{1,2,0:T(8,128)S(1)} %get-tuple-element.1469), kind=kOutput, calls=%fused_computation.192 | convolution fusion | flops 10203660288 | bytes 24772800 | tf_op jit(solution)/shard_map/acn,tkn->katc/dot_general | solution.py:146
  27.9 11.8 copy.33
  48.6 331.1 %while.159 = (s32[]{:T(128)}, f32[6,384]{1,0:T(8,128)S(1)}, f32[6,384]{1,0:T(8,128)S(1)}, f32[6,384]{1,0:T(8,128)S(1)}, bf16[6,384,384]{2,0,1:T(8,128)(2,1)S(1)}...) while((s32[]{:T(128)}, f32[6,384]{1,0:T(8,128)S(1)}, ...), condition=%wide.region_4.5_spmd.clone.clone, body=%wide.region_1.4_spmd.clone.clone.sunk | while | flops 430591 | bytes 2527546 | solution.py:93
  48.8 110.0 %while.162 = (s32[]{:T(128)}, f32[6,384]{1,0:T(8,128)S(1)}, f32[6,384]{1,0:T(8,128)S(1)}, f32[6,384]{1,0:T(8,128)S(1)}, bf16[16,8,6,384]{3,2,1,0:T(8,128)(2,1)S(...) while((s32[]{:T(128)}, f32[6,384]{1,0:T(8,128)S(1)}, ...), condition=%wide.region_3.3_spmd.clone, body=%wide.region_2.2_spmd.clone.sunk | while | flops 424441 | bytes 941511 | solution.py:60
  159.1 110.0 %while.162 = (s32[]{:T(128)}, f32[6,384]{1,0:T(8,128)S(1)}, f32[6,384]{1,0:T(8,128)S(1)}, f32[6,384]{1,0:T(8,128)S(1)}, bf16[16,8,6,384]{3,2,1,0:T(8,128)(2,1)S(...) while((s32[]{:T(128)}, f32[6,384]{1,0:T(8,128)S(1)}, ...), condition=%wide.region_3.3_spmd.clone, body=%wide.region_2.2_spmd.clone.sunk | while | flops 424441 | bytes 941511 | solution.py:60
  269.5 110.0 %while.162 = (s32[]{:T(128)}, f32[6,384]{1,0:T(8,128)S(1)}, f32[6,384]{1,0:T(8,128)S(1)}, f32[6,384]{1,0:T(8,128)S(1)}, bf16[16,8,6,384]{3,2,1,0:T(8,128)(2,1)S(...) while((s32[]{:T(128)}, f32[6,384]{1,0:T(8,128)S(1)}, ...), condition=%wide.region_3.3_spmd.clone, body=%wide.region_2.2_spmd.clone.sunk | while | flops 424441 | bytes 941511 | solution.py:60
  382.5 10.2 copy.34
  392.7 11.4 copy.35
  409.8 321.1 %while.161 = (s32[]{:T(128)}, f32[6,384]{1,0:T(8,128)S(1)}, f32[6,384]{1,0:T(8,128)S(1)}, f32[6,384]{1,0:T(8,128)S(1)}, bf16[6,384,384]{2,0,1:T(8,128)(2,1)S(1)}...) while((s32[]{:T(128)}, f32[6,384]{1,0:T(8,128)S(1)}, ...), condition=%wide.region_11.12_spmd.clone.clone, body=%wide.region_8.11_spmd.clone.clone.sunk | while | flops 430591 | bytes 2527546 | solution.py:93
  410.4 106.5 %while.163 = (s32[]{:T(128)}, f32[6,384]{1,0:T(8,128)S(1)}, f32[6,384]{1,0:T(8,128)S(1)}, f32[6,384]{1,0:T(8,128)S(1)}, bf16[16,8,6,384]{3,2,1,0:T(8,128)(2,1)S(...) while((s32[]{:T(128)}, f32[6,384]{1,0:T(8,128)S(1)}, ...), condition=%wide.region_10.10_spmd.clone, body=%wide.region_9.9_spmd.clone.sunk | while | flops 424441 | bytes 941511 | solution.py:60
  517.2 106.5 %while.163 = (s32[]{:T(128)}, f32[6,384]{1,0:T(8,128)S(1)}, f32[6,384]{1,0:T(8,128)S(1)}, f32[6,384]{1,0:T(8,128)S(1)}, bf16[16,8,6,384]{3,2,1,0:T(8,128)(2,1)S(...) while((s32[]{:T(128)}, f32[6,384]{1,0:T(8,128)S(1)}, ...), condition=%wide.region_10.10_spmd.clone, body=%wide.region_9.9_spmd.clone.sunk | while | flops 424441 | bytes 941511 | solution.py:60
  624.1 106.5 %while.163 = (s32[]{:T(128)}, f32[6,384]{1,0:T(8,128)S(1)}, f32[6,384]{1,0:T(8,128)S(1)}, f32[6,384]{1,0:T(8,128)S(1)}, bf16[16,8,6,384]{3,2,1,0:T(8,128)(2,1)S(...) while((s32[]{:T(128)}, f32[6,384]{1,0:T(8,128)S(1)}, ...), condition=%wide.region_10.10_spmd.clone, body=%wide.region_9.9_spmd.clone.sunk | while | flops 424441 | bytes 941511 | solution.py:60
  763.6 9.8 while.154
  785.8 9.9 while.155
  803.2 68.3 %copy.44 = bf16[12,384,2,384]{3,2,1,0:T(2,128)(2,1)S(1)} copy(bf16[12,384,2,384]{3,1,2,0:T(8,128)(2,1)S(1)} %maximum_maximum_fusion) | data formatting | bytes 14155776 | tf_op jit(solution)/shard_map/concatenate | solution.py:173
  893.6 24.2 %while.156 = (s32[]{:T(128)}, f32[6,384,2,384]{3,1,2,0:T(8,128)}, bf16[6,384,384]{1,2,0:T(8,128)(2,1)}, bf16[6,384,2,384]{3,2,1,0:T(2,128)(2,1)S(1)}, s32[]{:T(128)}, /*index=5*/s32[]{:T(128)}, s32[]{:T(128)}, s32[]{:T(128)}) while((s32[]{:T(128)}, f32[6,384,2,384]{3,1,2,0:T(8,128)}, bf16[6,384,384]{1,2,0:T(8,128)(2,1)}, ...), condition=%wide.region_15.16_spmd, body=%wide.region_14.15_spmd.sunk | while | flops 454754304 | bytes 18284684 | solution.py:123
  894.4 7.3 convolution_add_fusion.4
  902.5 7.3 convolution_add_fusion.4
  910.6 7.3 convolution_add_fusion.4
  917.8 12.9 copy.48
  941.0 24.4 %while.157 = (s32[]{:T(128)}, f32[6,384,2,384]{3,1,2,0:T(8,128)}, bf16[6,384,384]{1,2,0:T(8,128)(2,1)}, bf16[6,384,2,384]{3,2,1,0:T(2,128)(2,1)S(1)}, s32[]{:T(128)}, /*index=5*/s32[]{:T(128)}, s32[]{:T(128)}, s32[]{:T(128)}) while((s32[]{:T(128)}, f32[6,384,2,384]{3,1,2,0:T(8,128)}, bf16[6,384,384]{1,2,0:T(8,128)(2,1)}, ...), condition=%wide.region_17.18_spmd, body=%wide.region_16.17_spmd.sunk | while | flops 454754304 | bytes 18284684 | solution.py:123
  942.0 7.3 convolution_add_fusion.5
  950.1 7.3 convolution_add_fusion.5
  965.4 13.1 copy.51
  978.5 18.3 %pad_maximum_fusion = bf16[12,384,2,384]{1,2,0,3:T(2,128)(2,1)S(1)} fusion(bf16[6,384,2,384]{1,2,0,3:T(2,128)(2,1)} %copy.51, bf16[6,384,2,384]{1,2,0,3:T(2,128)(2,1)S(1)} %copy-done.1), kind=kLoop, calls=%fused_computation.194 | loop fusion | flops 3538944 | bytes 14155776 | tf_op jit(solution)/shard_map/concatenate | solution.py:189
  996.8 158.8 %all_to_all.69 = bf16[12,384,2,384]{1,2,0,3:T(2,128)(2,1)S(1)} all-to-all(bf16[12,384,2,384]{1,2,0,3:T(2,128)(2,1)S(1)} %pad_maximum_fusion), channel_id=1, replica_groups=mesh['lat'=8,'chan'=4] {'chan'}, dimensions={3} | all-to-all | bytes 14155776 | tf_op jit(solution)/shard_map/all_to_all | solution.py:190
  1161.1 20.6 %copy.54 = bf16[48,384,2,96]{3,2,0,1:T(2,128)(2,1)} copy(bf16[48,384,2,96]{1,3,2,0:T(8,128)(2,1)} %bitcast.405) | data formatting | bytes 14155776 | tf_op jit(solution)/shard_map/all_to_all | solution.py:190
  1186.8 105.3 %all-to-all-done.3 = bf16[48,384,2,96]{3,2,0,1:T(2,128)(2,1)} async-done(((bf16[48,384,2,96]{3,2,0,1:T(2,128)(2,1)}), bf16[48,384,2,96]{3,2,0,1:T(2,128)(2,1)}, u32[]{:S(2)}, u32[]{:S(2)}) %all-to-all-start.3) | async-done | bytes 7077920 | tf_op jit(solution)/shard_map/all_to_all | solution.py:191
  1292.1 11.1 copy.55
  1303.2 9.3 copy.56
  1312.5 26.7 %bitcast_convert_fusion = bf16[48,96,1440]{2,1,0:T(8,128)(2,1)} fusion(bf16[384,48,2,96]{3,1,2,0:T(8,128)(2,1)} %bitcast.410, f32[1,384,1440]{1,2,0:T(8,128)} %get-tuple-element.1470, f32[1,384,1440]{1,2,0:T(8,128)S(1)} %copy-done.3, f32[384]{0:T(512)S(1)} %compare_select_fusion.4), kind=kOutput, calls=%fused_computation.186 | convolution fusion | flops 10202112000 | bytes 24774144 | tf_op jit(solution)/shard_map/katc,tkn->acn/dot_general | solution.py:192
  (1545 shorter events, 305.3 us)
Async XLA Ops:
  10.2 17.7 %copy-start.2 = (f32[1,384,1440]{1,2,0:T(8,128)}, f32[1,384,1440]{1,2,0:T(8,128)S(1)}, u32[]{:S(2)}) copy-start(f32[1,384,1440]{1,2,0:T(8,128)S(1)} %get-tuple-element.1469) | copy-start | bytes 6635524
  39.7 342.8 %all-to-all-start = ((bf16[384,48,2,96]{3,1,2,0:T(8,128)(2,1)}), bf16[384,48,2,96]{3,1,2,0:T(8,128)(2,1)}, u32[]{:S(2)}, u32[]{:S(2)}) async-start(bf16[384,48,2,96]{3,1,2,0:T(8,128)(2,1)} %copy.33), calls=%async_computation | async-start | bytes 18874368 | tf_op jit(solution)/shard_map/all_to_all | solution.py:149
  379.7 13.1 copy-start
  404.1 343.0 %all-to-all-start.1 = ((bf16[48,384,2,96]{1,3,2,0:T(8,128)(2,1)}), bf16[48,384,2,96]{1,3,2,0:T(8,128)(2,1)}, u32[]{:S(2)}, u32[]{:S(2)}) async-start(bf16[48,384,2,96]{1,3,2,0:T(8,128)(2,1)} %copy.35), calls=%async_computation.1 | async-start | bytes 14155776 | tf_op jit(solution)/shard_map/all_to_all | solution.py:148
  738.2 4.1 copy-start.4
  742.5 2.6 copy-start.5
  965.4 13.1 copy-start.1
  1181.7 110.4 %all-to-all-start.3 = ((bf16[48,384,2,96]{3,2,0,1:T(2,128)(2,1)}), bf16[48,384,2,96]{3,2,0,1:T(2,128)(2,1)}, u32[]{:S(2)}, u32[]{:S(2)}) async-start(bf16[48,384,2,96]{3,2,0,1:T(2,128)(2,1)} %copy.54), calls=%async_computation.3 | async-start | bytes 18874368 | tf_op jit(solution)/shard_map/all_to_all | solution.py:191
  1303.2 9.3 copy-start.3
where the time goes:
time: 1360 us; the launch traced here: 1340 us
  loops' own time  486 us (36%)
  local copies, waits for them, and re-layouts  318 us (23%)
  blocking collectives  159 us (12%)
  other arithmetic  135 us (10%)
  matrix products  115 us (8%)
  waiting for transfers between devices  105 us (8%)
  starting transfers between devices  15.5 us (1%)
    another operation x6, loops' own time, legendre_rows(): carried, values = lax.scan(advance, recursion, degrees_here, unroll=8)  485 us
    all_to_all x1, blocking collectives, on_device(): back = lax.all_to_all(back, 'chan', split_axis=3, concat_axis=0, tiled=True)  159 us
    all_to_all x1, waiting for transfers between devices, on_device(): lax.all_to_all(back, 'lat', split_axis=1, concat_axis=0, tiled=True)  105 us
    while x672, other arithmetic  68.7 us
    concatenate x1, local copies, waits for them, and re-layouts, on_device(): filtered = jnp.concatenate(filtered_parts, 0)  68.3 us
    slice x96, local copies, waits for them, and re-layouts, legendre_rows(): carried, values = lax.scan(advance, recursion, degrees_here, unroll=8)  58.7 us
    dot_general x6, matrix products, synthesise_advance_block(): jnp.einsum('glj,gltc->gjtc', block_rows, block_values, preferred_element_...  43.5 us
    while x4, local copies, waits for them, and re-layouts, synthesise_rows(): lax.fori_loop(first_block, degrees // LB, synthesise_advance_block, empty...  32.8 us
  transfers between devices with their start and end apart: 3, of which 1 were waited for; matrix products, arithmetic and copies ran while one was open for 14% of the time, Pallas kernels for 0%

commit v1 on v0

v1 whole, which is shorter than its diff:
```python
import functools
import math

import jax
import jax.numpy as jnp
import numpy as np
from jax import lax
from jax.experimental import pallas as pl
from jax.experimental.pallas import tpu as pltpu
from jax.sharding import PartitionSpec as P

F32 = jnp.float32
BF16 = jnp.bfloat16
VMEM_BYTES = 56 << 20
STEP = 16


def params(**kw):
    return pltpu.CompilerParams(vmem_limit_bytes=VMEM_BYTES, **kw)


def fourier_tables(orders, lon_count):
    cells = jnp.arange(lon_count, dtype=jnp.int32)
    phase = orders[:, None] * cells[None, :] % lon_count
    angle = phase.astype(F32) * (2.0 * math.pi / lon_count)
    forward = jnp.stack([jnp.cos(angle), -jnp.sin(angle)], 0)
    factor = jnp.where(orders == 0, 1.0, 2.0).astype(F32)[None, :, None]
    return (forward.astype(BF16), (forward * factor).astype(BF16))


def latitude_terms(lat_index, lat_total, lon_count):
    theta = (lat_index.astype(F32) + 0.5) * (math.pi / lat_total)
    weight = jnp.sin(theta) * (2.0 * math.pi * math.pi / (lat_total * lon_count))
    return (jnp.cos(theta), jnp.log(jnp.sin(theta)), weight)


def seed_logs(orders, log_sine):
    order_f = orders.astype(F32)[:, None]
    base_term = 0.5 * jnp.log((2.0 * order_f + 1.0) / (4.0 * math.pi))
    ratio_term = 0.5 * (
        jax.scipy.special.gammaln(order_f + 0.5)
        - jax.scipy.special.gammaln(order_f + 1.0)
        - 0.5 * math.log(math.pi)
    )
    return base_term + ratio_term + order_f * log_sine[None, :]


def table_body(group_rows, seeds_ref, order_ref, cosine_ref, out_ref, rows_ref):
    degrees = out_ref.shape[2]
    lat_total = out_ref.shape[3]
    slots = seeds_ref.shape[0]
    per_step = slots // 2
    first = pl.program_id(0) * (per_step * group_rows)
    first_block = first // STEP
    blank = jnp.zeros((STEP, lat_total), out_ref.dtype)

    @pl.loop(0, first_block)
    def _(block):
        at = pl.multiple_of(block * STEP, STEP)
        for slot in range(slots):
            out_ref[slot // 2, slot % 2, pl.ds(at, STEP), :] = blank

    order = order_ref[:, :128]
    order_sq = order * order
    cosine = jnp.broadcast_to(cosine_ref[...], (slots, lat_total))
    wide = lat_total // 128

    def spread(x):
        return jnp.concatenate([x] * wide, axis=1)

    seeds = seeds_ref[...]
    zero = jnp.zeros((slots, lat_total), F32)
    start = (zero, zero, seeds, jnp.zeros((slots, 128), F32))

    def advance(block, carry):
        fresh, before, log_scale, coeff_b = carry
        at = pl.multiple_of(block * STEP, STEP)
        for half in range(STEP // 8):
            scale = jnp.exp(log_scale)
            for step in range(8):
                degree = (at + half * 8 + step).astype(F32)
                degree_v = jnp.full((slots, 128), degree, F32)
                degree_sq = degree_v * degree_v
                ratio = jnp.maximum(degree_sq - order_sq, 1.0) / jnp.maximum(4.0 * degree_sq - 1.0, 1.0)
                root = lax.rsqrt(ratio)
                root = root * (1.5 - 0.5 * ratio * root * root)
                starts = jnp.where(degree_v == order, 1.0, 0.0)
                grown = spread(root) * (cosine * fresh - spread(coeff_b) * before) + spread(starts)
                coeff_b = ratio * root
                before, fresh = fresh, grown
                rows_ref[half * 8 + step] = grown * scale
            size = jnp.abs(fresh) + jnp.abs(before)
            size = jnp.where(size == 0.0, 1.0, size)
            inverse = 1.0 / size
            fresh = fresh * inverse
            before = before * inverse
            log_scale = log_scale + jnp.log(size)
        for slot in range(slots):
            out_ref[slot // 2, slot % 2, pl.ds(at, STEP), :] = rows_ref[:, slot, :].astype(out_ref.dtype)
        return (fresh, before, log_scale, coeff_b)

    lax.fori_loop(first_block, degrees // STEP, advance, start)


def legendre_table(seeds, orders_f, cosine, group_rows, degrees):
    order_count, lat_total = seeds.shape
    groups = order_count // 2
    per_step = math.gcd(groups, 4)
    slots = 2 * per_step
    order_wide = jnp.broadcast_to(orders_f[:, None], (order_count, 128))
    steps = groups // per_step
    seeds = seeds.reshape(steps, slots, lat_total)
    order_wide = order_wide.reshape(steps, slots, 128)
    return pl.pallas_call(
        functools.partial(table_body, group_rows),
        grid=(steps,),
        in_specs=[
            pl.BlockSpec((None, slots, lat_total), lambda i: (i, 0, 0)),
            pl.BlockSpec((None, slots, 128), lambda i: (i, 0, 0)),
            pl.BlockSpec((1, lat_total), lambda i: (0, 0)),
        ],
        out_specs=pl.BlockSpec((per_step, 2, degrees, lat_total), lambda i: (i, 0, 0, 0)),
        out_shape=jax.ShapeDtypeStruct((groups, 2, degrees, lat_total), BF16),
        scratch_shapes=[pltpu.VMEM((STEP, slots, lat_total), F32)],
        compiler_params=params(),
        cost_estimate=pl.CostEstimate(
            flops=40_000_000, transcendentals=0, bytes_accessed=groups * 2 * degrees * lat_total * 2
        ),
        name="legendre_table",
    )(seeds, order_wide, cosine[None, :])


def lane_is_second(rows, lanes):
    lane = lax.broadcasted_iota(jnp.int32, (rows, lanes), 1)
    half = lanes // 2
    quarter = lanes // 4
    inner = jnp.where(lane >= half, lane - half, lane)
    return inner >= quarter


def analyse_body(plan, count_ref, chan_ref, fourier_ref, table_ref, gain_ref, cross_ref, *refs):
    outs, packed = refs[:-1], refs[-1]
    step = pl.program_id(0)
    degrees = table_ref.shape[1]
    lanes = fourier_ref.shape[-1]
    part = plan["part"]
    start = pl.multiple_of(count_ref[step], STEP)

    @pl.when(step == 0)
    def _():
        tail = plan["pad"] + plan["rows"]
        left = packed.shape[0] - tail
        if left:
            packed[tail:, :] = jnp.zeros((left, lanes), packed.dtype)

    rows_in = fourier_ref[...].reshape(table_ref.shape[2], lanes)
    even = jnp.dot(table_ref[0], rows_in, preferred_element_type=F32)
    odd = jnp.dot(table_ref[1], rows_in, preferred_element_type=F32)
    both = jnp.where(lane_is_second(degrees, lanes), odd, even)
    swapped = pltpu.roll(both, lanes // 2, 1)
    kept = both * gain_ref[...] + swapped * cross_ref[...]
    packed[pl.ds(start, degrees), :] = kept.astype(packed.dtype)

    @pl.when(step == pl.num_programs(0) - 1)
    def _():
        for shift, out in enumerate(outs):
            owner = lax.rem(chan_ref[0] + shift, len(outs))
            at = pl.multiple_of(plan["pad"] + owner * part, STEP)
            out[...] = packed[pl.ds(at, part), :]


def chunk_plan(groups, group_rows, degrees, chan_count):
    sizes = [degrees - group_rows * g for g in groups]
    offsets = [sum(sizes[:i]) for i in range(len(groups))]
    rows = sum(sizes)
    unit = STEP * chan_count
    total = -(-rows // unit) * unit
    pad = max([group_rows * g - o for g, o in zip(groups, offsets)] + [0])
    pad = -(-pad // STEP) * STEP
    starts = [pad + o - group_rows * g for g, o in zip(groups, offsets)]
    return {
        "groups": groups, "rows": rows, "total": total, "part": total // chan_count,
        "pad": pad, "starts": starts,
    }


def analyse(plan, chan, fourier, table, gain, cross, chan_count):
    bands, count, band_rows, lanes = fourier.shape
    _, _, degrees, lat_total = table.shape
    first = plan["groups"][0]
    last = plan["groups"][-1]
    starts = jnp.asarray(np.array(plan["starts"][::-1], np.int32))
    spec = pltpu.PrefetchScalarGridSpec(
        num_scalar_prefetch=2,
        grid=(count,),
        in_specs=[
            pl.BlockSpec((bands, None, band_rows, lanes), lambda i, s, c: (0, count - 1 - i, 0, 0)),
            pl.BlockSpec((None, 2, degrees, lat_total), lambda i, s, c: (last - i, 0, 0, 0)),
            pl.BlockSpec((degrees, lanes), lambda i, s, c: (0, 0)),
            pl.BlockSpec((degrees, lanes), lambda i, s, c: (0, 0)),
        ],
        out_specs=[pl.BlockSpec((plan["part"], lanes), lambda i, s, c: (0, 0))] * chan_count,
        scratch_shapes=[pltpu.VMEM((plan["pad"] + plan["total"], lanes), BF16)],
    )
    return pl.pallas_call(
        functools.partial(analyse_body, plan),
        grid_spec=spec,
        out_shape=[jax.ShapeDtypeStruct((plan["part"], lanes), BF16)] * chan_count,
        compiler_params=params(),
        cost_estimate=pl.CostEstimate(
            flops=count * 4 * degrees * lat_total * lanes,
            transcendentals=0,
            bytes_accessed=count * (2 * degrees * lat_total + lat_total * lanes) * 2 + plan["total"] * lanes * 2,
        ),
        name="analyse",
    )(starts, chan, fourier, table, gain, cross)


def mix_body(chan_count, *refs):
    ins, kernel_ref, outs = refs[:chan_count], refs[chan_count], refs[chan_count + 1:]
    gathered = jnp.concatenate([r[...] for r in ins], axis=1)
    for shift, out in enumerate(outs):
        out[...] = jnp.dot(gathered, kernel_ref[shift], preferred_element_type=F32).astype(out.dtype)


def mix(parts, kernel):
    chan_count = len(parts)
    rows, lanes = parts[0].shape
    return pl.pallas_call(
        functools.partial(mix_body, chan_count),
        out_shape=[jax.ShapeDtypeStruct((rows, lanes), BF16)] * chan_count,
        compiler_params=params(),
        cost_estimate=pl.CostEstimate(
            flops=2 * rows * (chan_count * lanes) ** 2,
            transcendentals=0,
            bytes_accessed=(chan_count * lanes) ** 2 * 2 + 4 * chan_count * rows * lanes,
        ),
        name="mix",
    )(*parts, kernel)


def synthesise_body(plan, count_ref, chan_ref, table_ref, *refs):
    chan_count = plan["total"] // plan["part"]
    ins, out_ref, packed = refs[:chan_count], refs[chan_count], refs[chan_count + 1]
    step = pl.program_id(0)
    degrees, lat_total = table_ref.shape[1:]
    lanes = packed.shape[1]
    part = plan["part"]

    @pl.when(step == 0)
    def _():
        for shift, part_ref in enumerate(ins):
            owner = lax.rem(chan_ref[0] + (chan_count - shift), chan_count)
            at = pl.multiple_of(plan["pad"] + owner * part, STEP)
            packed[pl.ds(at, part), :] = part_ref[...]

    start = pl.multiple_of(count_ref[0, step], STEP)
    below = count_ref[1, step]
    rows = packed[pl.ds(start, degrees), :]
    held = lax.broadcasted_iota(jnp.int32, rows.shape, 0) >= below
    rows = jnp.where(held, rows, jnp.zeros_like(rows))
    dims = (((0,), (0,)), ((), ()))
    even = lax.dot_general(table_ref[0], rows, dims, preferred_element_type=F32)
    odd = lax.dot_general(table_ref[1], rows, dims, preferred_element_type=F32)
    both = jnp.where(lane_is_second(lat_total, lanes), odd, even)
    out_ref[...] = both.astype(out_ref.dtype).reshape(out_ref.shape)


def synthesise(plan, chan, table, parts, bands):
    _, _, degrees, lat_total = table.shape
    count = len(plan["groups"])
    first = plan["groups"][0]
    chan_count = len(parts)
    part, lanes = parts[0].shape
    band_rows = lat_total // bands
    group_rows = plan["group_rows"]
    numbers = jnp.asarray(
        np.array([plan["starts"], [group_rows * g for g in plan["groups"]]], np.int32)
    )
    spec = pltpu.PrefetchScalarGridSpec(
        num_scalar_prefetch=2,
        grid=(count,),
        in_specs=[pl.BlockSpec((None, 2, degrees, lat_total), lambda i, s, c: (first + i, 0, 0, 0))]
        + [pl.BlockSpec((part, lanes), lambda i, s, c: (0, 0))] * chan_count,
        out_specs=pl.BlockSpec((bands, None, band_rows, lanes), lambda i, s, c: (0, i, 0, 0)),
        scratch_shapes=[pltpu.VMEM((plan["pad"] + plan["total"], lanes), BF16)],
    )
    return pl.pallas_call(
        functools.partial(synthesise_body, plan),
        grid_spec=spec,
        out_shape=jax.ShapeDtypeStruct((bands, count, band_rows, lanes), BF16),
        compiler_params=params(),
        cost_estimate=pl.CostEstimate(
            flops=count * 4 * degrees * lat_total * lanes,
            transcendentals=0,
            bytes_accessed=count * (2 * degrees * lat_total + lat_total * lanes) * 2 + plan["total"] * lanes * 2,
        ),
        name="synthesise",
    )(numbers, chan, table, *parts)


def split_groups(group_count):
    sizes = [group_count - g for g in range(group_count)]
    total = sum(sizes)
    marks = []
    run = 0
    for g, size in enumerate(sizes):
        run += size
        if len(marks) < 2 and run >= 0.3 * total * (len(marks) + 1):
            marks.append(g + 1)
    edges = [0] + marks + [group_count]
    pieces = [list(range(a, b)) for a, b in zip(edges[:-1], edges[1:]) if b > a]
    if len(pieces) == 3:
        pieces = [pieces[0], pieces[2], pieces[1]]
    return pieces


def on_device(signal, spectral_filter, channel_mix):
    lat_count = lax.axis_size("lat")
    chan_count = lax.axis_size("chan")
    lat_rows, quarter, lon_count = signal.shape
    lat_total = lat_rows * lat_count
    degrees = spectral_filter.shape[0]
    group_rows = 2 * lat_count
    group_count = degrees // group_rows
    lat_index = lax.axis_index("lat")
    chan_index = lax.axis_index("chan")
    chan = jnp.reshape(chan_index, (1,)).astype(jnp.int32)
    lanes = 4 * quarter

    k_at = jnp.arange(lat_count, dtype=jnp.int32)
    g_at = jnp.arange(group_count, dtype=jnp.int32)
    e_at = jnp.arange(2, dtype=jnp.int32)
    orders_all = group_rows * g_at[None, None, :] + 2 * k_at[None, :, None] + e_at[:, None, None]
    trig, synth = fourier_tables(orders_all.reshape(-1), lon_count)
    trig = trig.reshape(2, 2, lat_count, group_count, lon_count)
    synth = synth.reshape(2, 2, lat_count, group_count, lon_count)
    own_rows = lat_index * lat_rows + jnp.arange(lat_rows, dtype=jnp.int32)
    _, _, own_weight = latitude_terms(own_rows, lat_total, lon_count)
    cosine, log_sine, _ = latitude_terms(jnp.arange(lat_total, dtype=jnp.int32), lat_total, lon_count)
    orders_own = (group_rows * g_at[:, None] + 2 * lat_index + e_at[None, :]).reshape(-1)
    seeds = seed_logs(orders_own, log_sine)
    table = legendre_table(seeds, orders_own.astype(F32), cosine, group_rows, degrees)

    gains = lax.dynamic_slice_in_dim(spectral_filter, chan_index * quarter, quarter, 2)
    direct = jnp.tile(gains[:, 0, :], (1, 4))
    cross = jnp.concatenate([jnp.tile(-gains[:, 1, :], (1, 2)), jnp.tile(gains[:, 1, :], (1, 2))], 1)

    steps = jnp.arange(chan_count, dtype=jnp.int32)
    sources = (chan_index - steps) % chan_count
    targets = (chan_index + steps) % chan_count
    real_w, imag_w = channel_mix[0], channel_mix[1]
    full = jnp.stack([jnp.stack([real_w, imag_w], 0), jnp.stack([-imag_w, real_w], 0)], 0)
    full = full.reshape(2, 2, chan_count, quarter, chan_count, quarter)
    full = jnp.take(jnp.take(full, sources, axis=2), targets, axis=4)
    same = jnp.eye(2, dtype=BF16)
    kernel = full.transpose(4, 2, 0, 3, 1, 5)[:, :, :, None, :, :, None, :] * same[None, None, None, :, None, None, :, None]
    kernel = kernel.reshape(chan_count, chan_count * lanes, lanes)

    def moved(parts):
        out = [parts[0]]
        for shift in range(1, chan_count):
            pairs = [(i, (i + shift) % chan_count) for i in range(chan_count)]
            out.append(lax.ppermute(parts[shift], "chan", pairs))
        return out

    pieces = split_groups(group_count)
    returned = []
    for groups in pieces:
        plan = chunk_plan(groups, group_rows, degrees, chan_count)
        plan["group_rows"] = group_rows
        trig_part = trig[:, :, :, groups[0]:groups[-1] + 1, :]
        spectrum = jnp.einsum("jcn,tekgn->kgjtec", signal, trig_part, preferred_element_type=F32)
        spectrum = (spectrum * own_weight[None, None, :, None, None, None]).astype(BF16)
        spectrum = spectrum.reshape(lat_count, len(groups), lat_rows, lanes)
        fourier = lax.all_to_all(spectrum, "lat", split_axis=0, concat_axis=0, tiled=True)
        filtered = analyse(plan, chan, fourier, table, direct, cross, chan_count)
        mixed = mix(moved(filtered), kernel)
        back = synthesise(plan, chan, table, moved(mixed), lat_count)
        back = lax.all_to_all(back, "lat", split_axis=0, concat_axis=0, tiled=True)
        returned.append((groups, back))
    rows = jnp.concatenate([b for _, b in returned], 1)
    synth = jnp.concatenate([synth[:, :, :, g[0]:g[-1] + 1, :] for g, _ in returned], 3)
    rows = rows.reshape(lat_count, group_count, lat_rows, 2, 2, quarter)
    output = jnp.einsum("kgjued,uekgn->jdn", rows, synth, preferred_element_type=F32)
    return output.astype(BF16)


def solution(mesh):
    return jax.shard_map(
        on_device,
        mesh=mesh,
        in_specs=(P("lat", "chan", None), P(), P()),
        out_specs=P("lat", "chan", None),
        check_vma=False,
    )
```

time: 1360 us -> 579 us (0.43)
  loops' own time: 486 us -> 0 us
  local copies, waits for them, and re-layouts: 318 us -> 103 us
  blocking collectives: 159 us -> 0 us
  other arithmetic: 135 us -> 25.4 us
  Pallas kernels: 0 us -> 108 us
  waiting for transfers between devices: 105 us -> 200 us
  starting transfers between devices: 15.5 us -> 48.1 us
  matrix products: 115 us -> 84 us
    another operation x12 -> x0, loops' own time: 486 us -> none  [the longest x6 485 us: legendre_rows(): carried, values = lax.scan(advance, recursion, degrees_here, unroll=8)]
    all_to_all x1 -> x0, blocking collectives: 159 us -> none  [on_device(): back = lax.all_to_all(back, 'chan', split_axis=3, concat_axis=0, tiled=True)]
    ppermute x0 -> x18, waiting for transfers between devices: none -> 151 us  [moved(): out.append(lax.ppermute(parts[shift], 'chan', pairs))]
    pallas_call x0 -> x10, Pallas kernels: none -> 108 us  [the longest x3 31.9 us: analyse(): pl.pallas_call(functools.partial(analyse_body, plan), grid_spec=spec, out...]
    slice x103 -> x5, local copies, waits for them, and re-layouts: 88.7 us -> 3.82 us  [the longest x1 2.34 us: on_device(): gains[:, 1, :]]
    while x672 -> x0, other arithmetic: 68.7 us -> none
    concatenate x1 -> x0, local copies, waits for them, and re-layouts: 68.3 us -> none  [on_device(): filtered = jnp.concatenate(filtered_parts, 0)]
    all_to_all x7 -> x0, local copies, waits for them, and re-layouts: 68.2 us -> none  [the longest x3 26.2 us: on_device(): back = lax.all_to_all(back, 'chan', split_axis=3, concat_axis=0, tiled=True)]
  transfers between devices with their start and end apart: 3 -> 24, of which waited for: 1 -> 19; matrix products, arithmetic and copies ran while one was open for 14% -> 17% of each run, Pallas kernels for 0% -> 19%
where the time goes in v1:
time: 579 us; the launch traced here: 569 us
  waiting for transfers between devices  200 us (35%)
  Pallas kernels  108 us (19%)
  local copies, waits for them, and re-layouts  103 us (18%)
  matrix products  84 us (15%)
  starting transfers between devices  48.1 us (8%)
  other arithmetic  25.4 us (4%)
    ppermute x18, waiting for transfers between devices, moved(): out.append(lax.ppermute(parts[shift], 'chan', pairs))  151 us
    dot_general x1, matrix products, on_device(): jnp.einsum('kgjued,uekgn->jdn', rows, synth, preferred_element_type=F32)  51.1 us
    all_to_all x3, waiting for transfers between devices, on_device(): back = lax.all_to_all(back, 'lat', split_axis=0, concat_axis=0, tiled=True)  48.8 us
    dot_general x3, matrix products, on_device(): jnp.einsum('jcn,tekgn->kgjtec', signal, trig_part, preferred_element_type...  32.9 us
    pallas_call x3, Pallas kernels, analyse(): pl.pallas_call(functools.partial(analyse_body, plan), grid_spec=spec, out...  31.9 us
    pallas_call x3, Pallas kernels, synthesise(): pl.pallas_call(functools.partial(synthesise_body, plan), grid_spec=spec,...  28.9 us
    pallas_call x1, Pallas kernels, legendre_table(): pl.pallas_call(functools.partial(table_body, group_rows), grid=(steps,),...  28.5 us
    reshape x1, local copies, waits for them, and re-layouts, on_device(): rows = rows.reshape(lat_count, group_count, lat_rows, 2, 2, quarter)  25.4 us
  transfers between devices with their start and end apart: 24, of which 19 were waited for; matrix products, arithmetic and copies ran while one was open for 17% of the time, Pallas kernels for 19%

profile of v1, /device:TPU:8, one launch (start us, length us, event | category | flops | bytes accessed | tf_op | source)
XLA Modules:
  0.0 569.3 jit_solution(11720828498671299089)
XLA Ops:
  0.1 9.9 %fusion.17 = (f32[1,2,8,24,1440]{4,2,3,1,0:T(8,128)S(1)}, f32[1,2,8,24,1440]{4,2,3,1,0:T(8,128)S(1)}) fusion(s32[2,8,24]{1,2,0:T(8,128)S(1)} %iota_add_fusion), kind=kLoop, calls=%fused_computation.29 | loop fusion | flops 5529600 | bytes 4425216 | tf_op jit(solution)/shard_map/cos | solution.py:26
  12.6 9.9 %fusion.27 = bf16[8,4,48,2,2,96]{5,0,2,1,4,3:T(8,128)(2,1)S(1)} fusion(f32[48]{0:T(128)S(1)} %sine_multiply_fusion, bf16[48,96,1440]{2,1,0:T(8,128)(2,1)} %param.9, bf16[2,2,8,24,1440]{4,2,3,1,0:T(8,128)(2,1)S(1)} %fusion.10), kind=kOutput, calls=%fused_computation.36 | convolution fusion | flops 1699872768 | bytes 14844416 | tf_op jit(solution)/shard_map/jcn,tekgn->kgjtec/dot_general | solution.py:373
  31.2 9.9 %fusion.23 = bf16[8,5,48,2,2,96]{5,0,2,1,4,3:T(8,128)(2,1)} fusion(f32[48]{0:T(128)S(1)} %sine_multiply_fusion, bf16[48,96,1440]{2,1,0:T(8,128)(2,1)} %param.9, bf16[2,2,8,24,1440]{4,2,3,1,0:T(8,128)(2,1)} %copy-done.3), kind=kOutput, calls=%fused_computation.31 | convolution fusion | flops 2124840960 | bytes 16122048 | tf_op jit(solution)/shard_map/jcn,tekgn->kgjtec/dot_general | solution.py:373
  61.3 6.7 %mul.243 = bf16[4,4,2,2,96,2,2,96]{7,6,5,4,3,2,1,0:T(2,128)(2,1)} broadcast(bf16[4,4,2,96,2,96]{5,4,3,2,1,0:T(2,128)(2,1)S(1)} %copy.74), dimensions={0,1,2,4,5,7} | broadcast | bytes 5898240 | tf_op jit(solution)/shard_map/mul | solution.py:357
  68.0 14.5 %mul.244 = bf16[4,1536,384]{2,1,0:T(8,128)(2,1)} reshape(bf16[4,4,2,2,96,2,2,96]{7,6,5,4,3,2,1,0:T(2,128)(2,1)} %mul.243) | data formatting | bytes 9437184 | tf_op jit(solution)/shard_map/mul | solution.py:357
  84.6 28.5 %legendre_table.1.table_ref = bf16[24,2,384,384]{3,2,1,0:T(8,128)(2,1)} custom-call(f32[6,8,384]{2,1,0:T(8,128)} %multiply_add_fusion.seeds_ref, f32[6,8,128]{2,1,0:T(8,128)} %broadcast_in_dim.25.order_ref, f32[1,384]{1,0:T(1,128)} %multiply_cosine_fusion.cosine_ref), custom_call_target="tpu_custom_call" | custom-call | flops 40000000 | bytes 14155776 | tf_op jit(solution)/shard_map/legendre_table/pallas_call | solution.py:114
  118.2 7.1 %analyse.3 = (bf16[368,384]{1,0:T(8,128)(2,1)}, bf16[368,384]{1,0:T(8,128)(2,1)}, bf16[368,384]{1,0:T(8,128)(2,1)}, bf16[368,384]{1,0:T(8,128)(2,1)}) custom-call(s32[4]{0:T(128)} %constant.167.clone.count_ref, s32[1]{0:T(128)} %bitcast.chan_ref, bf16[8,4,48,384]{3,2,1,0:T(8,128)(2,1)} %all-to-all-done.fourier_ref, ...), custom_call_target="tpu_custom_call" | custom-call | flops 905969664 | bytes 4669440 | tf_op jit(solution)/shard_map/analyse/pallas_call | solution.py:205
  132.3 13.9 %collective-permute-done.refs_1_ = bf16[368,384]{1,0:T(8,128)(2,1)S(1)} collective-permute-done((bf16[368,384]{1,0:T(8,128)(2,1)}, bf16[368,384]{1,0:T(8,128)(2,1)S(1)}, u32[]{:S(2)}, u32[]{:S(2)}) %collective-permute-start) | collective-permute-done | bytes 282656 | tf_op jit(solution)/shard_map/ppermute | solution.py:364
  154.1 6.0 %mix.3 = (bf16[368,384]{1,0:T(8,128)(2,1)}, bf16[368,384]{1,0:T(8,128)(2,1)}, bf16[368,384]{1,0:T(8,128)(2,1)}, bf16[368,384]{1,0:T(8,128)(2,1)}) custom-call(bf16[368,384]{1,0:T(8,128)(2,1)} %get-tuple-element.29.refs_0_, bf16[368,384]{1,0:T(8,128)(2,1)} %copy-done.24, bf16[368,384]{1,0:T(8,128)(2,1)} %copy-done.25, bf16[368,384]{1,0:T(8,128)(2,1)} %copy-done.27, ...), custom_call_target="tpu_custom_call" | custom-call | flops 1736441856 | bytes 6979584 | tf_op jit(solution)/shard_map/mix/pallas_call | solution.py:229
  169.9 15.2 %collective-permute-done.4.refs_2_ = bf16[368,384]{1,0:T(8,128)(2,1)S(1)} collective-permute-done((bf16[368,384]{1,0:T(8,128)(2,1)}, bf16[368,384]{1,0:T(8,128)(2,1)S(1)}, u32[]{:S(2)}, u32[]{:S(2)}) %collective-permute-start.4) | collective-permute-done | bytes 282656 | tf_op jit(solution)/shard_map/ppermute | solution.py:364
  187.9 5.8 %synthesise.3 = bf16[8,4,48,384]{3,2,1,0:T(8,128)(2,1)} custom-call(s32[2,4]{1,0:T(2,128)} %constant.168.clone.count_ref, s32[1]{0:T(128)} %bitcast.chan_ref, bf16[24,2,384,384]{3,2,1,0:T(8,128)(2,1)} %legendre_table.1.table_ref, bf16[368,384]{1,0:T(8,128)(2,1)} %get-tuple-element.33.refs_0_, bf16[368,384]{1,0:T(8,128)(2,1)} %copy-done.13, ...), custom_call_target="tpu_custom_call" | custom-call | flops 905969664 | bytes 4669440 | tf_op jit(solution)/shard_map/synthesise/pallas_call | solution.py:288
  197.5 13.1 %fusion.7 = bf16[8,15,48,2,2,96]{5,1,2,0,4,3:T(8,128)(2,1)S(1)} fusion(f32[48]{0:T(128)S(1)} %sine_multiply_fusion, bf16[48,96,1440]{2,1,0:T(8,128)(2,1)} %param.9, bf16[2,2,8,15,1440,1]{4,2,3,1,0,5:T(8,128)(2,1)} %slice_bitcast_fusion), kind=kOutput, calls=%fused_computation.12 | convolution fusion | flops 6374522880 | bytes 19077312 | tf_op jit(solution)/shard_map/jcn,tekgn->kgjtec/dot_general | solution.py:373
  210.6 10.8 %copy.76 = bf16[8,15,48,2,2,96]{5,4,3,2,1,0:T(2,128)(2,1)} copy(bf16[8,15,48,2,2,96]{5,1,2,0,4,3:T(8,128)(2,1)S(1)} %fusion.7) | data formatting | bytes 8847360 | tf_op jit(solution)/shard_map/convert_element_type | solution.py:374
  221.4 13.7 %reshape.636 = bf16[8,15,48,384]{3,2,1,0:T(8,128)(2,1)} reshape(bf16[8,15,48,2,2,96]{5,4,3,2,1,0:T(2,128)(2,1)} %copy.76) | data formatting | bytes 8847360 | tf_op jit(solution)/shard_map/reshape | solution.py:375
  239.7 7.7 %analyse.5 = (bf16[368,384]{1,0:T(8,128)(2,1)}, bf16[368,384]{1,0:T(8,128)(2,1)}, bf16[368,384]{1,0:T(8,128)(2,1)}, bf16[368,384]{1,0:T(8,128)(2,1)}) custom-call(s32[5]{0:T(128)} %constant.171.clone.count_ref, s32[1]{0:T(128)} %bitcast.chan_ref, bf16[8,5,48,384]{3,2,1,0:T(8,128)(2,1)} %copy-done.5, bf16[24,2,384,384]{3,2,1,0:T(8,128)(2,1)} %legendre_table.1.table_ref, ...), custom_call_target="tpu_custom_call" | custom-call | flops 1132462080 | bytes 5554176 | tf_op jit(solution)/shard_map/analyse/pallas_call | solution.py:205
  251.0 6.2 %collective-permute-done.12.refs_1_ = bf16[368,384]{1,0:T(8,128)(2,1)S(1)} collective-permute-done((bf16[368,384]{1,0:T(8,128)(2,1)}, bf16[368,384]{1,0:T(8,128)(2,1)S(1)}, u32[]{:S(2)}, u32[]{:S(2)}) %collective-permute-start.12) | collective-permute-done | bytes 282656 | tf_op jit(solution)/shard_map/ppermute | solution.py:364
  257.2 15.5 %collective-permute-done.13.refs_2_ = bf16[368,384]{1,0:T(8,128)(2,1)S(1)} collective-permute-done((bf16[368,384]{1,0:T(8,128)(2,1)}, bf16[368,384]{1,0:T(8,128)(2,1)S(1)}, u32[]{:S(2)}, u32[]{:S(2)}) %collective-permute-start.13) | collective-permute-done | bytes 282656 | tf_op jit(solution)/shard_map/ppermute | solution.py:364
  275.4 5.9 %mix.5 = (bf16[368,384]{1,0:T(8,128)(2,1)}, bf16[368,384]{1,0:T(8,128)(2,1)}, bf16[368,384]{1,0:T(8,128)(2,1)}, bf16[368,384]{1,0:T(8,128)(2,1)}) custom-call(bf16[368,384]{1,0:T(8,128)(2,1)} %get-tuple-element.45.refs_0_, bf16[368,384]{1,0:T(8,128)(2,1)} %copy-done.26, bf16[368,384]{1,0:T(8,128)(2,1)} %copy-done.28, bf16[368,384]{1,0:T(8,128)(2,1)} %copy-done.29, ...), custom_call_target="tpu_custom_call" | custom-call | flops 1736441856 | bytes 6979584 | tf_op jit(solution)/shard_map/mix/pallas_call | solution.py:229
  284.7 6.4 %collective-permute-done.15.refs_1_ = bf16[368,384]{1,0:T(8,128)(2,1)S(1)} collective-permute-done((bf16[368,384]{1,0:T(8,128)(2,1)}, bf16[368,384]{1,0:T(8,128)(2,1)S(1)}, u32[]{:S(2)}, u32[]{:S(2)}) %collective-permute-start.15) | collective-permute-done | bytes 282656 | tf_op jit(solution)/shard_map/ppermute | solution.py:364
  291.2 15.3 %collective-permute-done.16.refs_2_ = bf16[368,384]{1,0:T(8,128)(2,1)S(1)} collective-permute-done((bf16[368,384]{1,0:T(8,128)(2,1)}, bf16[368,384]{1,0:T(8,128)(2,1)S(1)}, u32[]{:S(2)}, u32[]{:S(2)}) %collective-permute-start.16) | collective-permute-done | bytes 282656 | tf_op jit(solution)/shard_map/ppermute | solution.py:364
  308.6 7.0 %synthesise.5 = bf16[8,5,48,384]{3,2,1,0:T(8,128)(2,1)} custom-call(s32[2,5]{1,0:T(2,128)} %constant.172.clone.count_ref, s32[1]{0:T(128)} %bitcast.chan_ref, bf16[24,2,384,384]{3,2,1,0:T(8,128)(2,1)} %legendre_table.1.table_ref, bf16[368,384]{1,0:T(8,128)(2,1)} %get-tuple-element.49.refs_0_, bf16[368,384]{1,0:T(8,128)(2,1)} %copy-done.14, ...), custom_call_target="tpu_custom_call" | custom-call | flops 1132462080 | bytes 5554176 | tf_op jit(solution)/shard_map/synthesise/pallas_call | solution.py:288
  319.9 17.2 %analyse.4 = (bf16[480,384]{1,0:T(8,128)(2,1)}, bf16[480,384]{1,0:T(8,128)(2,1)}, bf16[480,384]{1,0:T(8,128)(2,1)}, bf16[480,384]{1,0:T(8,128)(2,1)}) custom-call(s32[15]{0:T(128)} %constant.169.clone.count_ref, s32[1]{0:T(128)} %bitcast.chan_ref, bf16[8,15,48,384]{3,2,1,0:T(8,128)(2,1)} %all-to-all-done.2.fourier_ref, ...), custom_call_target="tpu_custom_call" | custom-call | flops 3397386240 | bytes 14745600 | tf_op jit(solution)/shard_map/analyse/pallas_call | solution.py:205
  341.1 7.6 %collective-permute-done.6.refs_1_ = bf16[480,384]{1,0:T(8,128)(2,1)S(1)} collective-permute-done((bf16[480,384]{1,0:T(8,128)(2,1)}, bf16[480,384]{1,0:T(8,128)(2,1)S(1)}, u32[]{:S(2)}, u32[]{:S(2)}) %collective-permute-start.6) | collective-permute-done | bytes 368672 | tf_op jit(solution)/shard_map/ppermute | solution.py:364
  348.7 21.1 %collective-permute-done.7.refs_2_ = bf16[480,384]{1,0:T(8,128)(2,1)S(1)} collective-permute-done((bf16[480,384]{1,0:T(8,128)(2,1)}, bf16[480,384]{1,0:T(8,128)(2,1)S(1)}, u32[]{:S(2)}, u32[]{:S(2)}) %collective-permute-start.7) | collective-permute-done | bytes 368672 | tf_op jit(solution)/shard_map/ppermute | solution.py:364
  372.9 6.8 %mix.4 = (bf16[480,384]{1,0:T(8,128)(2,1)}, bf16[480,384]{1,0:T(8,128)(2,1)}, bf16[480,384]{1,0:T(8,128)(2,1)}, bf16[480,384]{1,0:T(8,128)(2,1)}) custom-call(bf16[480,384]{1,0:T(8,128)(2,1)} %get-tuple-element.37.refs_0_, bf16[480,384]{1,0:T(8,128)(2,1)} %copy-done.21, bf16[480,384]{1,0:T(8,128)(2,1)} %copy-done.22, bf16[480,384]{1,0:T(8,128)(2,1)} %copy-done.23, ...), custom_call_target="tpu_custom_call" | custom-call | flops 2264924160 | bytes 7667712 | tf_op jit(solution)/shard_map/mix/pallas_call | solution.py:229
  382.7 8.6 %collective-permute-done.9.refs_1_ = bf16[480,384]{1,0:T(8,128)(2,1)S(1)} collective-permute-done((bf16[480,384]{1,0:T(8,128)(2,1)}, bf16[480,384]{1,0:T(8,128)(2,1)S(1)}, u32[]{:S(2)}, u32[]{:S(2)}) %collective-permute-start.9) | collective-permute-done | bytes 368672 | tf_op jit(solution)/shard_map/ppermute | solution.py:364
  391.3 20.7 %collective-permute-done.10.refs_2_ = bf16[480,384]{1,0:T(8,128)(2,1)S(1)} collective-permute-done((bf16[480,384]{1,0:T(8,128)(2,1)}, bf16[480,384]{1,0:T(8,128)(2,1)S(1)}, u32[]{:S(2)}, u32[]{:S(2)}) %collective-permute-start.10) | collective-permute-done | bytes 368672 | tf_op jit(solution)/shard_map/ppermute | solution.py:364
  413.9 16.0 %synthesise.4 = bf16[8,15,48,384]{3,2,1,0:T(8,128)(2,1)} custom-call(s32[2,15]{1,0:T(2,128)} %constant.170.clone.count_ref, s32[1]{0:T(128)} %bitcast.chan_ref, bf16[24,2,384,384]{3,2,1,0:T(8,128)(2,1)} %legendre_table.1.table_ref, bf16[480,384]{1,0:T(8,128)(2,1)} %get-tuple-element.41.refs_0_, bf16[480,384]{1,0:T(8,128)(2,1)} %copy-done.10, ...), custom_call_target="tpu_custom_call" | custom-call | flops 3397386240 | bytes 14745600 | tf_op jit(solution)/shard_map/synthesise/pallas_call | solution.py:288
  437.5 48.8 %all-to-all-done.3 = bf16[8,15,48,384]{3,2,1,0:T(8,128)(2,1)} async-done(((bf16[8,15,48,384]{3,2,1,0:T(8,128)(2,1)}), bf16[8,15,48,384]{3,2,1,0:T(8,128)(2,1)}, u32[]{:S(2)}, u32[]{:S(2)}) %all-to-all-start.3) | async-done | bytes 4423712 | tf_op jit(solution)/shard_map/all_to_all | solution.py:380
  486.3 6.2 %pad_maximum_fusion = bf16[8,24,48,384]{3,2,1,0:T(8,128)(2,1)} fusion(bf16[8,5,48,384]{3,2,1,0:T(8,128)(2,1)} %all-to-all-done.5, bf16[8,15,48,384]{3,2,1,0:T(8,128)(2,1)} %all-to-all-done.3, bf16[8,4,48,384]{3,2,1,0:T(8,128)(2,1)S(1)} %all-to-all-done.1), kind=kLoop, calls=%fused_computation.11 | loop fusion | flops 7077888 | bytes 14155776 | tf_op jit(solution)/shard_map/concatenate | solution.py:382
  492.5 25.4 %reshape.638 = bf16[8,24,48,2,2,96]{5,4,3,2,1,0:T(2,128)(2,1)} reshape(bf16[8,24,48,384]{3,2,1,0:T(8,128)(2,1)} %pad_maximum_fusion) | data formatting | bytes 14155776 | tf_op jit(solution)/shard_map/reshape | solution.py:384
  517.8 51.1 %bitcast_convert_fusion = bf16[48,96,1440]{2,1,0:T(8,128)(2,1)} fusion(bf16[8,24,48,2,2,96]{5,4,3,2,1,0:T(2,128)(2,1)} %reshape.638, bf16[2,2,8,24,1440]{4,2,3,1,0:T(8,128)(2,1)S(1)} %pad_maximum_fusion.2), kind=kOutput, calls=%fused_computation.2 | convolution fusion | flops 10198794240 | bytes 22560768 | tf_op jit(solution)/shard_map/kgjued,uekgn->jdn/dot_general | solution.py:385
  (164 shorter events, 110.0 us)
Async XLA Ops:
  26.2 87.8 %all-to-all-start = ((bf16[8,4,48,384]{3,2,1,0:T(8,128)(2,1)}), bf16[8,4,48,384]{3,2,1,0:T(8,128)(2,1)}, u32[]{:S(2)}, u32[]{:S(2)}) async-start(bf16[8,4,48,384]{3,2,1,0:T(8,128)(2,1)} %reshape.635), calls=%async_computation | async-start | bytes 2359296 | tf_op jit(solution)/shard_map/all_to_all | solution.py:376
  84.5 28.5 %copy-start.8 = (f32[384,192]{1,0:T(8,128)S(1)}, f32[384,192]{1,0:T(8,128)}, u32[]{:S(2)}) copy-start(f32[384,192]{1,0:T(8,128)} %copy.68) | copy-start | bytes 884740
  84.6 28.5 %copy-start.9 = (f32[384,192]{1,0:T(8,128)S(1)}, f32[384,192]{1,0:T(8,128)}, u32[]{:S(2)}) copy-start(f32[384,192]{1,0:T(8,128)} %copy.69) | copy-start | bytes 884740
  114.0 79.7 %all-to-all-start.4 = ((bf16[8,5,48,384]{3,2,1,0:T(8,128)(2,1)}), bf16[8,5,48,384]{3,2,1,0:T(8,128)(2,1)S(1)}, u32[]{:S(2)}, u32[]{:S(2)}) async-start(bf16[8,5,48,384]{3,2,1,0:T(8,128)(2,1)} %reshape.637), calls=%async_computation.4 | async-start | bytes 2949120 | tf_op jit(solution)/shard_map/all_to_all | solution.py:376
  125.2 21.0 %collective-permute-start = (bf16[368,384]{1,0:T(8,128)(2,1)}, bf16[368,384]{1,0:T(8,128)(2,1)S(1)}, u32[]{:S(2)}, u32[]{:S(2)}) collective-permute-start(bf16[368,384]{1,0:T(8,128)(2,1)} %get-tuple-element.30), channel_id=1, source_target_pairs={{0,1},{1,2},{2,3},{3,0},{4,5},{5,6},{6,7},{7,4},{8,9},{9,10},{10,1... | collective-permute-start | bytes 847880 | tf_op jit(solution)/shard_map/ppermute | solution.py:364
  126.9 25.1 %collective-permute-start.1 = (bf16[368,384]{1,0:T(8,128)(2,1)}, bf16[368,384]{1,0:T(8,128)(2,1)S(1)}, u32[]{:S(2)}, u32[]{:S(2)}) collective-permute-start(bf16[368,384]{1,0:T(8,128)(2,1)} %get-tuple-element.31), channel_id=1, source_target_pairs={{0,2},{1,3},{2,0},{3,1},{4,6},{5,7},{6,4},{7,5},{8,10},{9,11},{10,... | collective-permute-start | bytes 847880 | tf_op jit(solution)/shard_map/ppermute | solution.py:364
  127.6 25.7 %collective-permute-start.2 = (bf16[368,384]{1,0:T(8,128)(2,1)}, bf16[368,384]{1,0:T(8,128)(2,1)S(1)}, u32[]{:S(2)}, u32[]{:S(2)}) collective-permute-start(bf16[368,384]{1,0:T(8,128)(2,1)} %get-tuple-element.32), channel_id=1, source_target_pairs={{0,3},{1,0},{2,1},{3,2},{4,7},{5,4},{6,5},{7,6},{8,11},{9,8},{10,9... | collective-permute-start | bytes 847880 | tf_op jit(solution)/shard_map/ppermute | solution.py:364
  160.1 9.8 %collective-permute-start.3 = (bf16[368,384]{1,0:T(8,128)(2,1)}, bf16[368,384]{1,0:T(8,128)(2,1)S(1)}, u32[]{:S(2)}, u32[]{:S(2)}) collective-permute-start(bf16[368,384]{1,0:T(8,128)(2,1)} %get-tuple-element.34), channel_id=1, source_target_pairs={{0,1},{1,2},{2,3},{3,0},{4,5},{5,6},{6,7},{7,4},{8,9},{9,10},{10,1... | collective-permute-start | bytes 847880 | tf_op jit(solution)/shard_map/ppermute | solution.py:364
  160.1 25.0 %collective-permute-start.4 = (bf16[368,384]{1,0:T(8,128)(2,1)}, bf16[368,384]{1,0:T(8,128)(2,1)S(1)}, u32[]{:S(2)}, u32[]{:S(2)}) collective-permute-start(bf16[368,384]{1,0:T(8,128)(2,1)} %get-tuple-element.35), channel_id=1, source_target_pairs={{0,2},{1,3},{2,0},{3,1},{4,6},{5,7},{6,4},{7,5},{8,10},{9,11},{10,... | collective-permute-start | bytes 847880 | tf_op jit(solution)/shard_map/ppermute | solution.py:364
  162.2 25.0 %collective-permute-start.5 = (bf16[368,384]{1,0:T(8,128)(2,1)}, bf16[368,384]{1,0:T(8,128)(2,1)S(1)}, u32[]{:S(2)}, u32[]{:S(2)}) collective-permute-start(bf16[368,384]{1,0:T(8,128)(2,1)} %get-tuple-element.36), channel_id=1, source_target_pairs={{0,3},{1,0},{2,1},{3,2},{4,7},{5,4},{6,5},{7,6},{8,11},{9,8},{10,9... | collective-permute-start | bytes 847880 | tf_op jit(solution)/shard_map/ppermute | solution.py:364
  169.9 17.3 %copy-start.13 = (bf16[368,384]{1,0:T(8,128)(2,1)}, bf16[368,384]{1,0:T(8,128)(2,1)S(1)}, u32[]{:S(2)}) copy-start(bf16[368,384]{1,0:T(8,128)(2,1)S(1)} %collective-permute-done.3.refs_1_) | copy-start | bytes 847876
  193.8 16.8 %copy-start.5 = (bf16[8,5,48,384]{3,2,1,0:T(8,128)(2,1)}, bf16[8,5,48,384]{3,2,1,0:T(8,128)(2,1)S(1)}, u32[]{:S(2)}) copy-start(bf16[8,5,48,384]{3,2,1,0:T(8,128)(2,1)S(1)} %all-to-all-done.4.fourier_ref) | copy-start | bytes 4423684
  193.8 41.3 %all-to-all-start.1 = ((bf16[8,4,48,384]{3,2,1,0:T(8,128)(2,1)}), bf16[8,4,48,384]{3,2,1,0:T(8,128)(2,1)S(1)}, u32[]{:S(2)}, u32[]{:S(2)}) async-start(bf16[8,4,48,384]{3,2,1,0:T(8,128)(2,1)} %synthesise.3), calls=%async_computation.1 | async-start | bytes 2359296 | tf_op jit(solution)/shard_map/all_to_all | solution.py:380
  235.1 80.5 %all-to-all-start.2 = ((bf16[8,15,48,384]{3,2,1,0:T(8,128)(2,1)}), bf16[8,15,48,384]{3,2,1,0:T(8,128)(2,1)}, u32[]{:S(2)}, u32[]{:S(2)}) async-start(bf16[8,15,48,384]{3,2,1,0:T(8,128)(2,1)} %reshape.636), calls=%async_computation.2 | async-start | bytes 8847360 | tf_op jit(solution)/shard_map/all_to_all | solution.py:376
  247.4 9.8 %collective-permute-start.12 = (bf16[368,384]{1,0:T(8,128)(2,1)}, bf16[368,384]{1,0:T(8,128)(2,1)S(1)}, u32[]{:S(2)}, u32[]{:S(2)}) collective-permute-start(bf16[368,384]{1,0:T(8,128)(2,1)} %get-tuple-element.46), channel_id=1, source_target_pairs={{0,1},{1,2},{2,3},{3,0},{4,5},{5,6},{6,7},{7,4},{8,9},{9,10},{10,1... | collective-permute-start | bytes 847880 | tf_op jit(solution)/shard_map/ppermute | solution.py:364
  247.4 25.3 %collective-permute-start.13 = (bf16[368,384]{1,0:T(8,128)(2,1)}, bf16[368,384]{1,0:T(8,128)(2,1)S(1)}, u32[]{:S(2)}, u32[]{:S(2)}) collective-permute-start(bf16[368,384]{1,0:T(8,128)(2,1)} %get-tuple-element.47), channel_id=1, source_target_pairs={{0,2},{1,3},{2,0},{3,1},{4,6},{5,7},{6,4},{7,5},{8,10},{9,11},{10,... | collective-permute-start | bytes 847880 | tf_op jit(solution)/shard_map/ppermute | solution.py:364
  249.0 25.7 %collective-permute-start.14 = (bf16[368,384]{1,0:T(8,128)(2,1)}, bf16[368,384]{1,0:T(8,128)(2,1)S(1)}, u32[]{:S(2)}, u32[]{:S(2)}) collective-permute-start(bf16[368,384]{1,0:T(8,128)(2,1)} %get-tuple-element.48), channel_id=1, source_target_pairs={{0,3},{1,0},{2,1},{3,2},{4,7},{5,4},{6,5},{7,6},{8,11},{9,8},{10,9... | collective-permute-start | bytes 847880 | tf_op jit(solution)/shard_map/ppermute | solution.py:364
  257.2 17.6 %copy-start.26 = (bf16[368,384]{1,0:T(8,128)(2,1)}, bf16[368,384]{1,0:T(8,128)(2,1)S(1)}, u32[]{:S(2)}) copy-start(bf16[368,384]{1,0:T(8,128)(2,1)S(1)} %collective-permute-done.12.refs_1_) | copy-start | bytes 847876
  281.4 9.8 %collective-permute-start.15 = (bf16[368,384]{1,0:T(8,128)(2,1)}, bf16[368,384]{1,0:T(8,128)(2,1)S(1)}, u32[]{:S(2)}, u32[]{:S(2)}) collective-permute-start(bf16[368,384]{1,0:T(8,128)(2,1)} %get-tuple-element.50), channel_id=1, source_target_pairs={{0,1},{1,2},{2,3},{3,0},{4,5},{5,6},{6,7},{7,4},{8,9},{9,10},{10,1... | collective-permute-start | bytes 847880 | tf_op jit(solution)/shard_map/ppermute | solution.py:364
  281.4 25.1 %collective-permute-start.16 = (bf16[368,384]{1,0:T(8,128)(2,1)}, bf16[368,384]{1,0:T(8,128)(2,1)S(1)}, u32[]{:S(2)}, u32[]{:S(2)}) collective-permute-start(bf16[368,384]{1,0:T(8,128)(2,1)} %get-tuple-element.51), channel_id=1, source_target_pairs={{0,2},{1,3},{2,0},{3,1},{4,6},{5,7},{6,4},{7,5},{8,10},{9,11},{10,... | collective-permute-start | bytes 847880 | tf_op jit(solution)/shard_map/ppermute | solution.py:364
  282.7 25.1 %collective-permute-start.17 = (bf16[368,384]{1,0:T(8,128)(2,1)}, bf16[368,384]{1,0:T(8,128)(2,1)S(1)}, u32[]{:S(2)}, u32[]{:S(2)}) collective-permute-start(bf16[368,384]{1,0:T(8,128)(2,1)} %get-tuple-element.52), channel_id=1, source_target_pairs={{0,3},{1,0},{2,1},{3,2},{4,7},{5,4},{6,5},{7,6},{8,11},{9,8},{10,9... | collective-permute-start | bytes 847880 | tf_op jit(solution)/shard_map/ppermute | solution.py:364
  291.2 16.7 %copy-start.14 = (bf16[368,384]{1,0:T(8,128)(2,1)}, bf16[368,384]{1,0:T(8,128)(2,1)S(1)}, u32[]{:S(2)}) copy-start(bf16[368,384]{1,0:T(8,128)(2,1)S(1)} %collective-permute-done.15.refs_1_) | copy-start | bytes 847876
  315.6 114.4 %all-to-all-start.5 = ((bf16[8,5,48,384]{3,2,1,0:T(8,128)(2,1)}), bf16[8,5,48,384]{3,2,1,0:T(8,128)(2,1)}, u32[]{:S(2)}, u32[]{:S(2)}) async-start(bf16[8,5,48,384]{3,2,1,0:T(8,128)(2,1)} %synthesise.5), calls=%async_computation.5 | async-start | bytes 2949120 | tf_op jit(solution)/shard_map/all_to_all | solution.py:380
  337.0 11.6 %collective-permute-start.6 = (bf16[480,384]{1,0:T(8,128)(2,1)}, bf16[480,384]{1,0:T(8,128)(2,1)S(1)}, u32[]{:S(2)}, u32[]{:S(2)}) collective-permute-start(bf16[480,384]{1,0:T(8,128)(2,1)} %get-tuple-element.38), channel_id=1, source_target_pairs={{0,1},{1,2},{2,3},{3,0},{4,5},{5,6},{6,7},{7,4},{8,9},{9,10},{10,1... | collective-permute-start | bytes 1105928 | tf_op jit(solution)/shard_map/ppermute | solution.py:364
  337.0 32.7 %collective-permute-start.7 = (bf16[480,384]{1,0:T(8,128)(2,1)}, bf16[480,384]{1,0:T(8,128)(2,1)S(1)}, u32[]{:S(2)}, u32[]{:S(2)}) collective-permute-start(bf16[480,384]{1,0:T(8,128)(2,1)} %get-tuple-element.39), channel_id=1, source_target_pairs={{0,2},{1,3},{2,0},{3,1},{4,6},{5,7},{6,4},{7,5},{8,10},{9,11},{10,... | collective-permute-start | bytes 1105928 | tf_op jit(solution)/shard_map/ppermute | solution.py:364
  339.1 33.0 %collective-permute-start.8 = (bf16[480,384]{1,0:T(8,128)(2,1)}, bf16[480,384]{1,0:T(8,128)(2,1)S(1)}, u32[]{:S(2)}, u32[]{:S(2)}) collective-permute-start(bf16[480,384]{1,0:T(8,128)(2,1)} %get-tuple-element.40), channel_id=1, source_target_pairs={{0,3},{1,0},{2,1},{3,2},{4,7},{5,4},{6,5},{7,6},{8,11},{9,8},{10,9... | collective-permute-start | bytes 1105928 | tf_op jit(solution)/shard_map/ppermute | solution.py:364
  348.7 23.4 %copy-start.21 = (bf16[480,384]{1,0:T(8,128)(2,1)}, bf16[480,384]{1,0:T(8,128)(2,1)S(1)}, u32[]{:S(2)}) copy-start(bf16[480,384]{1,0:T(8,128)(2,1)S(1)} %collective-permute-done.6.refs_1_) | copy-start | bytes 1105924
  379.6 11.7 %collective-permute-start.9 = (bf16[480,384]{1,0:T(8,128)(2,1)}, bf16[480,384]{1,0:T(8,128)(2,1)S(1)}, u32[]{:S(2)}, u32[]{:S(2)}) collective-permute-start(bf16[480,384]{1,0:T(8,128)(2,1)} %get-tuple-element.42), channel_id=1, source_target_pairs={{0,1},{1,2},{2,3},{3,0},{4,5},{5,6},{6,7},{7,4},{8,9},{9,10},{10,1... | collective-permute-start | bytes 1105928 | tf_op jit(solution)/shard_map/ppermute | solution.py:364
  379.6 32.3 %collective-permute-start.10 = (bf16[480,384]{1,0:T(8,128)(2,1)}, bf16[480,384]{1,0:T(8,128)(2,1)S(1)}, u32[]{:S(2)}, u32[]{:S(2)}) collective-permute-start(bf16[480,384]{1,0:T(8,128)(2,1)} %get-tuple-element.43), channel_id=1, source_target_pairs={{0,2},{1,3},{2,0},{3,1},{4,6},{5,7},{6,4},{7,5},{8,10},{9,11},{10,... | collective-permute-start | bytes 1105928 | tf_op jit(solution)/shard_map/ppermute | solution.py:364
  380.7 32.5 %collective-permute-start.11 = (bf16[480,384]{1,0:T(8,128)(2,1)}, bf16[480,384]{1,0:T(8,128)(2,1)S(1)}, u32[]{:S(2)}, u32[]{:S(2)}) collective-permute-start(bf16[480,384]{1,0:T(8,128)(2,1)} %get-tuple-element.44), channel_id=1, source_target_pairs={{0,3},{1,0},{2,1},{3,2},{4,7},{5,4},{6,5},{7,6},{8,11},{9,8},{10,9... | collective-permute-start | bytes 1105928 | tf_op jit(solution)/shard_map/ppermute | solution.py:364
  391.3 21.9 %copy-start.10 = (bf16[480,384]{1,0:T(8,128)(2,1)}, bf16[480,384]{1,0:T(8,128)(2,1)S(1)}, u32[]{:S(2)}) copy-start(bf16[480,384]{1,0:T(8,128)(2,1)S(1)} %collective-permute-done.9.refs_1_) | copy-start | bytes 1105924
  430.0 56.3 %all-to-all-start.3 = ((bf16[8,15,48,384]{3,2,1,0:T(8,128)(2,1)}), bf16[8,15,48,384]{3,2,1,0:T(8,128)(2,1)}, u32[]{:S(2)}, u32[]{:S(2)}) async-start(bf16[8,15,48,384]{3,2,1,0:T(8,128)(2,1)} %synthesise.4), calls=%async_computation.3 | async-start | bytes 8847360 | tf_op jit(solution)/shard_map/all_to_all | solution.py:380
  (24 other events, 105.6 us)

commit v2 on v1

v2 whole, which is shorter than its diff:
```python
import functools
import math

import jax
import jax.numpy as jnp
import numpy as np
from jax import lax
from jax.experimental import pallas as pl
from jax.experimental.pallas import tpu as pltpu
from jax.sharding import PartitionSpec as P

F32 = jnp.float32
BF16 = jnp.bfloat16
VMEM_BYTES = 56 << 20
STEP = 16
HELD = pl.BlockSpec(memory_space=pl.ANY)
LIGHT = pl.CostEstimate(flops=1000, transcendentals=0, bytes_accessed=1000)
HEAVY = pl.CostEstimate(flops=200_000_000_000, transcendentals=0, bytes_accessed=1000)


def params(**kw):
    return pltpu.CompilerParams(vmem_limit_bytes=VMEM_BYTES, **kw)


def turns(orders, lon_count):
    cells = jnp.arange(lon_count, dtype=jnp.int32)
    phase = orders[:, None] * cells[None, :] % lon_count
    angle = phase.astype(F32) * (2.0 * math.pi / lon_count)
    return jnp.cos(angle), jnp.sin(angle)


def fourier_tables(group_orders, lat_count, lon_count):
    cos_g, sin_g = turns(group_orders, lon_count)
    fine = jnp.arange(2, dtype=jnp.int32)[:, None] + 2 * jnp.arange(lat_count, dtype=jnp.int32)[None, :]
    cos_f, sin_f = turns(fine.reshape(-1), lon_count)
    cos_g, sin_g, cos_f, sin_f = lax.optimization_barrier((cos_g, sin_g, cos_f, sin_f))
    cos_g, sin_g = cos_g[None, :, None, :], sin_g[None, :, None, :]
    cos_f = cos_f.reshape(2, 1, lat_count, lon_count)
    sin_f = sin_f.reshape(2, 1, lat_count, lon_count)
    forward = jnp.stack([cos_g * cos_f - sin_g * sin_f, -(sin_g * cos_f + cos_g * sin_f)], 0)
    orders = group_orders[None, :, None] + fine[:, None, :]
    factor = jnp.where(orders == 0, 1.0, 2.0).astype(F32)[None, :, :, :, None]
    shape = (4, group_orders.shape[0] * lat_count, lon_count)
    return (forward.astype(BF16).reshape(shape), (forward * factor).astype(BF16).reshape(shape))


def latitude_terms(lat_index, lat_total, lon_count):
    theta = (lat_index.astype(F32) + 0.5) * (math.pi / lat_total)
    weight = jnp.sin(theta) * (2.0 * math.pi * math.pi / (lat_total * lon_count))
    return (jnp.cos(theta), jnp.log(jnp.sin(theta)), weight)


def seed_logs(orders, log_sine):
    order_f = orders.astype(F32)[:, None]
    base_term = 0.5 * jnp.log((2.0 * order_f + 1.0) / (4.0 * math.pi))
    ratio_term = 0.5 * (
        jax.scipy.special.gammaln(order_f + 0.5)
        - jax.scipy.special.gammaln(order_f + 1.0)
        - 0.5 * math.log(math.pi)
    )
    return base_term + ratio_term + order_f * log_sine[None, :]


def table_body(group_rows, groups, base, inverse_ref, seeds_ref, order_ref, cosine_ref, *refs):
    out_ref, rows_ref = refs[-2:]
    depth = out_ref.shape[1]
    slots, lat_total = seeds_ref.shape
    per_step = slots // 2
    first = (groups[0] + pl.program_id(0) * per_step) * group_rows - base
    first_block = first // STEP
    blank = jnp.zeros((STEP, 2 * lat_total), out_ref.dtype)

    @pl.loop(0, first_block)
    def _(block):
        at = pl.multiple_of(block * STEP, STEP)
        for group in range(per_step):
            out_ref[group, pl.ds(at, STEP), :] = blank

    order = order_ref[...]
    order_sq = order * order
    cosine = jnp.broadcast_to(cosine_ref[...], (slots, lat_total))
    wide = lat_total // 128

    def spread(x):
        return jnp.concatenate([x] * wide, axis=1)

    seeds = seeds_ref[...]
    zero = jnp.zeros((slots, lat_total), F32)
    start = (zero, zero, seeds, jnp.zeros((slots, 128), F32))

    def advance(block, carry):
        fresh, before, log_scale, coeff_b = carry
        at = pl.multiple_of(block * STEP, STEP)
        scale = jnp.exp(log_scale)
        for step in range(STEP):
            degree = base + at + step
            degree_v = jnp.full((slots, 128), degree.astype(F32), F32)
            ratio = jnp.maximum(degree_v * degree_v - order_sq, 1.0) * inverse_ref[degree]
            root = lax.rsqrt(ratio)
            root = root * (1.5 - 0.5 * ratio * root * root)
            starts = jnp.where(degree_v == order, 1.0, 0.0)
            grown = spread(root) * (cosine * fresh - spread(coeff_b) * before) + spread(starts)
            coeff_b = ratio * root
            before, fresh = fresh, grown
            rows_ref[step] = grown * scale
        size = jnp.abs(fresh) + jnp.abs(before)
        size = jnp.where(size == 0.0, 1.0, size)
        inverse = 1.0 / size
        for slot in range(slots):
            cut = slice((slot % 2) * lat_total, (slot % 2 + 1) * lat_total)
            out_ref[slot // 2, pl.ds(at, STEP), cut] = rows_ref[:, slot, :].astype(out_ref.dtype)
        return (fresh * inverse, before * inverse, log_scale + jnp.log(size), coeff_b)

    lax.fori_loop(first_block, depth // STEP, advance, start)


def legendre_table(plan, seeds, orders_f, cosine, degrees, after=()):
    order_count, lat_total = seeds.shape
    groups = order_count // 2
    per_step = max(n for n in range(1, 9) if groups % n == 0)
    slots = 2 * per_step
    base = plan["base"]
    depth = degrees - base
    order_wide = jnp.broadcast_to(orders_f[:, None], (order_count, 128))
    steps = groups // per_step
    seeds = seeds.reshape(steps, slots, lat_total)
    order_wide = order_wide.reshape(steps, slots, 128)
    at = np.arange(degrees, dtype=np.float32)
    inverse = jnp.asarray((1.0 / np.maximum(4.0 * at * at - 1.0, 1.0)).astype(np.float32))
    spec = pltpu.PrefetchScalarGridSpec(
        num_scalar_prefetch=1,
        grid=(steps,),
        in_specs=[
            pl.BlockSpec((None, slots, lat_total), lambda i, v: (i, 0, 0)),
            pl.BlockSpec((None, slots, 128), lambda i, v: (i, 0, 0)),
            pl.BlockSpec((1, lat_total), lambda i, v: (0, 0)),
        ]
        + [HELD] * len(after),
        out_specs=pl.BlockSpec((per_step, depth, 2 * lat_total), lambda i, v: (i, 0, 0)),
        scratch_shapes=[pltpu.VMEM((STEP, slots, lat_total), F32)],
    )
    return pl.pallas_call(
        functools.partial(table_body, plan["group_rows"], plan["groups"], base),
        grid_spec=spec,
        out_shape=jax.ShapeDtypeStruct((groups, depth, 2 * lat_total), BF16),
        compiler_params=params(),
        cost_estimate=LIGHT,
        name="legendre_table",
    )(inverse, seeds, order_wide, cosine[None, :], *after)


def parity_lanes(lanes):
    second = (np.arange(lanes) % (lanes // 2)) >= lanes // 4
    return jnp.asarray(np.stack([1.0 - second, second]).astype(np.float32)).astype(BF16)


def by_parity(rows, lanes_ref):
    return jnp.concatenate([rows * lanes_ref[0:1, :], rows * lanes_ref[1:2, :]], axis=0)


def analyse_body(plan, count_ref, chan_ref, fourier_ref, table_ref, gain_ref, cross_ref, lanes_ref, *refs):
    outs, packed = refs[-1 - plan["chans"]:-1], refs[-1]
    step = pl.program_id(0)
    depth = table_ref.shape[0]
    lat_total = table_ref.shape[1] // 2
    lanes = fourier_ref.shape[-1]
    part = plan["part"]
    base = plan["base"]
    start = pl.multiple_of(count_ref[step], STEP)

    @pl.when(step == 0)
    def _():
        tail = plan["pad"] + plan["rows"]
        left = packed.shape[0] - tail
        if left:
            packed[tail:, :] = jnp.zeros((left, lanes), packed.dtype)

    rows_in = by_parity(fourier_ref[...].reshape(lat_total, lanes), lanes_ref)
    both = jnp.dot(table_ref[...], rows_in, preferred_element_type=F32)
    swapped = pltpu.roll(both, lanes // 2, 1)
    kept = both * gain_ref[base:, :] + swapped * cross_ref[base:, :]
    packed[pl.ds(start, depth), :] = kept.astype(packed.dtype)

    @pl.when(step == pl.num_programs(0) - 1)
    def _():
        for shift, out in enumerate(outs):
            owner = lax.rem(chan_ref[0] + shift, len(outs))
            at = pl.multiple_of(plan["pad"] + owner * part, STEP)
            out[...] = packed[pl.ds(at, part), :]


def chunk_plan(groups, group_rows, degrees, chan_count):
    sizes = [degrees - group_rows * g for g in groups]
    offsets = [sum(sizes[:i]) for i in range(len(groups))]
    rows = sum(sizes)
    unit = STEP * chan_count
    total = -(-rows // unit) * unit
    base = group_rows * groups[0]
    skips = [group_rows * g - base for g in groups]
    pad = max([skip - o for skip, o in zip(skips, offsets)] + [0])
    pad = -(-pad // STEP) * STEP
    starts = [pad + o - skip for skip, o in zip(skips, offsets)]
    return {
        "base": base, "skips": skips, "group_rows": group_rows, "chans": chan_count,
        "groups": groups, "rows": rows, "total": total, "part": total // chan_count,
        "pad": pad, "starts": starts,
    }


def analyse(plan, chan, fourier, table, gain, cross, chan_count, after=()):
    bands, count, band_rows, lanes = fourier.shape
    _, depth, lat_wide = table.shape
    starts = jnp.asarray(np.array(plan["starts"][::-1], np.int32))
    spec = pltpu.PrefetchScalarGridSpec(
        num_scalar_prefetch=2,
        grid=(count,),
        in_specs=[
            pl.BlockSpec((bands, None, band_rows, lanes), lambda i, s, c: (0, count - 1 - i, 0, 0)),
            pl.BlockSpec((None, depth, lat_wide), lambda i, s, c: (count - 1 - i, 0, 0)),
            pl.BlockSpec(gain.shape, lambda i, s, c: (0, 0)),
            pl.BlockSpec(cross.shape, lambda i, s, c: (0, 0)),
            pl.BlockSpec((2, lanes), lambda i, s, c: (0, 0)),
        ]
        + [HELD] * len(after),
        out_specs=[pl.BlockSpec((plan["part"], lanes), lambda i, s, c: (0, 0))] * chan_count,
        scratch_shapes=[pltpu.VMEM((plan["pad"] + plan["total"], lanes), BF16)],
    )
    return pl.pallas_call(
        functools.partial(analyse_body, plan),
        grid_spec=spec,
        out_shape=[jax.ShapeDtypeStruct((plan["part"], lanes), BF16)] * chan_count,
        compiler_params=params(),
        cost_estimate=LIGHT,
        name="analyse",
    )(starts, chan, fourier, table, gain, cross, parity_lanes(lanes), *after)


def kernel_body(mix_ref, *refs):
    out_ref = refs[-1]
    real, imag = mix_ref[0], mix_ref[1]
    quarter = real.shape[0]
    table = [[real, imag], [-imag, real]]
    for target in range(out_ref.shape[0]):
        cut = slice(target * quarter, (target + 1) * quarter)
        for t in range(2):
            row = [table[t][u][:, cut] for u in range(2)]
            out_ref[target, t * quarter:(t + 1) * quarter, :] = jnp.concatenate(row, axis=1)


def mix_kernel(channel_mix, chan_count, after=()):
    channels = channel_mix.shape[1]
    quarter = channels // chan_count
    wide = 2 * quarter
    return pl.pallas_call(
        kernel_body,
        grid=(chan_count,),
        in_specs=[pl.BlockSpec((2, quarter, channels), lambda i: (0, i, 0))] + [HELD] * len(after),
        out_specs=pl.BlockSpec((None, chan_count, wide, wide), lambda i: (i, 0, 0, 0)),
        out_shape=jax.ShapeDtypeStruct((chan_count, chan_count, wide, wide), BF16),
        compiler_params=params(),
        cost_estimate=HEAVY,
        name="mix_kernel",
    )(channel_mix, *after)


def mix_body(chan_count, chan_ref, *refs):
    ins, kernel_ref, outs = refs[:chan_count], refs[chan_count], refs[-chan_count:]
    own = chan_ref[0]
    quarter = ins[0].shape[1] // 4
    sources = [lax.rem(own + (chan_count - back), chan_count) for back in range(chan_count)]
    left = []
    for e in range(2):
        pieces = []
        for part in ins:
            for t in range(2):
                at = (2 * t + e) * quarter
                pieces.append(part[:, at:at + quarter])
        left.append(jnp.concatenate(pieces, axis=1))
    for shift, out in enumerate(outs):
        target = lax.rem(own + shift, chan_count)
        right = jnp.concatenate([kernel_ref[source, target] for source in sources], axis=0)
        made = [jnp.dot(x, right, preferred_element_type=F32).astype(out.dtype) for x in left]
        out[...] = jnp.concatenate(
            [made[e][:, u * quarter:(u + 1) * quarter] for u in range(2) for e in range(2)], axis=1
        )


def mix(chan, parts, kernel, after=()):
    chan_count = len(parts)
    rows, lanes = parts[0].shape
    spec = pltpu.PrefetchScalarGridSpec(
        num_scalar_prefetch=1,
        grid=(1,),
        in_specs=[pl.BlockSpec((rows, lanes), lambda i, c: (0, 0))] * chan_count
        + [pl.BlockSpec(kernel.shape, lambda i, c: (0, 0, 0, 0))]
        + [HELD] * len(after),
        out_specs=[pl.BlockSpec((rows, lanes), lambda i, c: (0, 0))] * chan_count,
    )
    return pl.pallas_call(
        functools.partial(mix_body, chan_count),
        grid_spec=spec,
        out_shape=[jax.ShapeDtypeStruct((rows, lanes), BF16)] * chan_count,
        compiler_params=params(),
        cost_estimate=HEAVY,
        name="mix",
    )(chan, *parts, kernel, *after)


BAND = 16


def swap_matrix():
    at = np.arange(BAND * BAND)
    turned = (at % BAND) * BAND + at // BAND
    return jnp.asarray(np.eye(BAND * BAND, dtype=np.float32)[turned]).astype(BF16)


def forward_body(first_row, counts, weight_ref, signal_ref, trig_ref, swap_ref, *refs):
    outs, held_ref = refs[-1 - len(counts):-1], refs[-1]
    band, quarter, lon_count = signal_ref.shape
    bands = outs[0].shape[0]
    lanes = outs[0].shape[-1]
    rows = sum(counts) * bands
    flat = signal_ref[...].reshape(band * quarter, lon_count)
    base = pl.program_id(0) * band
    trig = trig_ref[:, first_row:first_row + rows, :].reshape(4 * rows, lon_count)
    spectrum = lax.dot_general(flat, trig, (((1,), (1,)), ((), ())), preferred_element_type=F32)
    for j in range(band):
        piece = (spectrum[j * quarter:(j + 1) * quarter] * weight_ref[base + j]).astype(BF16).T
        held_ref[j] = jnp.concatenate([piece[q * rows:(q + 1) * rows] for q in range(4)], axis=1)
    first = 0
    for out_ref, count in zip(outs, counts):
        for at in range(0, count * bands, BAND):
            block = held_ref[:, first + at:first + at + BAND, :].reshape(band * BAND, lanes)
            turned = jnp.dot(swap_ref[...], block, preferred_element_type=F32).astype(BF16)
            for r in range(BAND):
                g, k = divmod(at + r, bands)
                out_ref[k, g] = turned[r * band:(r + 1) * band]
        first += count * bands


def forward_rows(signal, trig, weight, swap, first_row, counts, lat_count, cost, after=()):
    lat_rows, quarter, lon_count = signal.shape
    rows = sum(counts) * lat_count
    lanes = 4 * quarter
    spec = pltpu.PrefetchScalarGridSpec(
        num_scalar_prefetch=1,
        grid=(lat_rows // BAND,),
        in_specs=[
            pl.BlockSpec((BAND, quarter, lon_count), lambda i, w: (i, 0, 0)),
            pl.BlockSpec(trig.shape, lambda i, w: (0, 0, 0)),
            pl.BlockSpec(swap.shape, lambda i, w: (0, 0)),
        ]
        + [HELD] * len(after),
        out_specs=[pl.BlockSpec((lat_count, n, BAND, lanes), lambda i, w: (0, 0, i, 0)) for n in counts],
        scratch_shapes=[pltpu.VMEM((BAND, rows, lanes), BF16)],
    )
    return pl.pallas_call(
        functools.partial(forward_body, first_row, counts),
        grid_spec=spec,
        out_shape=[jax.ShapeDtypeStruct((lat_count, n, lat_rows, lanes), BF16) for n in counts],
        compiler_params=params(),
        cost_estimate=cost,
        name="forward_rows",
    )(weight, signal, trig, swap, *after)


def inverse_body(counts, synth_ref, swap_ref, *refs):
    ins, out_ref, held_ref, turned_ref = refs[:-3], refs[-3], refs[-2], refs[-1]
    band, quarter, lon_count = out_ref.shape
    bands = ins[0].shape[0]
    lanes = held_ref.shape[-1]
    first = 0
    for part, count in zip(ins, counts):
        for at in range(0, count * bands, BAND):
            tiles = [part[(at + r) % bands, (at + r) // bands] for r in range(BAND)]
            block = jnp.concatenate(tiles, axis=0)
            turned = jnp.dot(swap_ref[...], block, preferred_element_type=F32).astype(BF16)
            held_ref[:, first + at:first + at + BAND, :] = turned.reshape(band, BAND, lanes)
        first += count * bands

    @pl.loop(0, band, unroll=4)
    def _(j):
        across = held_ref[j].T
        turned_ref[j] = jnp.concatenate(
            [across[q * quarter:(q + 1) * quarter] for q in range(4)], axis=1
        )

    split = 4
    @pl.loop(0, band // split)
    def _(block):
        at = block * split
        left = turned_ref[pl.ds(at, split)].reshape(split * quarter, turned_ref.shape[-1])
        total = jnp.dot(left, synth_ref[...], preferred_element_type=F32)
        out_ref[pl.ds(at, split)] = total.astype(out_ref.dtype).reshape(split, quarter, lon_count)


def inverse_rows(parts, synth, swap, lat_rows, quarter):
    lat_count = parts[0].shape[0]
    counts = [p.shape[1] for p in parts]
    rows = synth.shape[1]
    lon_count = synth.shape[2]
    lanes = 4 * quarter
    synth = synth.reshape(4 * rows, lon_count)
    return pl.pallas_call(
        functools.partial(inverse_body, counts),
        grid=(lat_rows // BAND,),
        in_specs=[
            pl.BlockSpec(synth.shape, lambda i: (0, 0)),
            pl.BlockSpec(swap.shape, lambda i: (0, 0)),
        ]
        + [pl.BlockSpec((lat_count, n, BAND, lanes), lambda i: (0, 0, i, 0)) for n in counts],
        out_specs=pl.BlockSpec((BAND, quarter, lon_count), lambda i: (i, 0, 0)),
        out_shape=jax.ShapeDtypeStruct((lat_rows, quarter, lon_count), BF16),
        scratch_shapes=[
            pltpu.VMEM((BAND, rows, lanes), BF16),
            pltpu.VMEM((BAND, quarter, 4 * rows), BF16),
        ],
        compiler_params=params(),
        cost_estimate=LIGHT,
        name="inverse_rows",
    )(synth, swap, *parts)


def synthesise_body(plan, count_ref, chan_ref, table_ref, lanes_ref, *refs):
    chan_count = plan["chans"]
    ins, out_ref, packed = refs[:chan_count], refs[-2], refs[-1]
    step = pl.program_id(0)
    depth = table_ref.shape[0]
    lat_total = table_ref.shape[1] // 2
    part = plan["part"]

    @pl.when(step == 0)
    def _():
        for shift, part_ref in enumerate(ins):
            owner = lax.rem(chan_ref[0] + (chan_count - shift), chan_count)
            at = pl.multiple_of(plan["pad"] + owner * part, STEP)
            packed[pl.ds(at, part), :] = part_ref[...]

    start = pl.multiple_of(count_ref[0, step], STEP)
    below = count_ref[1, step]
    rows = packed[pl.ds(start, depth), :]
    held = lax.broadcasted_iota(jnp.int32, rows.shape, 0) >= below
    rows = by_parity(jnp.where(held, rows, jnp.zeros_like(rows)), lanes_ref)
    table = jnp.concatenate([table_ref[:, :lat_total], table_ref[:, lat_total:]], axis=0)
    both = lax.dot_general(table, rows, (((0,), (0,)), ((), ())), preferred_element_type=F32)
    out_ref[...] = both.astype(out_ref.dtype).reshape(out_ref.shape)


def synthesise(plan, chan, table, parts, bands, after=()):
    _, depth, lat_wide = table.shape
    count = len(plan["groups"])
    chan_count = len(parts)
    part, lanes = parts[0].shape
    lat_total = lat_wide // 2
    band_rows = lat_total // bands
    numbers = jnp.asarray(np.array([plan["starts"], plan["skips"]], np.int32))
    spec = pltpu.PrefetchScalarGridSpec(
        num_scalar_prefetch=2,
        grid=(count,),
        in_specs=[
            pl.BlockSpec((None, depth, lat_wide), lambda i, s, c: (i, 0, 0)),
            pl.BlockSpec((2, lanes), lambda i, s, c: (0, 0)),
        ]
        + [pl.BlockSpec((part, lanes), lambda i, s, c: (0, 0))] * chan_count
        + [HELD] * len(after),
        out_specs=pl.BlockSpec((bands, None, band_rows, lanes), lambda i, s, c: (0, i, 0, 0)),
        scratch_shapes=[pltpu.VMEM((plan["pad"] + plan["total"], lanes), BF16)],
    )
    return pl.pallas_call(
        functools.partial(synthesise_body, plan),
        grid_spec=spec,
        out_shape=jax.ShapeDtypeStruct((bands, count, band_rows, lanes), BF16),
        compiler_params=params(),
        cost_estimate=HEAVY,
        name="synthesise",
    )(numbers, chan, table, parity_lanes(lanes), *parts, *after)


def split_groups(group_count, even):
    few = max(even, group_count // 6 // even * even)
    first = list(range(few))
    last = list(range(few, 2 * few))
    rest = list(range(2 * few, group_count))
    half = len(rest) * 5 // 8 // even * even
    return [p for p in (first, rest[:half], rest[half:], last) if p]


def on_device(signal, spectral_filter, channel_mix):
    lat_count = lax.axis_size("lat")
    chan_count = lax.axis_size("chan")
    lat_rows, quarter, lon_count = signal.shape
    lat_total = lat_rows * lat_count
    degrees = spectral_filter.shape[0]
    group_rows = 2 * lat_count
    group_count = degrees // group_rows
    lat_index = lax.axis_index("lat")
    chan_index = lax.axis_index("chan")
    chan = jnp.reshape(chan_index, (1,)).astype(jnp.int32)
    lanes = 4 * quarter

    kernels = lat_rows % BAND == 0 and quarter % BAND == 0 and (2 * lat_count) % BAND == 0 and group_count % 2 == 0
    pieces = split_groups(group_count, 2 if kernels else 1)

    e_at = jnp.arange(2, dtype=jnp.int32)
    group_orders = jnp.asarray(np.array([group_rows * g for p in pieces for g in p], np.int32))
    trig, synth = fourier_tables(group_orders, lat_count, lon_count)
    own_rows = lat_index * lat_rows + jnp.arange(lat_rows, dtype=jnp.int32)
    _, _, own_weight = latitude_terms(own_rows, lat_total, lon_count)
    cosine, log_sine, _ = latitude_terms(jnp.arange(lat_total, dtype=jnp.int32), lat_total, lon_count)
    orders_own = (group_orders[:, None] + 2 * lat_index + e_at[None, :]).reshape(-1)
    seeds = seed_logs(orders_own, log_sine)
    swap = swap_matrix()

    gains = lax.dynamic_slice_in_dim(spectral_filter, chan_index * quarter, quarter, 2)
    direct = jnp.tile(gains[:, 0, :], (1, 4))
    cross = jnp.concatenate([jnp.tile(-gains[:, 1, :], (1, 2)), jnp.tile(gains[:, 1, :], (1, 2))], 1)

    last_moved = [None] * chan_count

    def moved(parts):
        out = [parts[0]]
        for shift in range(1, chan_count):
            pairs = [(i, (i + shift) % chan_count) for i in range(chan_count)]
            part = parts[shift]
            if last_moved[shift] is not None:
                part = lax.optimization_barrier((part, last_moved[shift]))[0]
            last_moved[shift] = lax.ppermute(part, "chan", pairs)
            out.append(last_moved[shift])
        return out

    plans = [chunk_plan(groups, group_rows, degrees, chan_count) for groups in pieces]
    counts = [len(groups) for groups in pieces]
    edges = [sum(counts[:i]) for i in range(len(counts))]
    latest = [None]

    def queued(op, *args):
        held = tuple(x for x in latest if x is not None)
        del latest[1:]
        out = op(*args, after=held)
        latest[0] = out[0] if isinstance(out, (list, tuple)) else out
        return out

    chunks = len(plans)
    spectra, exchanged, tables, filtered, mixed, returned = {}, {}, {}, {}, {}, {}
    last_exchange = [None]

    def across_lat(x, *after):
        held = [a for a in after + (last_exchange[0],) if a is not None]
        if held:
            x = lax.optimization_barrier((x, *held))[0]
        last_exchange[0] = lax.all_to_all(x, "lat", split_axis=0, concat_axis=0, tiled=True)
        return last_exchange[0]

    def do_forward(which, cost):
        if kernels:
            first = edges[which[0]] * lat_count
            made = queued(
                forward_rows, signal, trig, own_weight, swap, first, [counts[i] for i in which],
                lat_count, cost
            )
            for i, out in zip(which, made):
                spectra[i] = out
            return
        for i in which:
            part = trig.reshape(4, group_count, lat_count, lon_count)[:, edges[i]:edges[i] + counts[i]]
            spectrum = jnp.einsum("jcn,qgkn->kgjqc", signal, part, preferred_element_type=F32)
            spectrum = (spectrum * own_weight[None, None, :, None, None]).astype(BF16)
            spectra[i] = spectrum.reshape(lat_count, counts[i], lat_rows, lanes)

    def do_exchange(i):
        exchanged[i] = across_lat(spectra[i])

    def do_table(i):
        own = slice(2 * edges[i], 2 * (edges[i] + counts[i]))
        tables[i] = queued(
            legendre_table, plans[i], seeds[own], orders_own[own].astype(F32), cosine, degrees
        )

    def do_analyse(i):
        filtered[i] = moved(queued(analyse, plans[i], chan, exchanged[i], tables[i], direct, cross, chan_count))

    def do_mix(i):
        mixed[i] = moved(queued(mix, chan, filtered[i], kernel))

    def do_synthesise(i):
        back = queued(synthesise, plans[i], chan, tables[i], mixed[i], lat_count)
        returned[i] = across_lat(back)

    do_forward([0, 1], LIGHT)
    do_exchange(0)
    do_table(0)
    do_analyse(0)
    do_exchange(1)
    kernel = queued(mix_kernel, channel_mix, chan_count)
    last = chunks - 1
    for i in range(1, chunks):
        do_table(i)
        do_analyse(i)
        if 1 < i < last:
            do_exchange(i + 1)
        if i == 1:
            do_forward(list(range(2, chunks)), HEAVY)
            do_exchange(2)
        if i <= 2:
            do_mix(i - 1)
    for i in range(max(chunks - 2, 0)):
        do_synthesise(i)
    for i in range(max(chunks - 2, 0), chunks):
        if i == last - 1 and i - 2 in returned:
            latest.append(returned[i - 2])
        if i not in mixed:
            do_mix(i)
    for i in range(max(chunks - 2, 0), chunks):
        if i == last - 1 and i - 1 in returned:
            latest.append(returned[i - 1])
        do_synthesise(i)
    returned = [returned[i] for i in range(chunks)]
    if kernels:
        return inverse_rows(returned, synth, swap, lat_rows, quarter)
    rows = jnp.concatenate(returned, 1).reshape(lat_count, group_count, lat_rows, 4, quarter)
    synth = synth.reshape(4, group_count, lat_count, lon_count)
    output = jnp.einsum("kgjqd,qgkn->jdn", rows, synth, preferred_element_type=F32)
    return output.astype(BF16)


def solution(mesh):
    return jax.shard_map(
        on_device,
        mesh=mesh,
        in_specs=(P("lat", "chan", None), P(), P()),
        out_specs=P("lat", "chan", None),
        check_vma=False,
    )
```

time: 579 us -> 350 us (0.60); the launches traced: 569 us -> 348 us
  waiting for transfers between devices: 200 us -> 80.8 us
  local copies, waits for them, and re-layouts: 103 us -> 14 us
  matrix products: 84 us -> 0 us
  Pallas kernels: 108 us -> 172 us
  starting transfers between devices: 48.1 us -> 68.4 us
  other arithmetic: 25.4 us -> 12.2 us
    ppermute x18 -> x24, waiting for transfers between devices: 151 us -> 15.3 us  [moved(): last_moved[shift] = lax.ppermute(part, 'chan', pairs)]
    dot_general x4 -> x0, matrix products: 84 us -> none  [the longest x1 51.1 us: on_device(): jnp.einsum('kgjued,uekgn->jdn', rows, synth, preferred_element_type=F32)]
    pallas_call x4 -> x12, Pallas kernels: 47.2 us -> 114 us  [the longest x4 37.1 us: legendre_table(): pl.pallas_call(functools.partial(table_body, plan['group_rows'], plan['gr...]
    reshape x4 -> x6, local copies, waits for them, and re-layouts: 43.6 us -> 4.6 us  [the longest x3 2.63 us: legendre_table(): seeds = seeds.reshape(steps, slots, lat_total)]
    mul x4 -> x2, local copies, waits for them, and re-layouts: 24 us -> 0.68 us  [fourier_tables(): forward * factor]
    all_to_all x6 -> x8, waiting for transfers between devices: 48.8 us -> 65.6 us  [across_lat(): lax.all_to_all(x, 'lat', split_axis=0, concat_axis=0, tiled=True)]
    convert_element_type x3 -> x4, local copies, waits for them, and re-layouts: 15.9 us -> 0.84 us  [do_table(): orders_own[own].astype(F32)]
    ppermute x18 -> x24, starting transfers between devices: 22.4 us -> 34.9 us  [moved(): last_moved[shift] = lax.ppermute(part, 'chan', pairs)]
  transfers between devices with their start and end apart: 24 -> 32, of which waited for: 19 -> 11; matrix products, arithmetic and copies ran while one was open for 17% -> 5% of each run, Pallas kernels for 19% -> 36%
where the time goes in v2:
time: 350 us; the launch traced here: 348 us
  Pallas kernels  172 us (49%)
  waiting for transfers between devices  80.8 us (23%)
  starting transfers between devices  68.4 us (20%)
  local copies, waits for them, and re-layouts  14 us (4%)
  other arithmetic  12.2 us (3%)
    all_to_all x8, waiting for transfers between devices, across_lat(): lax.all_to_all(x, 'lat', split_axis=0, concat_axis=0, tiled=True)  65.6 us
    pallas_call x4, Pallas kernels, legendre_table(): pl.pallas_call(functools.partial(table_body, plan['group_rows'], plan['gr...  37.1 us
    ppermute x24, starting transfers between devices, moved(): last_moved[shift] = lax.ppermute(part, 'chan', pairs)  34.9 us
    all_to_all x8, starting transfers between devices, across_lat(): lax.all_to_all(x, 'lat', split_axis=0, concat_axis=0, tiled=True)  33.5 us
    pallas_call x2, Pallas kernels, forward_rows(): pl.pallas_call(functools.partial(forward_body, first_row, counts), grid_s...  32.4 us
    pallas_call x4, Pallas kernels, analyse(): pl.pallas_call(functools.partial(analyse_body, plan), grid_spec=spec, out...  30 us
    pallas_call x4, Pallas kernels, synthesise(): pl.pallas_call(functools.partial(synthesise_body, plan), grid_spec=spec,...  27.7 us
    pallas_call x1, Pallas kernels, inverse_rows(): pl.pallas_call(functools.partial(inverse_body, counts), grid=(lat_rows //...  25.1 us
  transfers between devices with their start and end apart: 32, of which 11 were waited for; matrix products, arithmetic and copies ran while one was open for 5% of the time, Pallas kernels for 36%

profile of v2, /device:TPU:8, one launch (start us, length us, event | category | flops | bytes accessed | tf_op | source)
XLA Modules:
  0.0 348.0 jit_solution(1771453982352207210)
XLA Ops:
  6.0 16.4 %forward_rows.2 = (bf16[8,4,48,384]{3,2,1,0:T(8,128)(2,1)}, bf16[8,10,48,384]{3,2,1,0:T(8,128)(2,1)}) custom-call(f32[48]{0:T(128)} %sine_multiply_fusion.weight_ref, bf16[48,96,1440]{2,1,0:T(8,128)(2,1)} %signal_ref.3, bf16[4,192,1440]{2,1,0:T(8,128)(2,1)} %bitcast.21, bf16[256,256]{1,0:T(8,128)(2,1)} %constant.146.swap_ref), custom_call_target="tpu_custom_call" | custom-call | flops 1000 | bytes 1000 | tf_op jit(solution)/shard_map/forward_rows/pallas_call | solution.py:358
  22.5 3.9 %all-to-all-start = ((bf16[8,4,48,384]{3,2,1,0:T(8,128)(2,1)}), bf16[8,4,48,384]{3,2,1,0:T(8,128)(2,1)S(1)}, u32[]{:S(2)}, u32[]{:S(2)}) async-start(bf16[8,4,48,384]{3,2,1,0:T(8,128)(2,1)} %get-tuple-element.77.refs_0_), calls=%async_computation | async-start | bytes 2359296 | tf_op jit(solution)/shard_map/all_to_all | solution.py:552
  29.4 9.9 %legendre_table.4.table_ref.refs_0_ = bf16[4,384,768]{2,1,0:T(8,128)(2,1)} custom-call(f32[384]{0:T(512)} %constant.136.clone.inverse_ref, f32[1,8,384]{2,1,0:T(8,128)} %get-tuple-element.146.seeds_ref, f32[1,8,128]{2,1,0:T(8,128)} %reshape.436.order_ref, f32[1,384]{1,0:T(1,128)} %multiply_cosine_fusion.cosine_ref, ...), custom_call_target="tpu_custom_call" | custom-call | flops 1000 | bytes 1000 | tf_op jit(solution)/shard_map/legendre_table/pallas_call | solution.py:142
  46.8 4.4 %all-to-all-start.1 = ((bf16[8,10,48,384]{3,2,1,0:T(8,128)(2,1)}), bf16[8,10,48,384]{3,2,1,0:T(8,128)(2,1)}, u32[]{:S(2)}, u32[]{:S(2)}) async-start(bf16[8,10,48,384]{3,2,1,0:T(8,128)(2,1)} %get-tuple-element.83), calls=%async_computation.1 | async-start | bytes 5898240 | tf_op jit(solution)/shard_map/all_to_all | solution.py:552
  51.2 6.5 %analyse.4 = (bf16[368,384]{1,0:T(8,128)(2,1)}, bf16[368,384]{1,0:T(8,128)(2,1)}, bf16[368,384]{1,0:T(8,128)(2,1)}, bf16[368,384]{1,0:T(8,128)(2,1)}) custom-call(s32[4]{0:T(128)} %constant.137.clone.count_ref, s32[1]{0:T(128)} %bitcast.3.chan_ref, bf16[8,4,48,384]{3,2,1,0:T(8,128)(2,1)} %copy-done.4, bf16[4,384,768]{2,1,0:T(8,128)(2,1)} %legendre_table.4.table_ref.refs_0_, ...), custom_call_target="tpu_custom_call" | custom-call | flops 1000 | bytes 1000 | tf_op jit(solution)/shard_map/analyse/pallas_call | solution.py:228
  66.3 13.6 %legendre_table.5.table_ref.refs_0_ = bf16[10,256,768]{2,1,0:T(8,128)(2,1)} custom-call(f32[384]{0:T(512)} %constant.136.clone.inverse_ref, f32[2,10,384]{2,1,0:T(8,128)} %reshape.437.seeds_ref, f32[2,10,128]{2,1,0:T(8,128)} %broadcast_in_dim.10.order_ref, f32[1,384]{1,0:T(1,128)} %multiply_cosine_fusion.cosine_ref, ...), custom_call_target="tpu_custom_call" | custom-call | flops 1000 | bytes 1000 | tf_op jit(solution)/shard_map/legendre_table/pallas_call | solution.py:142
  79.9 7.0 %all-to-all-done.1.fourier_ref = bf16[8,10,48,384]{3,2,1,0:T(8,128)(2,1)} async-done(((bf16[8,10,48,384]{3,2,1,0:T(8,128)(2,1)}), bf16[8,10,48,384]{3,2,1,0:T(8,128)(2,1)}, u32[]{:S(2)}, u32[]{:S(2)}) %all-to-all-start.1) | async-done | bytes 2949152 | tf_op jit(solution)/shard_map/all_to_all | solution.py:552
  87.0 11.0 %analyse.5 = (bf16[464,384]{1,0:T(8,128)(2,1)}, bf16[464,384]{1,0:T(8,128)(2,1)}, bf16[464,384]{1,0:T(8,128)(2,1)}, bf16[464,384]{1,0:T(8,128)(2,1)}) custom-call(s32[10]{0:T(128)} %constant.139.clone.count_ref, s32[1]{0:T(128)} %bitcast.3.chan_ref, bf16[8,10,48,384]{3,2,1,0:T(8,128)(2,1)} %all-to-all-done.1.fourier_ref, ...), custom_call_target="tpu_custom_call" | custom-call | flops 1000 | bytes 1000 | tf_op jit(solution)/shard_map/analyse/pallas_call | solution.py:228
  103.2 16.0 %forward_rows.3 = (bf16[8,6,48,384]{3,2,1,0:T(8,128)(2,1)}, bf16[8,4,48,384]{3,2,1,0:T(8,128)(2,1)}) custom-call(f32[48]{0:T(128)} %sine_multiply_fusion.weight_ref, bf16[48,96,1440]{2,1,0:T(8,128)(2,1)} %signal_ref.3, bf16[4,192,1440]{2,1,0:T(8,128)(2,1)} %bitcast.22, bf16[256,256]{1,0:T(8,128)(2,1)} %constant.146.swap_ref, ...), custom_call_target="tpu_custom_call" | custom-call | flops 199999995904 | bytes 1000 | tf_op jit(solution)/shard_map/forward_rows/pallas_call | solution.py:358
  119.2 4.3 %all-to-all-start.2 = ((bf16[8,6,48,384]{3,2,1,0:T(8,128)(2,1)}), bf16[8,6,48,384]{3,2,1,0:T(8,128)(2,1)}, u32[]{:S(2)}, u32[]{:S(2)}) async-start(bf16[8,6,48,384]{3,2,1,0:T(8,128)(2,1)} %get-tuple-element.100.refs_5_), calls=%async_computation.2 | async-start | bytes 3538944 | tf_op jit(solution)/shard_map/all_to_all | solution.py:552
  123.5 4.3 %mix.4 = (bf16[368,384]{1,0:T(8,128)(2,1)}, bf16[368,384]{1,0:T(8,128)(2,1)}, bf16[368,384]{1,0:T(8,128)(2,1)}, bf16[368,384]{1,0:T(8,128)(2,1)}) custom-call(s32[1]{0:T(128)} %bitcast.3.chan_ref, bf16[368,384]{1,0:T(8,128)(2,1)} %get-tuple-element.78.refs_0_, bf16[368,384]{1,0:T(8,128)(2,1)} %collective-permute-done.refs_1_, ...), custom_call_target="tpu_custom_call" | custom-call | flops 199999995904 | bytes 1000 | tf_op jit(solution)/shard_map/mix/pallas_call | solution.py:299
  135.4 5.1 %legendre_table.6.table_ref.refs_0_ = bf16[6,96,768]{2,1,0:T(8,128)(2,1)} custom-call(f32[384]{0:T(512)} %constant.136.clone.inverse_ref, f32[1,12,384]{2,1,0:T(8,128)} %slice_bitcast_fusion.seeds_ref, f32[1,12,128]{2,1,0:T(8,128)} %reshape.441.order_ref, f32[1,384]{1,0:T(1,128)} %multiply_cosine_fusion.cosine_ref, bf16[368,384]{1,0:T(8,128)(2,1)} %get-tuple-element.86.refs_0_), custom_call_target="tpu_custom_call" | custom-call | flops 1000 | bytes 1000 | tf_op jit(solution)/shard_map/legendre_table/pallas_call | solution.py:142
  140.4 6.2 %all-to-all-done.2.fourier_ref = bf16[8,6,48,384]{3,2,1,0:T(8,128)(2,1)} async-done(((bf16[8,6,48,384]{3,2,1,0:T(8,128)(2,1)}), bf16[8,6,48,384]{3,2,1,0:T(8,128)(2,1)}, u32[]{:S(2)}, u32[]{:S(2)}) %all-to-all-start.2) | async-done | bytes 1769504 | tf_op jit(solution)/shard_map/all_to_all | solution.py:552
  146.6 4.2 %all-to-all-start.3 = ((bf16[8,4,48,384]{3,2,1,0:T(8,128)(2,1)}), bf16[8,4,48,384]{3,2,1,0:T(8,128)(2,1)}, u32[]{:S(2)}, u32[]{:S(2)}) async-start(bf16[8,4,48,384]{3,2,1,0:T(8,128)(2,1)} %get-tuple-element.101), calls=%async_computation.3 | async-start | bytes 2359296 | tf_op jit(solution)/shard_map/all_to_all | solution.py:552
  150.9 6.4 %analyse.6 = (bf16[96,384]{1,0:T(8,128)(2,1)}, bf16[96,384]{1,0:T(8,128)(2,1)}, bf16[96,384]{1,0:T(8,128)(2,1)}, bf16[96,384]{1,0:T(8,128)(2,1)}) custom-call(s32[6]{0:T(128)} %constant.140.clone.count_ref, s32[1]{0:T(128)} %bitcast.3.chan_ref, bf16[8,6,48,384]{3,2,1,0:T(8,128)(2,1)} %all-to-all-done.2.fourier_ref, ...), custom_call_target="tpu_custom_call" | custom-call | flops 1000 | bytes 1000 | tf_op jit(solution)/shard_map/analyse/pallas_call | solution.py:228
  161.3 4.8 %mix.5 = (bf16[464,384]{1,0:T(8,128)(2,1)}, bf16[464,384]{1,0:T(8,128)(2,1)}, bf16[464,384]{1,0:T(8,128)(2,1)}, bf16[464,384]{1,0:T(8,128)(2,1)}) custom-call(s32[1]{0:T(128)} %bitcast.3.chan_ref, bf16[464,384]{1,0:T(8,128)(2,1)} %get-tuple-element.84.refs_0_, bf16[464,384]{1,0:T(8,128)(2,1)} %collective-permute-done.3.refs_1_, ...), custom_call_target="tpu_custom_call" | custom-call | flops 199999995904 | bytes 1000 | tf_op jit(solution)/shard_map/mix/pallas_call | solution.py:299
  172.4 8.5 %legendre_table.7.table_ref.refs_0_ = bf16[4,320,768]{2,1,0:T(8,128)(2,1)} custom-call(f32[384]{0:T(512)} %constant.136.clone.inverse_ref, f32[1,8,384]{2,1,0:T(8,128)} %get-tuple-element.145.seeds_ref, f32[1,8,128]{2,1,0:T(8,128)} %reshape.439.order_ref, f32[1,384]{1,0:T(1,128)} %multiply_cosine_fusion.cosine_ref, bf16[464,384]{1,0:T(8,128)(2,1)} %get-tuple-element.103.refs_0_), custom_call_target="tpu_custom_call" | custom-call | flops 1000 | bytes 1000 | tf_op jit(solution)/shard_map/legendre_table/pallas_call | solution.py:142
  180.9 6.1 %analyse.7 = (bf16[304,384]{1,0:T(8,128)(2,1)}, bf16[304,384]{1,0:T(8,128)(2,1)}, bf16[304,384]{1,0:T(8,128)(2,1)}, bf16[304,384]{1,0:T(8,128)(2,1)}) custom-call(s32[4]{0:T(128)} %constant.141.clone.count_ref, s32[1]{0:T(128)} %bitcast.3.chan_ref, bf16[8,4,48,384]{3,2,1,0:T(8,128)(2,1)} %all-to-all-done.3.fourier_ref, ...), custom_call_target="tpu_custom_call" | custom-call | flops 1000 | bytes 1000 | tf_op jit(solution)/shard_map/analyse/pallas_call | solution.py:228
  187.1 5.5 %collective-permute-done.10.refs_1_ = bf16[464,384]{1,0:T(8,128)(2,1)S(1)} collective-permute-done((bf16[464,384]{1,0:T(8,128)(2,1)}, bf16[464,384]{1,0:T(8,128)(2,1)S(1)}, u32[]{:S(2)}, u32[]{:S(2)}) %collective-permute-start.10) | collective-permute-done | bytes 356384 | tf_op jit(solution)/shard_map/ppermute | solution.py:528
  192.6 6.0 %collective-permute-done.12.refs_2_ = bf16[464,384]{1,0:T(8,128)(2,1)S(1)} collective-permute-done((bf16[464,384]{1,0:T(8,128)(2,1)}, bf16[464,384]{1,0:T(8,128)(2,1)S(1)}, u32[]{:S(2)}, u32[]{:S(2)}) %collective-permute-start.12) | collective-permute-done | bytes 356384 | tf_op jit(solution)/shard_map/ppermute | solution.py:528
  200.9 5.7 %synthesise.4.refs_4_ = bf16[8,4,48,384]{3,2,1,0:T(8,128)(2,1)} custom-call(s32[2,4]{1,0:T(2,128)} %constant.142.clone.count_ref, s32[1]{0:T(128)} %bitcast.3.chan_ref, bf16[4,384,768]{2,1,0:T(8,128)(2,1)} %legendre_table.4.table_ref.refs_0_, bf16[2,384]{1,0:T(2,128)(2,1)} %constant.147.lanes_ref, bf16[368,384]{1,0:T(8,128)(2,1)} %get-tuple-element.86.refs_0_, ...), custom_call_target="tpu_custom_call" | custom-call | flops 199999995904 | bytes 1000 | tf_op jit(solution)/shard_map/synthesise/pallas_call | solution.py:470
  206.7 4.3 %all-to-all-start.4 = ((bf16[8,4,48,384]{3,2,1,0:T(8,128)(2,1)}), bf16[8,4,48,384]{3,2,1,0:T(8,128)(2,1)}, u32[]{:S(2)}, u32[]{:S(2)}) async-start(bf16[8,4,48,384]{3,2,1,0:T(8,128)(2,1)} %synthesise.4.refs_4_), calls=%async_computation.4 | async-start | bytes 2359296 | tf_op jit(solution)/shard_map/all_to_all | solution.py:552
  214.9 10.2 %synthesise.5.refs_5_ = bf16[8,10,48,384]{3,2,1,0:T(8,128)(2,1)} custom-call(s32[2,10]{1,0:T(2,128)} %constant.143.clone.count_ref, s32[1]{0:T(128)} %bitcast.3.chan_ref, bf16[10,256,768]{2,1,0:T(8,128)(2,1)} %legendre_table.5.table_ref.refs_0_, bf16[2,384]{1,0:T(2,128)(2,1)} %constant.147.lanes_ref, bf16[464,384]{1,0:T(8,128)(2,1)} %get-tuple-element.103.refs_0_, ...), custom_call_target="tpu_custom_call" | custom-call | flops 199999995904 | bytes 1000 | tf_op jit(solution)/shard_map/synthesise/pallas_call | solution.py:470
  227.8 4.4 %all-to-all-start.5 = ((bf16[8,10,48,384]{3,2,1,0:T(8,128)(2,1)}), bf16[8,10,48,384]{3,2,1,0:T(8,128)(2,1)}, u32[]{:S(2)}, u32[]{:S(2)}) async-start(bf16[8,10,48,384]{3,2,1,0:T(8,128)(2,1)} %synthesise.5.refs_5_), calls=%async_computation.5 | async-start | bytes 5898240 | tf_op jit(solution)/shard_map/all_to_all | solution.py:552
  239.2 4.1 %mix.7 = (bf16[304,384]{1,0:T(8,128)(2,1)}, bf16[304,384]{1,0:T(8,128)(2,1)}, bf16[304,384]{1,0:T(8,128)(2,1)}, bf16[304,384]{1,0:T(8,128)(2,1)}) custom-call(s32[1]{0:T(128)} %bitcast.3.chan_ref, bf16[304,384]{1,0:T(8,128)(2,1)} %get-tuple-element.104.refs_4_.refs_0_, bf16[304,384]{1,0:T(8,128)(2,1)} %collective-permute-done.15.refs_1_, ...), custom_call_target="tpu_custom_call" | custom-call | flops 199999995904 | bytes 1000 | tf_op jit(solution)/shard_map/mix/pallas_call | solution.py:299
  248.7 19.3 %all-to-all-done.5.refs_5_.refs_1_ = bf16[8,10,48,384]{3,2,1,0:T(8,128)(2,1)} async-done(((bf16[8,10,48,384]{3,2,1,0:T(8,128)(2,1)}), bf16[8,10,48,384]{3,2,1,0:T(8,128)(2,1)}, u32[]{:S(2)}, u32[]{:S(2)}) %all-to-all-start.5) | async-done | bytes 2949152 | tf_op jit(solution)/shard_map/all_to_all | solution.py:552
  268.1 6.1 %synthesise.6.refs_4_ = bf16[8,6,48,384]{3,2,1,0:T(8,128)(2,1)} custom-call(s32[2,6]{1,0:T(2,128)} %constant.144.clone.count_ref, s32[1]{0:T(128)} %bitcast.3.chan_ref, bf16[6,96,768]{2,1,0:T(8,128)(2,1)} %legendre_table.6.table_ref.refs_0_, bf16[2,384]{1,0:T(2,128)(2,1)} %constant.147.lanes_ref, bf16[96,384]{1,0:T(8,128)(2,1)} %get-tuple-element.119.refs_5_.refs_0_, ...), custom_call_target="tpu_custom_call" | custom-call | flops 199999995904 | bytes 1000 | tf_op jit(solution)/shard_map/synthesise/pallas_call | solution.py:470
  274.1 4.3 %all-to-all-start.6 = ((bf16[8,6,48,384]{3,2,1,0:T(8,128)(2,1)}), bf16[8,6,48,384]{3,2,1,0:T(8,128)(2,1)}, u32[]{:S(2)}, u32[]{:S(2)}) async-start(bf16[8,6,48,384]{3,2,1,0:T(8,128)(2,1)} %synthesise.6.refs_4_), calls=%async_computation.6 | async-start | bytes 3538944 | tf_op jit(solution)/shard_map/all_to_all | solution.py:552
  278.5 5.6 %synthesise.7 = bf16[8,4,48,384]{3,2,1,0:T(8,128)(2,1)} custom-call(s32[2,4]{1,0:T(2,128)} %constant.145.clone.count_ref, s32[1]{0:T(128)} %bitcast.3.chan_ref, bf16[4,320,768]{2,1,0:T(8,128)(2,1)} %legendre_table.7.table_ref.refs_0_, bf16[2,384]{1,0:T(2,128)(2,1)} %constant.147.lanes_ref, bf16[304,384]{1,0:T(8,128)(2,1)} %get-tuple-element.132.refs_4_.refs_0_, ...), custom_call_target="tpu_custom_call" | custom-call | flops 199999995904 | bytes 1000 | tf_op jit(solution)/shard_map/synthesise/pallas_call | solution.py:470
  284.1 17.5 %all-to-all-done.6.refs_2_ = bf16[8,6,48,384]{3,2,1,0:T(8,128)(2,1)} async-done(((bf16[8,6,48,384]{3,2,1,0:T(8,128)(2,1)}), bf16[8,6,48,384]{3,2,1,0:T(8,128)(2,1)}, u32[]{:S(2)}, u32[]{:S(2)}) %all-to-all-start.6) | async-done | bytes 1769504 | tf_op jit(solution)/shard_map/all_to_all | solution.py:552
  309.0 12.9 %all-to-all-done.7.refs_3_ = bf16[8,4,48,384]{3,2,1,0:T(8,128)(2,1)S(1)} async-done(((bf16[8,4,48,384]{3,2,1,0:T(8,128)(2,1)}), bf16[8,4,48,384]{3,2,1,0:T(8,128)(2,1)S(1)}, u32[]{:S(2)}, u32[]{:S(2)}) %all-to-all-start.7) | async-done | bytes 1179680 | tf_op jit(solution)/shard_map/all_to_all | solution.py:552
  323.0 25.1 %inverse_rows.1 = bf16[48,96,1440]{2,1,0:T(8,128)(2,1)} custom-call(bf16[768,1440]{1,0:T(8,128)(2,1)} %fusion.synth_ref, bf16[256,256]{1,0:T(8,128)(2,1)} %constant.146.swap_ref, bf16[8,4,48,384]{3,2,1,0:T(8,128)(2,1)} %all-to-all-done.4.refs_6_.refs_0_, bf16[8,10,48,384]{3,2,1,0:T(8,128)(2,1)} %all-to-all-done.5.refs_5_.refs_1_, ...), custom_call_target="tpu_custom_call" | custom-call | flops 1000 | bytes 1000 | tf_op jit(solution)/shard_map/inverse_rows/pallas_call | solution.py:405
  (139 shorter events, 77.8 us)
Async XLA Ops:
  22.5 23.3 %all-to-all-start = ((bf16[8,4,48,384]{3,2,1,0:T(8,128)(2,1)}), bf16[8,4,48,384]{3,2,1,0:T(8,128)(2,1)S(1)}, u32[]{:S(2)}, u32[]{:S(2)}) async-start(bf16[8,4,48,384]{3,2,1,0:T(8,128)(2,1)} %get-tuple-element.77.refs_0_), calls=%async_computation | async-start | bytes 2359296 | tf_op jit(solution)/shard_map/all_to_all | solution.py:552
  46.8 40.2 %all-to-all-start.1 = ((bf16[8,10,48,384]{3,2,1,0:T(8,128)(2,1)}), bf16[8,10,48,384]{3,2,1,0:T(8,128)(2,1)}, u32[]{:S(2)}, u32[]{:S(2)}) async-start(bf16[8,10,48,384]{3,2,1,0:T(8,128)(2,1)} %get-tuple-element.83), calls=%async_computation.1 | async-start | bytes 5898240 | tf_op jit(solution)/shard_map/all_to_all | solution.py:552
  57.7 40.3 %collective-permute-start = (bf16[368,384]{1,0:T(8,128)(2,1)}, bf16[368,384]{1,0:T(8,128)(2,1)}, u32[]{:S(2)}, u32[]{:S(2)}) collective-permute-start(bf16[368,384]{1,0:T(8,128)(2,1)} %get-tuple-element.79), channel_id=1, source_target_pairs={{0,1},{1,2},{2,3},{3,0},{4,5},{5,6},{6,7},{7,4},{8,9},{9,10},{10,1... | collective-permute-start | bytes 847880 | tf_op jit(solution)/shard_map/ppermute | solution.py:528
  59.2 38.8 %collective-permute-start.1 = (bf16[368,384]{1,0:T(8,128)(2,1)}, bf16[368,384]{1,0:T(8,128)(2,1)}, u32[]{:S(2)}, u32[]{:S(2)}) collective-permute-start(bf16[368,384]{1,0:T(8,128)(2,1)} %get-tuple-element.80), channel_id=1, source_target_pairs={{0,2},{1,3},{2,0},{3,1},{4,6},{5,7},{6,4},{7,5},{8,10},{9,11},{10,... | collective-permute-start | bytes 847880 | tf_op jit(solution)/shard_map/ppermute | solution.py:528
  60.5 37.5 %collective-permute-start.2 = (bf16[368,384]{1,0:T(8,128)(2,1)}, bf16[368,384]{1,0:T(8,128)(2,1)}, u32[]{:S(2)}, u32[]{:S(2)}) collective-permute-start(bf16[368,384]{1,0:T(8,128)(2,1)} %get-tuple-element.81), channel_id=1, source_target_pairs={{0,3},{1,0},{2,1},{3,2},{4,7},{5,4},{6,5},{7,6},{8,11},{9,8},{10,9... | collective-permute-start | bytes 847880 | tf_op jit(solution)/shard_map/ppermute | solution.py:528
  98.0 30.6 %collective-permute-start.7 = (bf16[464,384]{1,0:T(8,128)(2,1)}, bf16[464,384]{1,0:T(8,128)(2,1)}, u32[]{:S(2)}, u32[]{:S(2)}) collective-permute-start(bf16[464,384]{1,0:T(8,128)(2,1)} %get-tuple-element.97), channel_id=1, source_target_pairs={{0,3},{1,0},{2,1},{3,2},{4,7},{5,4},{6,5},{7,6},{8,11},{9,8},{10,9... | collective-permute-start | bytes 1069064 | tf_op jit(solution)/shard_map/ppermute | solution.py:528
  98.5 30.1 %collective-permute-start.5 = (bf16[464,384]{1,0:T(8,128)(2,1)}, bf16[464,384]{1,0:T(8,128)(2,1)}, u32[]{:S(2)}, u32[]{:S(2)}) collective-permute-start(bf16[464,384]{1,0:T(8,128)(2,1)} %get-tuple-element.93), channel_id=1, source_target_pairs={{0,2},{1,3},{2,0},{3,1},{4,6},{5,7},{6,4},{7,5},{8,10},{9,11},{10,... | collective-permute-start | bytes 1069064 | tf_op jit(solution)/shard_map/ppermute | solution.py:528
  101.0 27.6 %collective-permute-start.3 = (bf16[464,384]{1,0:T(8,128)(2,1)}, bf16[464,384]{1,0:T(8,128)(2,1)}, u32[]{:S(2)}, u32[]{:S(2)}) collective-permute-start(bf16[464,384]{1,0:T(8,128)(2,1)} %get-tuple-element.89), channel_id=1, source_target_pairs={{0,1},{1,2},{2,3},{3,0},{4,5},{5,6},{6,7},{7,4},{8,9},{9,10},{10,1... | collective-permute-start | bytes 1069064 | tf_op jit(solution)/shard_map/ppermute | solution.py:528
  119.2 27.5 %all-to-all-start.2 = ((bf16[8,6,48,384]{3,2,1,0:T(8,128)(2,1)}), bf16[8,6,48,384]{3,2,1,0:T(8,128)(2,1)}, u32[]{:S(2)}, u32[]{:S(2)}) async-start(bf16[8,6,48,384]{3,2,1,0:T(8,128)(2,1)} %get-tuple-element.100.refs_5_), calls=%async_computation.2 | async-start | bytes 3538944 | tf_op jit(solution)/shard_map/all_to_all | solution.py:552
  128.6 28.7 %collective-permute-start.8 = (bf16[368,384]{1,0:T(8,128)(2,1)}, bf16[368,384]{1,0:T(8,128)(2,1)S(1)}, u32[]{:S(2)}, u32[]{:S(2)}) collective-permute-start(bf16[368,384]{1,0:T(8,128)(2,1)} %get-tuple-element.98), channel_id=1, source_target_pairs={{0,3},{1,0},{2,1},{3,2},{4,7},{5,4},{6,5},{7,6},{8,11},{9,8},{10,9... | collective-permute-start | bytes 847880 | tf_op jit(solution)/shard_map/ppermute | solution.py:528
  129.8 27.5 %collective-permute-start.6 = (bf16[368,384]{1,0:T(8,128)(2,1)}, bf16[368,384]{1,0:T(8,128)(2,1)S(1)}, u32[]{:S(2)}, u32[]{:S(2)}) collective-permute-start(bf16[368,384]{1,0:T(8,128)(2,1)} %get-tuple-element.94), channel_id=1, source_target_pairs={{0,2},{1,3},{2,0},{3,1},{4,6},{5,7},{6,4},{7,5},{8,10},{9,11},{10,... | collective-permute-start | bytes 847880 | tf_op jit(solution)/shard_map/ppermute | solution.py:528
  132.6 24.8 %collective-permute-start.4 = (bf16[368,384]{1,0:T(8,128)(2,1)}, bf16[368,384]{1,0:T(8,128)(2,1)S(1)}, u32[]{:S(2)}, u32[]{:S(2)}) collective-permute-start(bf16[368,384]{1,0:T(8,128)(2,1)} %get-tuple-element.90), channel_id=1, source_target_pairs={{0,1},{1,2},{2,3},{3,0},{4,5},{5,6},{6,7},{7,4},{8,9},{9,10},{10,1... | collective-permute-start | bytes 847880 | tf_op jit(solution)/shard_map/ppermute | solution.py:528
  146.6 34.3 %all-to-all-start.3 = ((bf16[8,4,48,384]{3,2,1,0:T(8,128)(2,1)}), bf16[8,4,48,384]{3,2,1,0:T(8,128)(2,1)}, u32[]{:S(2)}, u32[]{:S(2)}) async-start(bf16[8,4,48,384]{3,2,1,0:T(8,128)(2,1)} %get-tuple-element.101), calls=%async_computation.3 | async-start | bytes 2359296 | tf_op jit(solution)/shard_map/all_to_all | solution.py:552
  157.4 13.5 %collective-permute-start.13 = (bf16[96,384]{1,0:T(8,128)(2,1)}, bf16[96,384]{1,0:T(8,128)(2,1)}, u32[]{:S(2)}, u32[]{:S(2)}) collective-permute-start(bf16[96,384]{1,0:T(8,128)(2,1)} %get-tuple-element.116), channel_id=1, source_target_pairs={{0,3},{1,0},{2,1},{3,2},{4,7},{5,4},{6,5},{7,6},{8,11},{9,8},{10,9... | collective-permute-start | bytes 221192 | tf_op jit(solution)/shard_map/ppermute | solution.py:528
  157.4 8.6 %collective-permute-start.11 = (bf16[96,384]{1,0:T(8,128)(2,1)}, bf16[96,384]{1,0:T(8,128)(2,1)}, u32[]{:S(2)}, u32[]{:S(2)}) collective-permute-start(bf16[96,384]{1,0:T(8,128)(2,1)} %get-tuple-element.112), channel_id=1, source_target_pairs={{0,2},{1,3},{2,0},{3,1},{4,6},{5,7},{6,4},{7,5},{8,10},{9,11},{10,... | collective-permute-start | bytes 221192 | tf_op jit(solution)/shard_map/ppermute | solution.py:528
  158.9 7.2 %collective-permute-start.9 = (bf16[96,384]{1,0:T(8,128)(2,1)}, bf16[96,384]{1,0:T(8,128)(2,1)}, u32[]{:S(2)}, u32[]{:S(2)}) collective-permute-start(bf16[96,384]{1,0:T(8,128)(2,1)} %get-tuple-element.108), channel_id=1, source_target_pairs={{0,1},{1,2},{2,3},{3,0},{4,5},{5,6},{6,7},{7,4},{8,9},{9,10},{10,1... | collective-permute-start | bytes 221192 | tf_op jit(solution)/shard_map/ppermute | solution.py:528
  166.1 26.5 %collective-permute-start.10 = (bf16[464,384]{1,0:T(8,128)(2,1)}, bf16[464,384]{1,0:T(8,128)(2,1)S(1)}, u32[]{:S(2)}, u32[]{:S(2)}) collective-permute-start(bf16[464,384]{1,0:T(8,128)(2,1)} %get-tuple-element.109), channel_id=1, source_target_pairs={{0,1},{1,2},{2,3},{3,0},{4,5},{5,6},{6,7},{7,4},{8,9},{9,10},{10,1... | collective-permute-start | bytes 1069064 | tf_op jit(solution)/shard_map/ppermute | solution.py:528
  168.2 30.4 %collective-permute-start.12 = (bf16[464,384]{1,0:T(8,128)(2,1)}, bf16[464,384]{1,0:T(8,128)(2,1)S(1)}, u32[]{:S(2)}, u32[]{:S(2)}) collective-permute-start(bf16[464,384]{1,0:T(8,128)(2,1)} %get-tuple-element.113), channel_id=1, source_target_pairs={{0,2},{1,3},{2,0},{3,1},{4,6},{5,7},{6,4},{7,5},{8,10},{9,11},{10,... | collective-permute-start | bytes 1069064 | tf_op jit(solution)/shard_map/ppermute | solution.py:528
  170.9 30.1 %collective-permute-start.14 = (bf16[464,384]{1,0:T(8,128)(2,1)}, bf16[464,384]{1,0:T(8,128)(2,1)S(1)}, u32[]{:S(2)}, u32[]{:S(2)}) collective-permute-start(bf16[464,384]{1,0:T(8,128)(2,1)} %get-tuple-element.117), channel_id=1, source_target_pairs={{0,3},{1,0},{2,1},{3,2},{4,7},{5,4},{6,5},{7,6},{8,11},{9,8},{10,9... | collective-permute-start | bytes 1069064 | tf_op jit(solution)/shard_map/ppermute | solution.py:528
  206.7 21.1 %all-to-all-start.4 = ((bf16[8,4,48,384]{3,2,1,0:T(8,128)(2,1)}), bf16[8,4,48,384]{3,2,1,0:T(8,128)(2,1)}, u32[]{:S(2)}, u32[]{:S(2)}) async-start(bf16[8,4,48,384]{3,2,1,0:T(8,128)(2,1)} %synthesise.4.refs_4_), calls=%async_computation.4 | async-start | bytes 2359296 | tf_op jit(solution)/shard_map/all_to_all | solution.py:552
  211.0 24.2 %collective-permute-start.19 = (bf16[304,384]{1,0:T(8,128)(2,1)}, bf16[304,384]{1,0:T(8,128)(2,1)}, u32[]{:S(2)}, u32[]{:S(2)}) collective-permute-start(bf16[304,384]{1,0:T(8,128)(2,1)} %get-tuple-element.130), channel_id=1, source_target_pairs={{0,3},{1,0},{2,1},{3,2},{4,7},{5,4},{6,5},{7,6},{8,11},{9,8},{10,9... | collective-permute-start | bytes 700424 | tf_op jit(solution)/shard_map/ppermute | solution.py:528
  211.1 24.2 %collective-permute-start.17 = (bf16[304,384]{1,0:T(8,128)(2,1)}, bf16[304,384]{1,0:T(8,128)(2,1)}, u32[]{:S(2)}, u32[]{:S(2)}) collective-permute-start(bf16[304,384]{1,0:T(8,128)(2,1)} %get-tuple-element.126), channel_id=1, source_target_pairs={{0,2},{1,3},{2,0},{3,1},{4,6},{5,7},{6,4},{7,5},{8,10},{9,11},{10,... | collective-permute-start | bytes 700424 | tf_op jit(solution)/shard_map/ppermute | solution.py:528
  212.2 24.3 %collective-permute-start.15 = (bf16[304,384]{1,0:T(8,128)(2,1)}, bf16[304,384]{1,0:T(8,128)(2,1)}, u32[]{:S(2)}, u32[]{:S(2)}) collective-permute-start(bf16[304,384]{1,0:T(8,128)(2,1)} %get-tuple-element.122), channel_id=1, source_target_pairs={{0,1},{1,2},{2,3},{3,0},{4,5},{5,6},{6,7},{7,4},{8,9},{9,10},{10,1... | collective-permute-start | bytes 700424 | tf_op jit(solution)/shard_map/ppermute | solution.py:528
  227.8 40.2 %all-to-all-start.5 = ((bf16[8,10,48,384]{3,2,1,0:T(8,128)(2,1)}), bf16[8,10,48,384]{3,2,1,0:T(8,128)(2,1)}, u32[]{:S(2)}, u32[]{:S(2)}) async-start(bf16[8,10,48,384]{3,2,1,0:T(8,128)(2,1)} %synthesise.5.refs_5_), calls=%async_computation.5 | async-start | bytes 5898240 | tf_op jit(solution)/shard_map/all_to_all | solution.py:552
  235.2 8.0 %collective-permute-start.20 = (bf16[96,384]{1,0:T(8,128)(2,1)}, bf16[96,384]{1,0:T(8,128)(2,1)}, u32[]{:S(2)}, u32[]{:S(2)}) collective-permute-start(bf16[96,384]{1,0:T(8,128)(2,1)} %get-tuple-element.131), channel_id=1, source_target_pairs={{0,3},{1,0},{2,1},{3,2},{4,7},{5,4},{6,5},{7,6},{8,11},{9,8},{10,9... | collective-permute-start | bytes 221192 | tf_op jit(solution)/shard_map/ppermute | solution.py:528
  235.3 7.9 %collective-permute-start.18 = (bf16[96,384]{1,0:T(8,128)(2,1)}, bf16[96,384]{1,0:T(8,128)(2,1)}, u32[]{:S(2)}, u32[]{:S(2)}) collective-permute-start(bf16[96,384]{1,0:T(8,128)(2,1)} %get-tuple-element.127), channel_id=1, source_target_pairs={{0,2},{1,3},{2,0},{3,1},{4,6},{5,7},{6,4},{7,5},{8,10},{9,11},{10,... | collective-permute-start | bytes 221192 | tf_op jit(solution)/shard_map/ppermute | solution.py:528
  236.4 7.3 %collective-permute-start.16 = (bf16[96,384]{1,0:T(8,128)(2,1)}, bf16[96,384]{1,0:T(8,128)(2,1)}, u32[]{:S(2)}, u32[]{:S(2)}) collective-permute-start(bf16[96,384]{1,0:T(8,128)(2,1)} %get-tuple-element.123), channel_id=1, source_target_pairs={{0,1},{1,2},{2,3},{3,0},{4,5},{5,6},{6,7},{7,4},{8,9},{9,10},{10,1... | collective-permute-start | bytes 221192 | tf_op jit(solution)/shard_map/ppermute | solution.py:528
  243.8 34.7 %collective-permute-start.21 = (bf16[304,384]{1,0:T(8,128)(2,1)}, bf16[304,384]{1,0:T(8,128)(2,1)}, u32[]{:S(2)}, u32[]{:S(2)}) collective-permute-start(bf16[304,384]{1,0:T(8,128)(2,1)} %get-tuple-element.135), channel_id=1, source_target_pairs={{0,1},{1,2},{2,3},{3,0},{4,5},{5,6},{6,7},{7,4},{8,9},{9,10},{10,1... | collective-permute-start | bytes 700424 | tf_op jit(solution)/shard_map/ppermute | solution.py:528
  245.9 32.5 %collective-permute-start.23 = (bf16[304,384]{1,0:T(8,128)(2,1)}, bf16[304,384]{1,0:T(8,128)(2,1)}, u32[]{:S(2)}, u32[]{:S(2)}) collective-permute-start(bf16[304,384]{1,0:T(8,128)(2,1)} %get-tuple-element.139), channel_id=1, source_target_pairs={{0,3},{1,0},{2,1},{3,2},{4,7},{5,4},{6,5},{7,6},{8,11},{9,8},{10,9... | collective-permute-start | bytes 700424 | tf_op jit(solution)/shard_map/ppermute | solution.py:528
  246.4 32.1 %collective-permute-start.22 = (bf16[304,384]{1,0:T(8,128)(2,1)}, bf16[304,384]{1,0:T(8,128)(2,1)}, u32[]{:S(2)}, u32[]{:S(2)}) collective-permute-start(bf16[304,384]{1,0:T(8,128)(2,1)} %get-tuple-element.137), channel_id=1, source_target_pairs={{0,2},{1,3},{2,0},{3,1},{4,6},{5,7},{6,4},{7,5},{8,10},{9,11},{10,... | collective-permute-start | bytes 700424 | tf_op jit(solution)/shard_map/ppermute | solution.py:528
  274.1 27.5 %all-to-all-start.6 = ((bf16[8,6,48,384]{3,2,1,0:T(8,128)(2,1)}), bf16[8,6,48,384]{3,2,1,0:T(8,128)(2,1)}, u32[]{:S(2)}, u32[]{:S(2)}) async-start(bf16[8,6,48,384]{3,2,1,0:T(8,128)(2,1)} %synthesise.6.refs_4_), calls=%async_computation.6 | async-start | bytes 3538944 | tf_op jit(solution)/shard_map/all_to_all | solution.py:552
  301.6 20.3 %all-to-all-start.7 = ((bf16[8,4,48,384]{3,2,1,0:T(8,128)(2,1)}), bf16[8,4,48,384]{3,2,1,0:T(8,128)(2,1)S(1)}, u32[]{:S(2)}, u32[]{:S(2)}) async-start(bf16[8,4,48,384]{3,2,1,0:T(8,128)(2,1)} %synthesise.7), calls=%async_computation.7 | async-start | bytes 2359296 | tf_op jit(solution)/shard_map/all_to_all | solution.py:552
  (20 other events, 145.1 us)

commit v3 on v2

--- a/solution.py
+++ b/solution.py
@@ -15,6 +15,7 @@
 STEP = 16
 HELD = pl.BlockSpec(memory_space=pl.ANY)
 LIGHT = pl.CostEstimate(flops=1000, transcendentals=0, bytes_accessed=1000)
+MEDIUM = pl.CostEstimate(flops=10_000_000_000, transcendentals=0, bytes_accessed=1000)
 HEAVY = pl.CostEstimate(flops=200_000_000_000, transcendentals=0, bytes_accessed=1000)
 
 
@@ -61,12 +62,12 @@
     return base_term + ratio_term + order_f * log_sine[None, :]
 
 
-def table_body(group_rows, groups, base, inverse_ref, seeds_ref, order_ref, cosine_ref, *refs):
+def table_body(group_rows, first_group, base, inverse_ref, seeds_ref, order_ref, cosine_ref, swap_ref, *refs):
     out_ref, rows_ref = refs[-2:]
     depth = out_ref.shape[1]
     slots, lat_total = seeds_ref.shape
     per_step = slots // 2
-    first = (groups[0] + pl.program_id(0) * per_step) * group_rows - base
+    first = (first_group + pl.program_id(0) * per_step) * group_rows - base
     first_block = first // STEP
     blank = jnp.zeros((STEP, 2 * lat_total), out_ref.dtype)
 
@@ -102,24 +103,28 @@
             grown = spread(root) * (cosine * fresh - spread(coeff_b) * before) + spread(starts)
             coeff_b = ratio * root
             before, fresh = fresh, grown
-            rows_ref[step] = grown * scale
+            rows_ref[step] = (grown * scale).astype(rows_ref.dtype)
         size = jnp.abs(fresh) + jnp.abs(before)
         size = jnp.where(size == 0.0, 1.0, size)
         inverse = 1.0 / size
+        if slots == STEP:
+            rows = rows_ref[...].reshape(STEP * slots, lat_total)
+            turned = jnp.dot(swap_ref[...], rows, preferred_element_type=F32).astype(out_ref.dtype)
         for slot in range(slots):
             cut = slice((slot % 2) * lat_total, (slot % 2 + 1) * lat_total)
-            out_ref[slot // 2, pl.ds(at, STEP), cut] = rows_ref[:, slot, :].astype(out_ref.dtype)
+            made = turned[slot * STEP:(slot + 1) * STEP] if slots == STEP else rows_ref[:, slot, :]
+            out_ref[slot // 2, pl.ds(at, STEP), cut] = made.astype(out_ref.dtype)
         return (fresh * inverse, before * inverse, log_scale + jnp.log(size), coeff_b)
 
     lax.fori_loop(first_block, depth // STEP, advance, start)
 
 
-def legendre_table(plan, seeds, orders_f, cosine, degrees, after=()):
+def legendre_table(all_groups, group_rows, seeds, orders_f, cosine, degrees, cost, after=()):
     order_count, lat_total = seeds.shape
     groups = order_count // 2
     per_step = max(n for n in range(1, 9) if groups % n == 0)
     slots = 2 * per_step
-    base = plan["base"]
+    base = group_rows * all_groups[0]
     depth = degrees - base
     order_wide = jnp.broadcast_to(orders_f[:, None], (order_count, 128))
     steps = groups // per_step
@@ -134,19 +139,20 @@
             pl.BlockSpec((None, slots, lat_total), lambda i, v: (i, 0, 0)),
             pl.BlockSpec((None, slots, 128), lambda i, v: (i, 0, 0)),
             pl.BlockSpec((1, lat_total), lambda i, v: (0, 0)),
+            pl.BlockSpec((STEP * STEP, STEP * STEP), lambda i, v: (0, 0)),
         ]
         + [HELD] * len(after),
         out_specs=pl.BlockSpec((per_step, depth, 2 * lat_total), lambda i, v: (i, 0, 0)),
-        scratch_shapes=[pltpu.VMEM((STEP, slots, lat_total), F32)],
-    )
-    return pl.pallas_call(
-        functools.partial(table_body, plan["group_rows"], plan["groups"], base),
+        scratch_shapes=[pltpu.VMEM((STEP, slots, lat_total), BF16 if slots == STEP else F32)],
+    )
+    return pl.pallas_call(
+        functools.partial(table_body, group_rows, all_groups[0], base),
         grid_spec=spec,
         out_shape=jax.ShapeDtypeStruct((groups, depth, 2 * lat_total), BF16),
         compiler_params=params(),
-        cost_estimate=LIGHT,
+        cost_estimate=cost,
         name="legendre_table",
-    )(inverse, seeds, order_wide, cosine[None, :], *after)
+    )(inverse, seeds, order_wide, cosine[None, :], swap_matrix(), *after)
 
 
 def parity_lanes(lanes):
@@ -207,16 +213,18 @@
     }
 
 
-def analyse(plan, chan, fourier, table, gain, cross, chan_count, after=()):
+def analyse(plan, chan, fourier, table, gain, cross, chan_count, cost, after=()):
     bands, count, band_rows, lanes = fourier.shape
-    _, depth, lat_wide = table.shape
+    table, first, row = table
+    _, whole, lat_wide = table.shape
+    depth = whole - row
     starts = jnp.asarray(np.array(plan["starts"][::-1], np.int32))
     spec = pltpu.PrefetchScalarGridSpec(
         num_scalar_prefetch=2,
         grid=(count,),
         in_specs=[
             pl.BlockSpec((bands, None, band_rows, lanes), lambda i, s, c: (0, count - 1 - i, 0, 0)),
-            pl.BlockSpec((None, depth, lat_wide), lambda i, s, c: (count - 1 - i, 0, 0)),
+            pl.BlockSpec((None, pl.Element(depth), pl.Element(lat_wide)), lambda i, s, c: (first + count - 1 - i, row, 0)),
             pl.BlockSpec(gain.shape, lambda i, s, c: (0, 0)),
             pl.BlockSpec(cross.shape, lambda i, s, c: (0, 0)),
             pl.BlockSpec((2, lanes), lambda i, s, c: (0, 0)),
@@ -230,9 +238,40 @@
         grid_spec=spec,
         out_shape=[jax.ShapeDtypeStruct((plan["part"], lanes), BF16)] * chan_count,
         compiler_params=params(),
-        cost_estimate=LIGHT,
+        cost_estimate=cost,
         name="analyse",
     )(starts, chan, fourier, table, gain, cross, parity_lanes(lanes), *after)
+
+
+def gain_body(chan_ref, filter_ref, direct_ref, cross_ref):
+    quarter = direct_ref.shape[1] // 4
+    channels = filter_ref.shape[1] // 2
+    for q in range(channels // quarter):
+        @pl.when(chan_ref[0] == q)
+        def _():
+            real = filter_ref[:, q * quarter:(q + 1) * quarter]
+            imag = filter_ref[:, channels + q * quarter:channels + (q + 1) * quarter]
+            direct_ref[...] = jnp.concatenate([real] * 4, axis=1)
+            cross_ref[...] = jnp.concatenate([-imag, -imag, imag, imag], axis=1)
+
+
+def gain_tables(spectral_filter, chan, quarter):
+    degrees = spectral_filter.shape[0]
+    table = jax.ShapeDtypeStruct((degrees, 4 * quarter), F32)
+    spec = pltpu.PrefetchScalarGridSpec(
+        num_scalar_prefetch=1,
+        grid=(1,),
+        in_specs=[pl.BlockSpec(spectral_filter.shape, lambda i, c: (0, 0))],
+        out_specs=[pl.BlockSpec(table.shape, lambda i, c: (0, 0))] * 2,
+    )
+    return pl.pallas_call(
+        gain_body,
+        grid_spec=spec,
+        out_shape=[table] * 2,
+        compiler_params=params(),
+        cost_estimate=LIGHT,
+        name="gain_tables",
+    )(chan, spectral_filter)
 
 
 def kernel_body(mix_ref, *refs):
@@ -285,7 +324,7 @@
         )
 
 
-def mix(chan, parts, kernel, after=()):
+def mix(chan, parts, kernel, cost, after=()):
     chan_count = len(parts)
     rows, lanes = parts[0].shape
     spec = pltpu.PrefetchScalarGridSpec(
@@ -301,7 +340,7 @@
         grid_spec=spec,
         out_shape=[jax.ShapeDtypeStruct((rows, lanes), BF16)] * chan_count,
         compiler_params=params(),
-        cost_estimate=HEAVY,
+        cost_estimate=cost,
         name="mix",
     )(chan, *parts, kernel, *after)
 
@@ -365,9 +404,8 @@
     )(weight, signal, trig, swap, *after)
 
 
-def inverse_body(counts, synth_ref, swap_ref, *refs):
-    ins, out_ref, held_ref, turned_ref = refs[:-3], refs[-3], refs[-2], refs[-1]
-    band, quarter, lon_count = out_ref.shape
+def turn_rows(counts, swap_ref, ins, held_ref, turned_ref):
+    band, quarter, _ = turned_ref.shape
     bands = ins[0].shape[0]
     lanes = held_ref.shape[-1]
     first = 0
@@ -386,30 +424,62 @@
             [across[q * quarter:(q + 1) * quarter] for q in range(4)], axis=1
         )
 
+
+def early_body(counts, swap_ref, *refs):
+    turn_rows(counts, swap_ref, refs[:-2], refs[-1], refs[-2])
+
+
+def early_rows(parts, swap, lat_rows, quarter):
+    lat_count = parts[0].shape[0]
+    counts = [p.shape[1] for p in parts]
+    rows = sum(counts) * lat_count
+    lanes = 4 * quarter
+    return pl.pallas_call(
+        functools.partial(early_body, counts),
+        grid=(lat_rows // BAND,),
+        in_specs=[pl.BlockSpec(swap.shape, lambda i: (0, 0))]
+        + [pl.BlockSpec((lat_count, n, BAND, lanes), lambda i: (0, 0, i, 0)) for n in counts],
+        out_specs=pl.BlockSpec((BAND, quarter, 4 * rows), lambda i: (i, 0, 0)),
+        out_shape=jax.ShapeDtypeStruct((lat_rows, quarter, 4 * rows), BF16),
+        scratch_shapes=[pltpu.VMEM((BAND, rows, lanes), BF16)],
+        compiler_params=params(),
+        cost_estimate=LIGHT,
+        name="early_rows",
+    )(swap, *parts)
+
+
+def inverse_body(counts, synth_ref, swap_ref, early_ref, part_ref, out_ref, held_ref, turned_ref):
+    band, quarter, lon_count = out_ref.shape
+    turn_rows(counts, swap_ref, [part_ref], held_ref, turned_ref)
     split = 4
+
     @pl.loop(0, band // split)
     def _(block):
         at = block * split
-        left = turned_ref[pl.ds(at, split)].reshape(split * quarter, turned_ref.shape[-1])
+        left = jnp.concatenate([early_ref[pl.ds(at, split)], turned_ref[pl.ds(at, split)]], axis=2)
+        left = left.reshape(split * quarter, left.shape[-1])
         total = jnp.dot(left, synth_ref[...], preferred_element_type=F32)
         out_ref[pl.ds(at, split)] = total.astype(out_ref.dtype).reshape(split, quarter, lon_count)
 
 
-def inverse_rows(parts, synth, swap, lat_rows, quarter):
-    lat_count = parts[0].shape[0]
-    counts = [p.shape[1] for p in parts]
-    rows = synth.shape[1]
+def inverse_rows(early, part, synth, swap):
+    lat_rows, quarter, wide = early.shape
+    lat_count, count, _, lanes = part.shape
+    rows = count * lat_count
     lon_count = synth.shape[2]
-    lanes = 4 * quarter
-    synth = synth.reshape(4 * rows, lon_count)
-    return pl.pallas_call(
-        functools.partial(inverse_body, counts),
+    first = wide // 4
+    synth = jnp.concatenate(
+        [synth[:, :first].reshape(wide, lon_count), synth[:, first:].reshape(4 * rows, lon_count)], 0
+    )
+    return pl.pallas_call(
+        functools.partial(inverse_body, [count]),
         grid=(lat_rows // BAND,),
         in_specs=[
             pl.BlockSpec(synth.shape, lambda i: (0, 0)),
             pl.BlockSpec(swap.shape, lambda i: (0, 0)),
-        ]
-        + [pl.BlockSpec((lat_count, n, BAND, lanes), lambda i: (0, 0, i, 0)) for n in counts],
+            pl.BlockSpec((BAND, quarter, wide), lambda i: (i, 0, 0)),
+            pl.BlockSpec((lat_count, count, BAND, lanes), lambda i: (0, 0, i, 0)),
+        ],
         out_specs=pl.BlockSpec((BAND, quarter, lon_count), lambda i: (i, 0, 0)),
         out_shape=jax.ShapeDtypeStruct((lat_rows, quarter, lon_count), BF16),
         scratch_shapes=[
@@ -419,7 +489,7 @@
         compiler_params=params(),
         cost_estimate=LIGHT,
         name="inverse_rows",
-    )(synth, swap, *parts)
+    )(synth, swap, early, part)
 
 
 def synthesise_body(plan, count_ref, chan_ref, table_ref, lanes_ref, *refs):
@@ -447,8 +517,10 @@
     out_ref[...] = both.astype(out_ref.dtype).reshape(out_ref.shape)
 
 
-def synthesise(plan, chan, table, parts, bands, after=()):
-    _, depth, lat_wide = table.shape
+def synthesise(plan, chan, table, parts, bands, cost, after=()):
+    table, first, row = table
+    _, whole, lat_wide = table.shape
+    depth = whole - row
     count = len(plan["groups"])
     chan_count = len(parts)
     part, lanes = parts[0].shape
@@ -459,7 +531,7 @@
         num_scalar_prefetch=2,
         grid=(count,),
         in_specs=[
-            pl.BlockSpec((None, depth, lat_wide), lambda i, s, c: (i, 0, 0)),
+            pl.BlockSpec((None, pl.Element(depth), pl.Element(lat_wide)), lambda i, s, c: (first + i, row, 0)),
             pl.BlockSpec((2, lanes), lambda i, s, c: (0, 0)),
         ]
         + [pl.BlockSpec((part, lanes), lambda i, s, c: (0, 0))] * chan_count
@@ -472,7 +544,7 @@
         grid_spec=spec,
         out_shape=jax.ShapeDtypeStruct((bands, count, band_rows, lanes), BF16),
         compiler_params=params(),
-        cost_estimate=HEAVY,
+        cost_estimate=cost,
         name="synthesise",
     )(numbers, chan, table, parity_lanes(lanes), *parts, *after)
 
@@ -483,7 +555,7 @@
     last = list(range(few, 2 * few))
     rest = list(range(2 * few, group_count))
     half = len(rest) * 5 // 8 // even * even
-    return [p for p in (first, rest[:half], rest[half:], last) if p]
+    return [first, rest[:half], rest[half:], last]
 
 
 def on_device(signal, spectral_filter, channel_mix):
@@ -492,6 +564,7 @@
     lat_rows, quarter, lon_count = signal.shape
     lat_total = lat_rows * lat_count
     degrees = spectral_filter.shape[0]
+    full_channels = channel_mix.shape[1]
     group_rows = 2 * lat_count
     group_count = degrees // group_rows
     lat_index = lax.axis_index("lat")
@@ -512,9 +585,7 @@
     seeds = seed_logs(orders_own, log_sine)
     swap = swap_matrix()
 
-    gains = lax.dynamic_slice_in_dim(spectral_filter, chan_index * quarter, quarter, 2)
-    direct = jnp.tile(gains[:, 0, :], (1, 4))
-    cross = jnp.concatenate([jnp.tile(-gains[:, 1, :], (1, 2)), jnp.tile(gains[:, 1, :], (1, 2))], 1)
+    direct, cross = gain_tables(spectral_filter.reshape(degrees, 2 * full_channels), chan, quarter)
 
     last_moved = [None] * chan_count
 
@@ -523,10 +594,10 @@
         for shift in range(1, chan_count):
             pairs = [(i, (i + shift) % chan_count) for i in range(chan_count)]
             part = parts[shift]
-            if last_moved[shift] is not None:
-                part = lax.optimization_barrier((part, last_moved[shift]))[0]
-            last_moved[shift] = lax.ppermute(part, "chan", pairs)
-            out.append(last_moved[shift])
+            if last_moved[0] is not None:
+                part = lax.optimization_barrier((part, last_moved[0]))[0]
+            out.append(lax.ppermute(part, "chan", pairs))
+        last_moved[0] = out[chan_count // 2]
         return out
 
     plans = [chunk_plan(groups, group_rows, degrees, chan_count) for groups in pieces]
@@ -571,53 +642,55 @@
     def do_exchange(i):
         exchanged[i] = across_lat(spectra[i])
 
-    def do_table(i):
-        own = slice(2 * edges[i], 2 * (edges[i] + counts[i]))
-        tables[i] = queued(
-            legendre_table, plans[i], seeds[own], orders_own[own].astype(F32), cosine, degrees
+    def do_table(which, cost):
+        which = sorted(which, key=lambda i: pieces[i][0])
+        joined = [g for i in which for g in pieces[i]]
+        own_seeds = jnp.concatenate([seeds[2 * edges[i]:2 * (edges[i] + counts[i])] for i in which], 0)
+        own_orders = jnp.concatenate([orders_own[2 * edges[i]:2 * (edges[i] + counts[i])] for i in which], 0)
+        table = queued(
+            legendre_table, joined, group_rows, own_seeds, own_orders.astype(F32), cosine, degrees, cost
         )
-
-    def do_analyse(i):
-        filtered[i] = moved(queued(analyse, plans[i], chan, exchanged[i], tables[i], direct, cross, chan_count))
-
-    def do_mix(i):
-        mixed[i] = moved(queued(mix, chan, filtered[i], kernel))
-
-    def do_synthesise(i):
-        back = queued(synthesise, plans[i], chan, tables[i], mixed[i], lat_count)
+        for i in which:
+            skip = pieces[i][0] - joined[0]
+            tables[i] = (table, skip, skip * group_rows)
+
+    def do_analyse(i, cost):
+        filtered[i] = moved(
+            queued(analyse, plans[i], chan, exchanged[i], tables[i], direct, cross, chan_count, cost)
+        )
+
+    def do_mix(i, cost):
+        mixed[i] = moved(queued(mix, chan, filtered[i], kernel, cost))
+
+    def do_synthesise(i, cost):
+        back = queued(synthesise, plans[i], chan, tables[i], mixed[i], lat_count, cost)
         returned[i] = across_lat(back)
 
     do_forward([0, 1], LIGHT)
     do_exchange(0)
-    do_table(0)
-    do_analyse(0)
+    do_table([0, 3], LIGHT)
+    do_analyse(0, LIGHT)
     do_exchange(1)
     kernel = queued(mix_kernel, channel_mix, chan_count)
-    last = chunks - 1
-    for i in range(1, chunks):
-        do_table(i)
-        do_analyse(i)
-        if 1 < i < last:
-            do_exchange(i + 1)
-        if i == 1:
-            do_forward(list(range(2, chunks)), HEAVY)
-            do_exchange(2)
-        if i <= 2:
-            do_mix(i - 1)
-    for i in range(max(chunks - 2, 0)):
-        do_synthesise(i)
-    for i in range(max(chunks - 2, 0), chunks):
-        if i == last - 1 and i - 2 in returned:
-            latest.append(returned[i - 2])
-        if i not in mixed:
-            do_mix(i)
-    for i in range(max(chunks - 2, 0), chunks):
-        if i == last - 1 and i - 1 in returned:
-            latest.append(returned[i - 1])
-        do_synthesise(i)
+    do_forward([2, 3], LIGHT)
+    do_mix(0, LIGHT)
+    do_exchange(2)
+    do_table([1, 2], HEAVY)
+    do_analyse(1, LIGHT)
+    do_exchange(3)
+    do_synthesise(0, HEAVY)
+    do_analyse(2, LIGHT)
+    do_mix(1, HEAVY)
+    do_analyse(3, LIGHT)
+    do_synthesise(1, MEDIUM)
+    do_mix(2, MEDIUM)
+    do_mix(3, MEDIUM)
+    do_synthesise(2, MEDIUM)
+    do_synthesise(3, HEAVY)
     returned = [returned[i] for i in range(chunks)]
     if kernels:
-        return inverse_rows(returned, synth, swap, lat_rows, quarter)
+        early = early_rows(returned[:-1], swap, lat_rows, quarter)
+        return inverse_rows(early, returned[-1], synth, swap)
     rows = jnp.concatenate(returned, 1).reshape(lat_count, group_count, lat_rows, 4, quarter)
     synth = synth.reshape(4, group_count, lat_count, lon_count)
     output = jnp.einsum("kgjqd,qgkn->jdn", rows, synth, preferred_element_type=F32)

time: 350 us -> 333 us (0.951)
  waiting for transfers between devices: 80.8 us -> 63.9 us
    all_to_all x8, waiting for transfers between devices: 65.6 us -> 32.8 us  [across_lat(): lax.all_to_all(x, 'lat', split_axis=0, concat_axis=0, tiled=True)]
    ppermute x24, waiting for transfers between devices: 15.3 us -> 31.2 us  [moved(): out.append(lax.ppermute(part, 'chan', pairs))]
    unnamed x40 -> x45, local copies, waits for them, and re-layouts: 2.89 us -> 8.47 us
    ppermute x24, starting transfers between devices: 34.9 us -> 38.7 us  [moved(): out.append(lax.ppermute(part, 'chan', pairs))]
  transfers between devices with their start and end apart: 32 -> 32, of which waited for: 11 -> 8; matrix products, arithmetic and copies ran while one was open for 5% -> 3% of each run, Pallas kernels for 36% -> 38%
where the time goes in v3:
time: 333 us; the launch traced here: 329 us
  Pallas kernels  170 us (51%)
  starting transfers between devices  71.4 us (21%)
  waiting for transfers between devices  63.9 us (19%)
  local copies, waits for them, and re-layouts  11.8 us (4%)
  other arithmetic  11.3 us (3%)
    ppermute x24, starting transfers between devices, moved(): out.append(lax.ppermute(part, 'chan', pairs))  38.7 us
    all_to_all x8, waiting for transfers between devices, across_lat(): lax.all_to_all(x, 'lat', split_axis=0, concat_axis=0, tiled=True)  32.8 us
    all_to_all x8, starting transfers between devices, across_lat(): lax.all_to_all(x, 'lat', split_axis=0, concat_axis=0, tiled=True)  32.7 us
    pallas_call x2, Pallas kernels, forward_rows(): pl.pallas_call(functools.partial(forward_body, first_row, counts), grid_s...  32.5 us
    ppermute x24, waiting for transfers between devices, moved(): out.append(lax.ppermute(part, 'chan', pairs))  31.2 us
    pallas_call x4, Pallas kernels, analyse(): pl.pallas_call(functools.partial(analyse_body, plan), grid_spec=spec, out...  30 us
    pallas_call x4, Pallas kernels, synthesise(): pl.pallas_call(functools.partial(synthesise_body, plan), grid_spec=spec,...  27.9 us
    pallas_call x2, Pallas kernels, legendre_table(): pl.pallas_call(functools.partial(table_body, group_rows, all_groups[0], b...  25 us
  transfers between devices with their start and end apart: 32, of which 8 were waited for; matrix products, arithmetic and copies ran while one was open for 3% of the time, Pallas kernels for 38%

profile of v3, /device:TPU:8, one launch (start us, length us, event | category | flops | bytes accessed | tf_op | source)
XLA Modules:
  0.0 328.9 jit_solution(11268088048410057980)
XLA Ops:
  7.4 16.5 %forward_rows.2 = (bf16[8,4,48,384]{3,2,1,0:T(8,128)(2,1)}, bf16[8,10,48,384]{3,2,1,0:T(8,128)(2,1)}) custom-call(f32[48]{0:T(128)} %sine_multiply_fusion.weight_ref, bf16[48,96,1440]{2,1,0:T(8,128)(2,1)} %signal_ref.3, bf16[4,192,1440]{2,1,0:T(8,128)(2,1)} %convert_element_type.110.trig_ref, bf16[256,256]{1,0:T(8,128)(2,1)} %constant.141.swap_ref), custom_call_target="tpu_custom_call" | custom-call | flops 1000 | bytes 1000 | tf_op jit(solution)/shard_map/forward_rows/pallas_call | solution.py:397
  24.0 3.9 %all-to-all-start = ((bf16[8,4,48,384]{3,2,1,0:T(8,128)(2,1)}), bf16[8,4,48,384]{3,2,1,0:T(8,128)(2,1)S(1)}, u32[]{:S(2)}, u32[]{:S(2)}) async-start(bf16[8,4,48,384]{3,2,1,0:T(8,128)(2,1)} %get-tuple-element.79.refs_0_), calls=%async_computation | async-start | bytes 2359296 | tf_op jit(solution)/shard_map/all_to_all | solution.py:623
  34.5 12.6 %legendre_table.2.table_ref.refs_0_ = bf16[8,384,768]{2,1,0:T(8,128)(2,1)} custom-call(f32[384]{0:T(512)} %constant.131.clone.inverse_ref, f32[1,16,384]{2,1,0:T(8,128)} %maximum_bitcast_fusion.seeds_ref, f32[1,16,128]{2,1,0:T(8,128)} %reshape.427.order_ref, f32[1,384]{1,0:T(1,128)} %multiply_cosine_fusion.cosine_ref, bf16[256,256]{1,0:T(8,128)(2,1)} %constant.141.swap_ref, ...), custom_call_target="tpu_custom_call" | custom-call | flops 1000 | bytes 1000 | tf_op jit(solution)/shard_map/legendre_table/pallas_call | solution.py:148
  49.7 6.5 %analyse.4 = (bf16[368,384]{1,0:T(8,128)(2,1)}, bf16[368,384]{1,0:T(8,128)(2,1)}, bf16[368,384]{1,0:T(8,128)(2,1)}, bf16[368,384]{1,0:T(8,128)(2,1)}) custom-call(s32[4]{0:T(128)} %constant.132.clone.count_ref, s32[1]{0:T(128)} %bitcast.5.chan_ref, bf16[8,4,48,384]{3,2,1,0:T(8,128)(2,1)} %copy-done.3, bf16[8,384,768]{2,1,0:T(8,128)(2,1)} %legendre_table.2.table_ref.refs_0_, ...), custom_call_target="tpu_custom_call" | custom-call | flops 1000 | bytes 1000 | tf_op jit(solution)/shard_map/analyse/pallas_call | solution.py:236
  60.5 3.7 %mix_kernel.1.refs_0_.refs_4_ = bf16[4,4,192,192]{3,2,1,0:T(8,128)(2,1)} custom-call(bf16[2,384,384]{2,1,0:T(8,128)(2,1)} %mix_ref.1, bf16[368,384]{1,0:T(8,128)(2,1)} %get-tuple-element.82.refs_0_), custom_call_target="tpu_custom_call" | custom-call | flops 199999995904 | bytes 1000 | tf_op jit(solution)/shard_map/mix_kernel/pallas_call | solution.py:293
  64.2 4.6 %all-to-all-start.1 = ((bf16[8,10,48,384]{3,2,1,0:T(8,128)(2,1)}), bf16[8,10,48,384]{3,2,1,0:T(8,128)(2,1)}, u32[]{:S(2)}, u32[]{:S(2)}) async-start(bf16[8,10,48,384]{3,2,1,0:T(8,128)(2,1)} %get-tuple-element.95), calls=%async_computation.1 | async-start | bytes 5898240 | tf_op jit(solution)/shard_map/all_to_all | solution.py:623
  68.8 16.0 %forward_rows.3 = (bf16[8,6,48,384]{3,2,1,0:T(8,128)(2,1)}, bf16[8,4,48,384]{3,2,1,0:T(8,128)(2,1)}) custom-call(f32[48]{0:T(128)} %sine_multiply_fusion.weight_ref, bf16[48,96,1440]{2,1,0:T(8,128)(2,1)} %signal_ref.3, bf16[4,192,1440]{2,1,0:T(8,128)(2,1)} %convert_element_type.110.trig_ref, bf16[256,256]{1,0:T(8,128)(2,1)} %constant.141.swap_ref, ...), custom_call_target="tpu_custom_call" | custom-call | flops 1000 | bytes 1000 | tf_op jit(solution)/shard_map/forward_rows/pallas_call | solution.py:397
  84.8 4.3 %mix.4 = (bf16[368,384]{1,0:T(8,128)(2,1)}, bf16[368,384]{1,0:T(8,128)(2,1)}, bf16[368,384]{1,0:T(8,128)(2,1)}, bf16[368,384]{1,0:T(8,128)(2,1)}) custom-call(s32[1]{0:T(128)} %bitcast.5.chan_ref, bf16[368,384]{1,0:T(8,128)(2,1)} %get-tuple-element.82.refs_0_, bf16[368,384]{1,0:T(8,128)(2,1)} %collective-permute-done.refs_1_, ...), custom_call_target="tpu_custom_call" | custom-call | flops 1000 | bytes 1000 | tf_op jit(solution)/shard_map/mix/pallas_call | solution.py:338
  94.2 12.4 %legendre_table.3.table_ref.refs_0_ = bf16[16,256,768]{2,1,0:T(8,128)(2,1)} custom-call(f32[384]{0:T(512)} %constant.131.clone.inverse_ref, f32[2,16,384]{2,1,0:T(8,128)} %bitcast.21, f32[2,16,128]{2,1,0:T(8,128)} %broadcast_in_dim.10.order_ref, f32[1,384]{1,0:T(1,128)} %multiply_cosine_fusion.cosine_ref, bf16[256,256]{1,0:T(8,128)(2,1)} %constant.141.swap_ref, ...), custom_call_target="tpu_custom_call" | custom-call | flops 199999995904 | bytes 1000 | tf_op jit(solution)/shard_map/legendre_table/pallas_call | solution.py:148
  106.6 4.3 %all-to-all-start.2 = ((bf16[8,6,48,384]{3,2,1,0:T(8,128)(2,1)}), bf16[8,6,48,384]{3,2,1,0:T(8,128)(2,1)}, u32[]{:S(2)}, u32[]{:S(2)}) async-start(bf16[8,6,48,384]{3,2,1,0:T(8,128)(2,1)} %get-tuple-element.98.refs_5_), calls=%async_computation.2 | async-start | bytes 3538944 | tf_op jit(solution)/shard_map/all_to_all | solution.py:623
  110.9 11.0 %analyse.5 = (bf16[464,384]{1,0:T(8,128)(2,1)}, bf16[464,384]{1,0:T(8,128)(2,1)}, bf16[464,384]{1,0:T(8,128)(2,1)}, bf16[464,384]{1,0:T(8,128)(2,1)}) custom-call(s32[10]{0:T(128)} %constant.134.clone.count_ref, s32[1]{0:T(128)} %bitcast.5.chan_ref, bf16[8,10,48,384]{3,2,1,0:T(8,128)(2,1)} %all-to-all-done.1.fourier_ref, ...), custom_call_target="tpu_custom_call" | custom-call | flops 1000 | bytes 1000 | tf_op jit(solution)/shard_map/analyse/pallas_call | solution.py:236
  126.2 5.8 %synthesise.4.refs_0_ = bf16[8,4,48,384]{3,2,1,0:T(8,128)(2,1)} custom-call(s32[2,4]{1,0:T(2,128)} %constant.135.clone.count_ref, s32[1]{0:T(128)} %bitcast.5.chan_ref, bf16[8,384,768]{2,1,0:T(8,128)(2,1)} %legendre_table.2.table_ref.refs_0_, bf16[2,384]{1,0:T(2,128)(2,1)} %constant.142.lanes_ref, bf16[368,384]{1,0:T(8,128)(2,1)} %get-tuple-element.87.refs_0_, ...), custom_call_target="tpu_custom_call" | custom-call | flops 199999995904 | bytes 1000 | tf_op jit(solution)/shard_map/synthesise/pallas_call | solution.py:542
  134.0 4.3 %all-to-all-start.3 = ((bf16[8,4,48,384]{3,2,1,0:T(8,128)(2,1)}), bf16[8,4,48,384]{3,2,1,0:T(8,128)(2,1)}, u32[]{:S(2)}, u32[]{:S(2)}) async-start(bf16[8,4,48,384]{3,2,1,0:T(8,128)(2,1)} %get-tuple-element.99), calls=%async_computation.3 | async-start | bytes 2359296 | tf_op jit(solution)/shard_map/all_to_all | solution.py:623
  138.3 6.4 %analyse.6 = (bf16[96,384]{1,0:T(8,128)(2,1)}, bf16[96,384]{1,0:T(8,128)(2,1)}, bf16[96,384]{1,0:T(8,128)(2,1)}, bf16[96,384]{1,0:T(8,128)(2,1)}) custom-call(s32[6]{0:T(128)} %constant.136.clone.count_ref, s32[1]{0:T(128)} %bitcast.5.chan_ref, bf16[8,6,48,384]{3,2,1,0:T(8,128)(2,1)} %all-to-all-done.2.fourier_ref, ...), custom_call_target="tpu_custom_call" | custom-call | flops 1000 | bytes 1000 | tf_op jit(solution)/shard_map/analyse/pallas_call | solution.py:236
  151.4 4.3 %collective-permute-done.6.refs_1_ = bf16[464,384]{1,0:T(8,128)(2,1)} collective-permute-done((bf16[464,384]{1,0:T(8,128)(2,1)}, bf16[464,384]{1,0:T(8,128)(2,1)}, u32[]{:S(2)}, u32[]{:S(2)}) %collective-permute-start.6) | collective-permute-done | bytes 356384 | tf_op jit(solution)/shard_map/ppermute | solution.py:599
  155.6 4.8 %mix.5 = (bf16[464,384]{1,0:T(8,128)(2,1)}, bf16[464,384]{1,0:T(8,128)(2,1)}, bf16[464,384]{1,0:T(8,128)(2,1)}, bf16[464,384]{1,0:T(8,128)(2,1)}) custom-call(s32[1]{0:T(128)} %bitcast.5.chan_ref, bf16[464,384]{1,0:T(8,128)(2,1)} %get-tuple-element.96.refs_4_.refs_0_, bf16[464,384]{1,0:T(8,128)(2,1)} %collective-permute-done.6.refs_1_, ...), custom_call_target="tpu_custom_call" | custom-call | flops 199999995904 | bytes 1000 | tf_op jit(solution)/shard_map/mix/pallas_call | solution.py:338
  160.5 6.1 %collective-permute-start.12 = (bf16[464,384]{1,0:T(8,128)(2,1)}, bf16[464,384]{1,0:T(8,128)(2,1)S(1)}, u32[]{:S(2)}, u32[]{:S(2)}) collective-permute-start(bf16[464,384]{1,0:T(8,128)(2,1)} %get-tuple-element.116), channel_id=1, source_target_pairs={{0,3},{1,0},{2,1},{3,2},{4,7},{5,4},{6,5},{7,6},{8,11},{9,8},{10,9... | collective-permute-start | bytes 1069064 | tf_op jit(solution)/shard_map/ppermute | solution.py:599
  166.6 3.9 %all-to-all-start.4 = ((bf16[8,4,48,384]{3,2,1,0:T(8,128)(2,1)}), bf16[8,4,48,384]{3,2,1,0:T(8,128)(2,1)S(1)}, u32[]{:S(2)}, u32[]{:S(2)}) async-start(bf16[8,4,48,384]{3,2,1,0:T(8,128)(2,1)} %synthesise.4.refs_0_), calls=%async_computation.4 | async-start | bytes 2359296 | tf_op jit(solution)/shard_map/all_to_all | solution.py:623
  172.6 6.1 %analyse.7 = (bf16[304,384]{1,0:T(8,128)(2,1)}, bf16[304,384]{1,0:T(8,128)(2,1)}, bf16[304,384]{1,0:T(8,128)(2,1)}, bf16[304,384]{1,0:T(8,128)(2,1)}) custom-call(s32[4]{0:T(128)} %constant.137.clone.count_ref, s32[1]{0:T(128)} %bitcast.5.chan_ref, bf16[8,4,48,384]{3,2,1,0:T(8,128)(2,1)} %all-to-all-done.3.fourier_ref, ...), custom_call_target="tpu_custom_call" | custom-call | flops 1000 | bytes 1000 | tf_op jit(solution)/shard_map/analyse/pallas_call | solution.py:236
  178.7 6.2 %collective-permute-done.11.refs_2_ = bf16[464,384]{1,0:T(8,128)(2,1)S(1)} collective-permute-done((bf16[464,384]{1,0:T(8,128)(2,1)}, bf16[464,384]{1,0:T(8,128)(2,1)S(1)}, u32[]{:S(2)}, u32[]{:S(2)}) %collective-permute-start.11) | collective-permute-done | bytes 356384 | tf_op jit(solution)/shard_map/ppermute | solution.py:599
  188.2 17.4 %collective-permute-done.12.refs_3_ = bf16[464,384]{1,0:T(8,128)(2,1)S(1)} collective-permute-done((bf16[464,384]{1,0:T(8,128)(2,1)}, bf16[464,384]{1,0:T(8,128)(2,1)S(1)}, u32[]{:S(2)}, u32[]{:S(2)}) %collective-permute-start.12) | collective-permute-done | bytes 356384 | tf_op jit(solution)/shard_map/ppermute | solution.py:599
  207.6 10.3 %synthesise.5.refs_5_ = bf16[8,10,48,384]{3,2,1,0:T(8,128)(2,1)} custom-call(s32[2,10]{1,0:T(2,128)} %constant.138.clone.count_ref, s32[1]{0:T(128)} %bitcast.5.chan_ref, bf16[16,256,768]{2,1,0:T(8,128)(2,1)} %legendre_table.3.table_ref.refs_0_, bf16[2,384]{1,0:T(2,128)(2,1)} %constant.142.lanes_ref, bf16[464,384]{1,0:T(8,128)(2,1)} %get-tuple-element.108.refs_0_, ...), custom_call_target="tpu_custom_call" | custom-call | flops 10000000000 | bytes 1000 | tf_op jit(solution)/shard_map/synthesise/pallas_call | solution.py:542
  218.9 3.9 %all-to-all-start.5 = ((bf16[8,10,48,384]{3,2,1,0:T(8,128)(2,1)}), bf16[8,10,48,384]{3,2,1,0:T(8,128)(2,1)S(1)}, u32[]{:S(2)}, u32[]{:S(2)}) async-start(bf16[8,10,48,384]{3,2,1,0:T(8,128)(2,1)} %synthesise.5.refs_5_), calls=%async_computation.5 | async-start | bytes 5898240 | tf_op jit(solution)/shard_map/all_to_all | solution.py:623
  228.8 4.0 %mix.7 = (bf16[304,384]{1,0:T(8,128)(2,1)}, bf16[304,384]{1,0:T(8,128)(2,1)}, bf16[304,384]{1,0:T(8,128)(2,1)}, bf16[304,384]{1,0:T(8,128)(2,1)}) custom-call(s32[1]{0:T(128)} %bitcast.5.chan_ref, bf16[304,384]{1,0:T(8,128)(2,1)} %get-tuple-element.117.refs_4_.refs_0_, bf16[304,384]{1,0:T(8,128)(2,1)} %copy-done.15, bf16[304,384]{1,0:T(8,128)(2,1)} %copy-done.14, ...), custom_call_target="tpu_custom_call" | custom-call | flops 10000000000 | bytes 1000 | tf_op jit(solution)/shard_map/mix/pallas_call | solution.py:338
  235.1 4.2 %collective-permute-start.22 = (bf16[304,384]{1,0:T(8,128)(2,1)}, bf16[304,384]{1,0:T(8,128)(2,1)S(1)}, u32[]{:S(2)}, u32[]{:S(2)}) collective-permute-start(bf16[304,384]{1,0:T(8,128)(2,1)} %get-tuple-element.141), channel_id=1, source_target_pairs={{0,2},{1,3},{2,0},{3,1},{4,6},{5,7},{6,4},{7,5},{8,10},{9,11},{10,... | collective-permute-start | bytes 700424 | tf_op jit(solution)/shard_map/ppermute | solution.py:599
  239.9 6.1 %synthesise.6.refs_4_ = bf16[8,6,48,384]{3,2,1,0:T(8,128)(2,1)} custom-call(s32[2,6]{1,0:T(2,128)} %constant.139.clone.count_ref, s32[1]{0:T(128)} %bitcast.5.chan_ref, bf16[16,256,768]{2,1,0:T(8,128)(2,1)} %legendre_table.3.table_ref.refs_0_, bf16[2,384]{1,0:T(2,128)(2,1)} %constant.142.lanes_ref, bf16[96,384]{1,0:T(8,128)(2,1)} %get-tuple-element.123.refs_5_.refs_0_, ...), custom_call_target="tpu_custom_call" | custom-call | flops 10000000000 | bytes 1000 | tf_op jit(solution)/shard_map/synthesise/pallas_call | solution.py:542
  246.0 12.5 %all-to-all-done.5.refs_1_ = bf16[8,10,48,384]{3,2,1,0:T(8,128)(2,1)S(1)} async-done(((bf16[8,10,48,384]{3,2,1,0:T(8,128)(2,1)}), bf16[8,10,48,384]{3,2,1,0:T(8,128)(2,1)S(1)}, u32[]{:S(2)}, u32[]{:S(2)}) %all-to-all-start.5) | async-done | bytes 2949152 | tf_op jit(solution)/shard_map/all_to_all | solution.py:623
  258.5 4.3 %all-to-all-start.6 = ((bf16[8,6,48,384]{3,2,1,0:T(8,128)(2,1)}), bf16[8,6,48,384]{3,2,1,0:T(8,128)(2,1)}, u32[]{:S(2)}, u32[]{:S(2)}) async-start(bf16[8,6,48,384]{3,2,1,0:T(8,128)(2,1)} %synthesise.6.refs_4_), calls=%async_computation.6 | async-start | bytes 3538944 | tf_op jit(solution)/shard_map/all_to_all | solution.py:623
  263.7 5.7 %synthesise.7 = bf16[8,4,48,384]{3,2,1,0:T(8,128)(2,1)} custom-call(s32[2,4]{1,0:T(2,128)} %constant.140.clone.count_ref, s32[1]{0:T(128)} %bitcast.5.chan_ref, bf16[8,384,768]{2,1,0:T(8,128)(2,1)} %legendre_table.2.table_ref.refs_0_, bf16[2,384]{1,0:T(2,128)(2,1)} %constant.142.lanes_ref, bf16[304,384]{1,0:T(8,128)(2,1)} %get-tuple-element.136.refs_4_.refs_0_, ...), custom_call_target="tpu_custom_call" | custom-call | flops 199999995904 | bytes 1000 | tf_op jit(solution)/shard_map/synthesise/pallas_call | solution.py:542
  269.3 16.7 %all-to-all-done.6.refs_2_ = bf16[8,6,48,384]{3,2,1,0:T(8,128)(2,1)} async-done(((bf16[8,6,48,384]{3,2,1,0:T(8,128)(2,1)}), bf16[8,6,48,384]{3,2,1,0:T(8,128)(2,1)}, u32[]{:S(2)}, u32[]{:S(2)}) %all-to-all-start.6) | async-done | bytes 1769504 | tf_op jit(solution)/shard_map/all_to_all | solution.py:623
  294.2 10.5 %early_rows.1.early_ref = bf16[48,96,640]{2,1,0:T(8,128)(2,1)} custom-call(bf16[256,256]{1,0:T(8,128)(2,1)} %constant.141.swap_ref, bf16[8,4,48,384]{3,2,1,0:T(8,128)(2,1)} %copy-done.2, bf16[8,10,48,384]{3,2,1,0:T(8,128)(2,1)} %copy-done.1, bf16[8,6,48,384]{3,2,1,0:T(8,128)(2,1)} %all-to-all-done.6.refs_2_), custom_call_target="tpu_custom_call" | custom-call | flops 1000 | bytes 1000 | tf_op jit(solution)/shard_map/early_rows/pallas_call | solution.py:437
  307.3 21.6 %inverse_rows.1 = bf16[48,96,1440]{2,1,0:T(8,128)(2,1)} custom-call(bf16[768,1440]{1,0:T(8,128)(2,1)} %pad_maximum_fusion.1.synth_ref, bf16[256,256]{1,0:T(8,128)(2,1)} %constant.141.swap_ref, bf16[48,96,640]{2,1,0:T(8,128)(2,1)} %early_rows.1.early_ref, bf16[8,4,48,384]{3,2,1,0:T(8,128)(2,1)} %copy-done.4), custom_call_target="tpu_custom_call" | custom-call | flops 1000 | bytes 1000 | tf_op jit(solution)/shard_map/inverse_rows/pallas_call | solution.py:474
  (135 shorter events, 68.0 us)
Async XLA Ops:
  24.0 24.7 %all-to-all-start = ((bf16[8,4,48,384]{3,2,1,0:T(8,128)(2,1)}), bf16[8,4,48,384]{3,2,1,0:T(8,128)(2,1)S(1)}, u32[]{:S(2)}, u32[]{:S(2)}) async-start(bf16[8,4,48,384]{3,2,1,0:T(8,128)(2,1)} %get-tuple-element.79.refs_0_), calls=%async_computation | async-start | bytes 2359296 | tf_op jit(solution)/shard_map/all_to_all | solution.py:623
  56.2 28.6 %collective-permute-start = (bf16[368,384]{1,0:T(8,128)(2,1)}, bf16[368,384]{1,0:T(8,128)(2,1)}, u32[]{:S(2)}, u32[]{:S(2)}) collective-permute-start(bf16[368,384]{1,0:T(8,128)(2,1)} %get-tuple-element.83), channel_id=1, source_target_pairs={{0,1},{1,2},{2,3},{3,0},{4,5},{5,6},{6,7},{7,4},{8,9},{9,10},{10,1... | collective-permute-start | bytes 847880 | tf_op jit(solution)/shard_map/ppermute | solution.py:599
  57.7 27.0 %collective-permute-start.1 = (bf16[368,384]{1,0:T(8,128)(2,1)}, bf16[368,384]{1,0:T(8,128)(2,1)}, u32[]{:S(2)}, u32[]{:S(2)}) collective-permute-start(bf16[368,384]{1,0:T(8,128)(2,1)} %get-tuple-element.84), channel_id=1, source_target_pairs={{0,2},{1,3},{2,0},{3,1},{4,6},{5,7},{6,4},{7,5},{8,10},{9,11},{10,... | collective-permute-start | bytes 847880 | tf_op jit(solution)/shard_map/ppermute | solution.py:599
  58.7 26.1 %collective-permute-start.2 = (bf16[368,384]{1,0:T(8,128)(2,1)}, bf16[368,384]{1,0:T(8,128)(2,1)}, u32[]{:S(2)}, u32[]{:S(2)}) collective-permute-start(bf16[368,384]{1,0:T(8,128)(2,1)} %get-tuple-element.85), channel_id=1, source_target_pairs={{0,3},{1,0},{2,1},{3,2},{4,7},{5,4},{6,5},{7,6},{8,11},{9,8},{10,9... | collective-permute-start | bytes 847880 | tf_op jit(solution)/shard_map/ppermute | solution.py:599
  64.2 42.4 %all-to-all-start.1 = ((bf16[8,10,48,384]{3,2,1,0:T(8,128)(2,1)}), bf16[8,10,48,384]{3,2,1,0:T(8,128)(2,1)}, u32[]{:S(2)}, u32[]{:S(2)}) async-start(bf16[8,10,48,384]{3,2,1,0:T(8,128)(2,1)} %get-tuple-element.95), calls=%async_computation.1 | async-start | bytes 5898240 | tf_op jit(solution)/shard_map/all_to_all | solution.py:623
  89.0 37.1 %collective-permute-start.5 = (bf16[368,384]{1,0:T(8,128)(2,1)}, bf16[368,384]{1,0:T(8,128)(2,1)}, u32[]{:S(2)}, u32[]{:S(2)}) collective-permute-start(bf16[368,384]{1,0:T(8,128)(2,1)} %get-tuple-element.93), channel_id=1, source_target_pairs={{0,3},{1,0},{2,1},{3,2},{4,7},{5,4},{6,5},{7,6},{8,11},{9,8},{10,9... | collective-permute-start | bytes 847880 | tf_op jit(solution)/shard_map/ppermute | solution.py:599
  90.7 31.2 %collective-permute-start.4 = (bf16[368,384]{1,0:T(8,128)(2,1)}, bf16[368,384]{1,0:T(8,128)(2,1)}, u32[]{:S(2)}, u32[]{:S(2)}) collective-permute-start(bf16[368,384]{1,0:T(8,128)(2,1)} %get-tuple-element.91), channel_id=1, source_target_pairs={{0,2},{1,3},{2,0},{3,1},{4,6},{5,7},{6,4},{7,5},{8,10},{9,11},{10,... | collective-permute-start | bytes 847880 | tf_op jit(solution)/shard_map/ppermute | solution.py:599
  90.7 35.4 %collective-permute-start.3 = (bf16[368,384]{1,0:T(8,128)(2,1)}, bf16[368,384]{1,0:T(8,128)(2,1)}, u32[]{:S(2)}, u32[]{:S(2)}) collective-permute-start(bf16[368,384]{1,0:T(8,128)(2,1)} %get-tuple-element.89), channel_id=1, source_target_pairs={{0,1},{1,2},{2,3},{3,0},{4,5},{5,6},{6,7},{7,4},{8,9},{9,10},{10,1... | collective-permute-start | bytes 847880 | tf_op jit(solution)/shard_map/ppermute | solution.py:599
  106.6 27.5 %all-to-all-start.2 = ((bf16[8,6,48,384]{3,2,1,0:T(8,128)(2,1)}), bf16[8,6,48,384]{3,2,1,0:T(8,128)(2,1)}, u32[]{:S(2)}, u32[]{:S(2)}) async-start(bf16[8,6,48,384]{3,2,1,0:T(8,128)(2,1)} %get-tuple-element.98.refs_5_), calls=%async_computation.2 | async-start | bytes 3538944 | tf_op jit(solution)/shard_map/all_to_all | solution.py:623
  121.9 29.5 %collective-permute-start.8 = (bf16[464,384]{1,0:T(8,128)(2,1)}, bf16[464,384]{1,0:T(8,128)(2,1)}, u32[]{:S(2)}, u32[]{:S(2)}) collective-permute-start(bf16[464,384]{1,0:T(8,128)(2,1)} %get-tuple-element.106), channel_id=1, source_target_pairs={{0,3},{1,0},{2,1},{3,2},{4,7},{5,4},{6,5},{7,6},{8,11},{9,8},{10,9... | collective-permute-start | bytes 1069064 | tf_op jit(solution)/shard_map/ppermute | solution.py:599
  121.9 26.1 %collective-permute-start.7 = (bf16[464,384]{1,0:T(8,128)(2,1)}, bf16[464,384]{1,0:T(8,128)(2,1)}, u32[]{:S(2)}, u32[]{:S(2)}) collective-permute-start(bf16[464,384]{1,0:T(8,128)(2,1)} %get-tuple-element.104), channel_id=1, source_target_pairs={{0,2},{1,3},{2,0},{3,1},{4,6},{5,7},{6,4},{7,5},{8,10},{9,11},{10,... | collective-permute-start | bytes 1069064 | tf_op jit(solution)/shard_map/ppermute | solution.py:599
  124.0 31.6 %collective-permute-start.6 = (bf16[464,384]{1,0:T(8,128)(2,1)}, bf16[464,384]{1,0:T(8,128)(2,1)}, u32[]{:S(2)}, u32[]{:S(2)}) collective-permute-start(bf16[464,384]{1,0:T(8,128)(2,1)} %get-tuple-element.102), channel_id=1, source_target_pairs={{0,1},{1,2},{2,3},{3,0},{4,5},{5,6},{6,7},{7,4},{8,9},{9,10},{10,1... | collective-permute-start | bytes 1069064 | tf_op jit(solution)/shard_map/ppermute | solution.py:599
  134.0 32.5 %all-to-all-start.3 = ((bf16[8,4,48,384]{3,2,1,0:T(8,128)(2,1)}), bf16[8,4,48,384]{3,2,1,0:T(8,128)(2,1)}, u32[]{:S(2)}, u32[]{:S(2)}) async-start(bf16[8,4,48,384]{3,2,1,0:T(8,128)(2,1)} %get-tuple-element.99), calls=%async_computation.3 | async-start | bytes 2359296 | tf_op jit(solution)/shard_map/all_to_all | solution.py:623
  148.0 12.4 %collective-permute-start.9 = (bf16[96,384]{1,0:T(8,128)(2,1)}, bf16[96,384]{1,0:T(8,128)(2,1)}, u32[]{:S(2)}, u32[]{:S(2)}) collective-permute-start(bf16[96,384]{1,0:T(8,128)(2,1)} %get-tuple-element.111), channel_id=1, source_target_pairs={{0,2},{1,3},{2,0},{3,1},{4,6},{5,7},{6,4},{7,5},{8,10},{9,11},{10,... | collective-permute-start | bytes 221192 | tf_op jit(solution)/shard_map/ppermute | solution.py:599
  160.4 24.5 %collective-permute-start.11 = (bf16[464,384]{1,0:T(8,128)(2,1)}, bf16[464,384]{1,0:T(8,128)(2,1)S(1)}, u32[]{:S(2)}, u32[]{:S(2)}) collective-permute-start(bf16[464,384]{1,0:T(8,128)(2,1)} %get-tuple-element.114), channel_id=1, source_target_pairs={{0,2},{1,3},{2,0},{3,1},{4,6},{5,7},{6,4},{7,5},{8,10},{9,11},{10,... | collective-permute-start | bytes 1069064 | tf_op jit(solution)/shard_map/ppermute | solution.py:599
  160.5 45.0 %collective-permute-start.12 = (bf16[464,384]{1,0:T(8,128)(2,1)}, bf16[464,384]{1,0:T(8,128)(2,1)S(1)}, u32[]{:S(2)}, u32[]{:S(2)}) collective-permute-start(bf16[464,384]{1,0:T(8,128)(2,1)} %get-tuple-element.116), channel_id=1, source_target_pairs={{0,3},{1,0},{2,1},{3,2},{4,7},{5,4},{6,5},{7,6},{8,11},{9,8},{10,9... | collective-permute-start | bytes 1069064 | tf_op jit(solution)/shard_map/ppermute | solution.py:599
  166.6 39.0 %collective-permute-start.10 = (bf16[464,384]{1,0:T(8,128)(2,1)}, bf16[464,384]{1,0:T(8,128)(2,1)S(1)}, u32[]{:S(2)}, u32[]{:S(2)}) collective-permute-start(bf16[464,384]{1,0:T(8,128)(2,1)} %get-tuple-element.112), channel_id=1, source_target_pairs={{0,1},{1,2},{2,3},{3,0},{4,5},{5,6},{6,7},{7,4},{8,9},{9,10},{10,1... | collective-permute-start | bytes 1069064 | tf_op jit(solution)/shard_map/ppermute | solution.py:599
  166.6 51.3 %all-to-all-start.4 = ((bf16[8,4,48,384]{3,2,1,0:T(8,128)(2,1)}), bf16[8,4,48,384]{3,2,1,0:T(8,128)(2,1)S(1)}, u32[]{:S(2)}, u32[]{:S(2)}) async-start(bf16[8,4,48,384]{3,2,1,0:T(8,128)(2,1)} %synthesise.4.refs_0_), calls=%async_computation.4 | async-start | bytes 2359296 | tf_op jit(solution)/shard_map/all_to_all | solution.py:623
  170.5 52.3 %collective-permute-start.13 = (bf16[96,384]{1,0:T(8,128)(2,1)}, bf16[96,384]{1,0:T(8,128)(2,1)}, u32[]{:S(2)}, u32[]{:S(2)}) collective-permute-start(bf16[96,384]{1,0:T(8,128)(2,1)} %get-tuple-element.120), channel_id=1, source_target_pairs={{0,1},{1,2},{2,3},{3,0},{4,5},{5,6},{6,7},{7,4},{8,9},{9,10},{10,1... | collective-permute-start | bytes 221192 | tf_op jit(solution)/shard_map/ppermute | solution.py:599
  171.7 51.1 %collective-permute-start.14 = (bf16[96,384]{1,0:T(8,128)(2,1)S(1)}, bf16[96,384]{1,0:T(8,128)(2,1)}, u32[]{:S(2)}, u32[]{:S(2)}) collective-permute-start(bf16[96,384]{1,0:T(8,128)(2,1)S(1)} %copy-done.18), channel_id=1, source_target_pairs={{0,3},{1,0},{2,1},{3,2},{4,7},{5,4},{6,5},{7,6},{8,11},{9,8},{10,9... | collective-permute-start | bytes 221192 | tf_op jit(solution)/shard_map/ppermute | solution.py:599
  184.9 40.9 %collective-permute-start.15 = (bf16[304,384]{1,0:T(8,128)(2,1)}, bf16[304,384]{1,0:T(8,128)(2,1)S(1)}, u32[]{:S(2)}, u32[]{:S(2)}) collective-permute-start(bf16[304,384]{1,0:T(8,128)(2,1)} %get-tuple-element.126), channel_id=1, source_target_pairs={{0,2},{1,3},{2,0},{3,1},{4,6},{5,7},{6,4},{7,5},{8,10},{9,11},{10,... | collective-permute-start | bytes 700424 | tf_op jit(solution)/shard_map/ppermute | solution.py:599
  205.5 22.5 %collective-permute-start.19 = (bf16[304,384]{1,0:T(8,128)(2,1)}, bf16[304,384]{1,0:T(8,128)(2,1)S(1)}, u32[]{:S(2)}, u32[]{:S(2)}) collective-permute-start(bf16[304,384]{1,0:T(8,128)(2,1)} %get-tuple-element.133), channel_id=1, source_target_pairs={{0,1},{1,2},{2,3},{3,0},{4,5},{5,6},{6,7},{7,4},{8,9},{9,10},{10,1... | collective-permute-start | bytes 700424 | tf_op jit(solution)/shard_map/ppermute | solution.py:599
  205.6 22.5 %collective-permute-start.20 = (bf16[304,384]{1,0:T(8,128)(2,1)}, bf16[304,384]{1,0:T(8,128)(2,1)}, u32[]{:S(2)}, u32[]{:S(2)}) collective-permute-start(bf16[304,384]{1,0:T(8,128)(2,1)} %get-tuple-element.135), channel_id=1, source_target_pairs={{0,3},{1,0},{2,1},{3,2},{4,7},{5,4},{6,5},{7,6},{8,11},{9,8},{10,9... | collective-permute-start | bytes 700424 | tf_op jit(solution)/shard_map/ppermute | solution.py:599
  218.9 39.6 %all-to-all-start.5 = ((bf16[8,10,48,384]{3,2,1,0:T(8,128)(2,1)}), bf16[8,10,48,384]{3,2,1,0:T(8,128)(2,1)S(1)}, u32[]{:S(2)}, u32[]{:S(2)}) async-start(bf16[8,10,48,384]{3,2,1,0:T(8,128)(2,1)} %synthesise.5.refs_5_), calls=%async_computation.5 | async-start | bytes 5898240 | tf_op jit(solution)/shard_map/all_to_all | solution.py:623
  225.8 13.5 %collective-permute-start.18 = (bf16[96,384]{1,0:T(8,128)(2,1)}, bf16[96,384]{1,0:T(8,128)(2,1)S(1)}, u32[]{:S(2)}, u32[]{:S(2)}) collective-permute-start(bf16[96,384]{1,0:T(8,128)(2,1)} %get-tuple-element.131), channel_id=1, source_target_pairs={{0,3},{1,0},{2,1},{3,2},{4,7},{5,4},{6,5},{7,6},{8,11},{9,8},{10,9... | collective-permute-start | bytes 221192 | tf_op jit(solution)/shard_map/ppermute | solution.py:599
  226.5 6.3 %collective-permute-start.17 = (bf16[96,384]{1,0:T(8,128)(2,1)}, bf16[96,384]{1,0:T(8,128)(2,1)S(1)}, u32[]{:S(2)}, u32[]{:S(2)}) collective-permute-start(bf16[96,384]{1,0:T(8,128)(2,1)} %get-tuple-element.129), channel_id=1, source_target_pairs={{0,2},{1,3},{2,0},{3,1},{4,6},{5,7},{6,4},{7,5},{8,10},{9,11},{10,... | collective-permute-start | bytes 221192 | tf_op jit(solution)/shard_map/ppermute | solution.py:599
  227.3 11.9 %collective-permute-start.16 = (bf16[96,384]{1,0:T(8,128)(2,1)}, bf16[96,384]{1,0:T(8,128)(2,1)S(1)}, u32[]{:S(2)}, u32[]{:S(2)}) collective-permute-start(bf16[96,384]{1,0:T(8,128)(2,1)} %get-tuple-element.127), channel_id=1, source_target_pairs={{0,1},{1,2},{2,3},{3,0},{4,5},{5,6},{6,7},{7,4},{8,9},{9,10},{10,1... | collective-permute-start | bytes 221192 | tf_op jit(solution)/shard_map/ppermute | solution.py:599
  232.8 30.0 %collective-permute-start.21 = (bf16[304,384]{1,0:T(8,128)(2,1)}, bf16[304,384]{1,0:T(8,128)(2,1)S(1)}, u32[]{:S(2)}, u32[]{:S(2)}) collective-permute-start(bf16[304,384]{1,0:T(8,128)(2,1)} %get-tuple-element.139), channel_id=1, source_target_pairs={{0,1},{1,2},{2,3},{3,0},{4,5},{5,6},{6,7},{7,4},{8,9},{9,10},{10,1... | collective-permute-start | bytes 700424 | tf_op jit(solution)/shard_map/ppermute | solution.py:599
  235.1 27.8 %collective-permute-start.22 = (bf16[304,384]{1,0:T(8,128)(2,1)}, bf16[304,384]{1,0:T(8,128)(2,1)S(1)}, u32[]{:S(2)}, u32[]{:S(2)}) collective-permute-start(bf16[304,384]{1,0:T(8,128)(2,1)} %get-tuple-element.141), channel_id=1, source_target_pairs={{0,2},{1,3},{2,0},{3,1},{4,6},{5,7},{6,4},{7,5},{8,10},{9,11},{10,... | collective-permute-start | bytes 700424 | tf_op jit(solution)/shard_map/ppermute | solution.py:599
  239.2 23.7 %collective-permute-start.23 = (bf16[304,384]{1,0:T(8,128)(2,1)}, bf16[304,384]{1,0:T(8,128)(2,1)}, u32[]{:S(2)}, u32[]{:S(2)}) collective-permute-start(bf16[304,384]{1,0:T(8,128)(2,1)} %get-tuple-element.143), channel_id=1, source_target_pairs={{0,3},{1,0},{2,1},{3,2},{4,7},{5,4},{6,5},{7,6},{8,11},{9,8},{10,9... | collective-permute-start | bytes 700424 | tf_op jit(solution)/shard_map/ppermute | solution.py:599
  258.5 27.5 %all-to-all-start.6 = ((bf16[8,6,48,384]{3,2,1,0:T(8,128)(2,1)}), bf16[8,6,48,384]{3,2,1,0:T(8,128)(2,1)}, u32[]{:S(2)}, u32[]{:S(2)}) async-start(bf16[8,6,48,384]{3,2,1,0:T(8,128)(2,1)} %synthesise.6.refs_4_), calls=%async_computation.6 | async-start | bytes 3538944 | tf_op jit(solution)/shard_map/all_to_all | solution.py:623
  286.0 20.3 %all-to-all-start.7 = ((bf16[8,4,48,384]{3,2,1,0:T(8,128)(2,1)}), bf16[8,4,48,384]{3,2,1,0:T(8,128)(2,1)S(1)}, u32[]{:S(2)}, u32[]{:S(2)}) async-start(bf16[8,4,48,384]{3,2,1,0:T(8,128)(2,1)} %synthesise.7), calls=%async_computation.7 | async-start | bytes 2359296 | tf_op jit(solution)/shard_map/all_to_all | solution.py:623
  (22 other events, 126.3 us)

commit v4 on v3

--- a/solution.py
+++ b/solution.py
@@ -554,7 +554,7 @@
     first = list(range(few))
     last = list(range(few, 2 * few))
     rest = list(range(2 * few, group_count))
-    half = len(rest) * 5 // 8 // even * even
+    half = len(rest) // 2 // even * even
     return [first, rest[:half], rest[half:], last]
 
 

time: 333 us -> 331 us (level)
  waiting for transfers between devices: 63.9 us -> 59.2 us
    all_to_all x8, waiting for transfers between devices: 32.8 us -> 29 us  [across_lat(): lax.all_to_all(x, 'lat', split_axis=0, concat_axis=0, tiled=True)]
    unnamed x45 -> x55, local copies, waits for them, and re-layouts: 8.47 us -> 11.3 us
  transfers between devices with their start and end apart: 32 -> 32, of which waited for: 8 -> 9; matrix products, arithmetic and copies ran while one was open for 3% -> 3% of each run, Pallas kernels for 38% -> 38%
where the time goes in v4:
time: 331 us; the launch traced here: 326 us
  Pallas kernels  170 us (51%)
  starting transfers between devices  71 us (21%)
  waiting for transfers between devices  59.2 us (18%)
  local copies, waits for them, and re-layouts  14.7 us (4%)
  other arithmetic  11.2 us (3%)
    ppermute x24, starting transfers between devices, moved(): out.append(lax.ppermute(part, 'chan', pairs))  38.2 us
    all_to_all x8, starting transfers between devices, across_lat(): lax.all_to_all(x, 'lat', split_axis=0, concat_axis=0, tiled=True)  32.7 us
    pallas_call x2, Pallas kernels, forward_rows(): pl.pallas_call(functools.partial(forward_body, first_row, counts), grid_s...  32.6 us
    ppermute x24, waiting for transfers between devices, moved(): out.append(lax.ppermute(part, 'chan', pairs))  30.2 us
    pallas_call x4, Pallas kernels, analyse(): pl.pallas_call(functools.partial(analyse_body, plan), grid_spec=spec, out...  29.9 us
    all_to_all x8, waiting for transfers between devices, across_lat(): lax.all_to_all(x, 'lat', split_axis=0, concat_axis=0, tiled=True)  29 us
    pallas_call x4, Pallas kernels, synthesise(): pl.pallas_call(functools.partial(synthesise_body, plan), grid_spec=spec,...  27.6 us
    pallas_call x2, Pallas kernels, legendre_table(): pl.pallas_call(functools.partial(table_body, group_rows, all_groups[0], b...  25 us
  transfers between devices with their start and end apart: 32, of which 9 were waited for; matrix products, arithmetic and copies ran while one was open for 3% of the time, Pallas kernels for 38%

profile of v4, /device:TPU:8, one launch (start us, length us, event | category | flops | bytes accessed | tf_op | source)
XLA Modules:
  0.0 326.2 jit_solution(16549874680798873450)
XLA Ops:
  7.4 16.3 %forward_rows.2 = (bf16[8,4,48,384]{3,2,1,0:T(8,128)(2,1)}, bf16[8,8,48,384]{3,2,1,0:T(8,128)(2,1)}) custom-call(f32[48]{0:T(128)} %sine_multiply_fusion.weight_ref, bf16[48,96,1440]{2,1,0:T(8,128)(2,1)} %signal_ref.3, bf16[4,192,1440]{2,1,0:T(8,128)(2,1)} %convert_element_type.110.trig_ref, bf16[256,256]{1,0:T(8,128)(2,1)} %constant.141.swap_ref), custom_call_target="tpu_custom_call" | custom-call | flops 1000 | bytes 1000 | tf_op jit(solution)/shard_map/forward_rows/pallas_call | solution.py:397
  23.7 3.9 %all-to-all-start = ((bf16[8,4,48,384]{3,2,1,0:T(8,128)(2,1)}), bf16[8,4,48,384]{3,2,1,0:T(8,128)(2,1)S(1)}, u32[]{:S(2)}, u32[]{:S(2)}) async-start(bf16[8,4,48,384]{3,2,1,0:T(8,128)(2,1)} %get-tuple-element.79.refs_0_), calls=%async_computation | async-start | bytes 2359296 | tf_op jit(solution)/shard_map/all_to_all | solution.py:623
  34.3 12.7 %legendre_table.2.table_ref.refs_0_ = bf16[8,384,768]{2,1,0:T(8,128)(2,1)} custom-call(f32[384]{0:T(512)} %constant.131.clone.inverse_ref, f32[1,16,384]{2,1,0:T(8,128)} %maximum_bitcast_fusion.seeds_ref, f32[1,16,128]{2,1,0:T(8,128)} %reshape.427.order_ref, f32[1,384]{1,0:T(1,128)} %multiply_cosine_fusion.cosine_ref, bf16[256,256]{1,0:T(8,128)(2,1)} %constant.141.swap_ref, ...), custom_call_target="tpu_custom_call" | custom-call | flops 1000 | bytes 1000 | tf_op jit(solution)/shard_map/legendre_table/pallas_call | solution.py:148
  49.5 6.5 %analyse.4 = (bf16[368,384]{1,0:T(8,128)(2,1)}, bf16[368,384]{1,0:T(8,128)(2,1)}, bf16[368,384]{1,0:T(8,128)(2,1)}, bf16[368,384]{1,0:T(8,128)(2,1)}) custom-call(s32[4]{0:T(128)} %constant.132.clone.count_ref, s32[1]{0:T(128)} %bitcast.5.chan_ref, bf16[8,4,48,384]{3,2,1,0:T(8,128)(2,1)} %copy-done.3, bf16[8,384,768]{2,1,0:T(8,128)(2,1)} %legendre_table.2.table_ref.refs_0_, ...), custom_call_target="tpu_custom_call" | custom-call | flops 1000 | bytes 1000 | tf_op jit(solution)/shard_map/analyse/pallas_call | solution.py:236
  60.3 3.7 %mix_kernel.1.refs_0_.refs_4_ = bf16[4,4,192,192]{3,2,1,0:T(8,128)(2,1)} custom-call(bf16[2,384,384]{2,1,0:T(8,128)(2,1)} %mix_ref.1, bf16[368,384]{1,0:T(8,128)(2,1)} %get-tuple-element.82.refs_0_), custom_call_target="tpu_custom_call" | custom-call | flops 199999995904 | bytes 1000 | tf_op jit(solution)/shard_map/mix_kernel/pallas_call | solution.py:293
  64.0 4.6 %all-to-all-start.1 = ((bf16[8,8,48,384]{3,2,1,0:T(8,128)(2,1)}), bf16[8,8,48,384]{3,2,1,0:T(8,128)(2,1)}, u32[]{:S(2)}, u32[]{:S(2)}) async-start(bf16[8,8,48,384]{3,2,1,0:T(8,128)(2,1)} %get-tuple-element.95), calls=%async_computation.1 | async-start | bytes 4718592 | tf_op jit(solution)/shard_map/all_to_all | solution.py:623
  68.5 16.3 %forward_rows.3 = (bf16[8,8,48,384]{3,2,1,0:T(8,128)(2,1)}, bf16[8,4,48,384]{3,2,1,0:T(8,128)(2,1)}) custom-call(f32[48]{0:T(128)} %sine_multiply_fusion.weight_ref, bf16[48,96,1440]{2,1,0:T(8,128)(2,1)} %signal_ref.3, bf16[4,192,1440]{2,1,0:T(8,128)(2,1)} %convert_element_type.110.trig_ref, bf16[256,256]{1,0:T(8,128)(2,1)} %constant.141.swap_ref, ...), custom_call_target="tpu_custom_call" | custom-call | flops 1000 | bytes 1000 | tf_op jit(solution)/shard_map/forward_rows/pallas_call | solution.py:397
  84.9 4.2 %mix.4 = (bf16[368,384]{1,0:T(8,128)(2,1)}, bf16[368,384]{1,0:T(8,128)(2,1)}, bf16[368,384]{1,0:T(8,128)(2,1)}, bf16[368,384]{1,0:T(8,128)(2,1)}) custom-call(s32[1]{0:T(128)} %bitcast.5.chan_ref, bf16[368,384]{1,0:T(8,128)(2,1)} %get-tuple-element.82.refs_0_, bf16[368,384]{1,0:T(8,128)(2,1)} %collective-permute-done.refs_1_, ...), custom_call_target="tpu_custom_call" | custom-call | flops 1000 | bytes 1000 | tf_op jit(solution)/shard_map/mix/pallas_call | solution.py:338
  93.9 12.4 %legendre_table.3.table_ref.refs_0_ = bf16[16,256,768]{2,1,0:T(8,128)(2,1)} custom-call(f32[384]{0:T(512)} %constant.131.clone.inverse_ref, f32[2,16,384]{2,1,0:T(8,128)} %bitcast.21, f32[2,16,128]{2,1,0:T(8,128)} %broadcast_in_dim.10.order_ref, f32[1,384]{1,0:T(1,128)} %multiply_cosine_fusion.cosine_ref, bf16[256,256]{1,0:T(8,128)(2,1)} %constant.141.swap_ref, ...), custom_call_target="tpu_custom_call" | custom-call | flops 199999995904 | bytes 1000 | tf_op jit(solution)/shard_map/legendre_table/pallas_call | solution.py:148
  106.3 4.4 %all-to-all-start.2 = ((bf16[8,8,48,384]{3,2,1,0:T(8,128)(2,1)}), bf16[8,8,48,384]{3,2,1,0:T(8,128)(2,1)}, u32[]{:S(2)}, u32[]{:S(2)}) async-start(bf16[8,8,48,384]{3,2,1,0:T(8,128)(2,1)} %get-tuple-element.98.refs_5_), calls=%async_computation.2 | async-start | bytes 4718592 | tf_op jit(solution)/shard_map/all_to_all | solution.py:623
  110.7 9.2 %analyse.5 = (bf16[400,384]{1,0:T(8,128)(2,1)}, bf16[400,384]{1,0:T(8,128)(2,1)}, bf16[400,384]{1,0:T(8,128)(2,1)}, bf16[400,384]{1,0:T(8,128)(2,1)}) custom-call(s32[8]{0:T(128)} %constant.134.clone.count_ref, s32[1]{0:T(128)} %bitcast.5.chan_ref, bf16[8,8,48,384]{3,2,1,0:T(8,128)(2,1)} %all-to-all-done.1.fourier_ref, ...), custom_call_target="tpu_custom_call" | custom-call | flops 1000 | bytes 1000 | tf_op jit(solution)/shard_map/analyse/pallas_call | solution.py:236
  124.6 5.8 %synthesise.4.refs_0_ = bf16[8,4,48,384]{3,2,1,0:T(8,128)(2,1)} custom-call(s32[2,4]{1,0:T(2,128)} %constant.135.clone.count_ref, s32[1]{0:T(128)} %bitcast.5.chan_ref, bf16[8,384,768]{2,1,0:T(8,128)(2,1)} %legendre_table.2.table_ref.refs_0_, bf16[2,384]{1,0:T(2,128)(2,1)} %constant.142.lanes_ref, bf16[368,384]{1,0:T(8,128)(2,1)} %get-tuple-element.87.refs_0_, ...), custom_call_target="tpu_custom_call" | custom-call | flops 199999995904 | bytes 1000 | tf_op jit(solution)/shard_map/synthesise/pallas_call | solution.py:542
  130.4 9.8 %all-to-all-done.2.fourier_ref = bf16[8,8,48,384]{3,2,1,0:T(8,128)(2,1)} async-done(((bf16[8,8,48,384]{3,2,1,0:T(8,128)(2,1)}), bf16[8,8,48,384]{3,2,1,0:T(8,128)(2,1)}, u32[]{:S(2)}, u32[]{:S(2)}) %all-to-all-start.2) | async-done | bytes 2359328 | tf_op jit(solution)/shard_map/all_to_all | solution.py:623
  140.2 4.3 %all-to-all-start.3 = ((bf16[8,4,48,384]{3,2,1,0:T(8,128)(2,1)}), bf16[8,4,48,384]{3,2,1,0:T(8,128)(2,1)}, u32[]{:S(2)}, u32[]{:S(2)}) async-start(bf16[8,4,48,384]{3,2,1,0:T(8,128)(2,1)} %get-tuple-element.99), calls=%async_computation.3 | async-start | bytes 2359296 | tf_op jit(solution)/shard_map/all_to_all | solution.py:623
  144.4 8.1 %analyse.6 = (bf16[144,384]{1,0:T(8,128)(2,1)}, bf16[144,384]{1,0:T(8,128)(2,1)}, bf16[144,384]{1,0:T(8,128)(2,1)}, bf16[144,384]{1,0:T(8,128)(2,1)}) custom-call(s32[8]{0:T(128)} %constant.136.clone.count_ref, s32[1]{0:T(128)} %bitcast.5.chan_ref, bf16[8,8,48,384]{3,2,1,0:T(8,128)(2,1)} %all-to-all-done.2.fourier_ref, ...), custom_call_target="tpu_custom_call" | custom-call | flops 1000 | bytes 1000 | tf_op jit(solution)/shard_map/analyse/pallas_call | solution.py:236
  154.3 4.4 %mix.5 = (bf16[400,384]{1,0:T(8,128)(2,1)}, bf16[400,384]{1,0:T(8,128)(2,1)}, bf16[400,384]{1,0:T(8,128)(2,1)}, bf16[400,384]{1,0:T(8,128)(2,1)}) custom-call(s32[1]{0:T(128)} %bitcast.5.chan_ref, bf16[400,384]{1,0:T(8,128)(2,1)} %get-tuple-element.96.refs_4_.refs_0_, bf16[400,384]{1,0:T(8,128)(2,1)} %collective-permute-done.6.refs_1_, ...), custom_call_target="tpu_custom_call" | custom-call | flops 199999995904 | bytes 1000 | tf_op jit(solution)/shard_map/mix/pallas_call | solution.py:338
  165.2 3.9 %all-to-all-start.4 = ((bf16[8,4,48,384]{3,2,1,0:T(8,128)(2,1)}), bf16[8,4,48,384]{3,2,1,0:T(8,128)(2,1)S(1)}, u32[]{:S(2)}, u32[]{:S(2)}) async-start(bf16[8,4,48,384]{3,2,1,0:T(8,128)(2,1)} %synthesise.4.refs_0_), calls=%async_computation.4 | async-start | bytes 2359296 | tf_op jit(solution)/shard_map/all_to_all | solution.py:623
  171.2 6.1 %analyse.7 = (bf16[304,384]{1,0:T(8,128)(2,1)}, bf16[304,384]{1,0:T(8,128)(2,1)}, bf16[304,384]{1,0:T(8,128)(2,1)}, bf16[304,384]{1,0:T(8,128)(2,1)}) custom-call(s32[4]{0:T(128)} %constant.137.clone.count_ref, s32[1]{0:T(128)} %bitcast.5.chan_ref, bf16[8,4,48,384]{3,2,1,0:T(8,128)(2,1)} %all-to-all-done.3.fourier_ref, ...), custom_call_target="tpu_custom_call" | custom-call | flops 1000 | bytes 1000 | tf_op jit(solution)/shard_map/analyse/pallas_call | solution.py:236
  177.3 4.8 %collective-permute-done.11.refs_2_ = bf16[400,384]{1,0:T(8,128)(2,1)S(1)} collective-permute-done((bf16[400,384]{1,0:T(8,128)(2,1)}, bf16[400,384]{1,0:T(8,128)(2,1)S(1)}, u32[]{:S(2)}, u32[]{:S(2)}) %collective-permute-start.11) | collective-permute-done | bytes 307232 | tf_op jit(solution)/shard_map/ppermute | solution.py:599
  185.6 17.3 %collective-permute-done.12.refs_3_ = bf16[400,384]{1,0:T(8,128)(2,1)S(1)} collective-permute-done((bf16[400,384]{1,0:T(8,128)(2,1)}, bf16[400,384]{1,0:T(8,128)(2,1)S(1)}, u32[]{:S(2)}, u32[]{:S(2)}) %collective-permute-start.12) | collective-permute-done | bytes 307232 | tf_op jit(solution)/shard_map/ppermute | solution.py:599
  205.0 8.6 %synthesise.5.refs_5_ = bf16[8,8,48,384]{3,2,1,0:T(8,128)(2,1)} custom-call(s32[2,8]{1,0:T(2,128)} %constant.138.clone.count_ref, s32[1]{0:T(128)} %bitcast.5.chan_ref, bf16[16,256,768]{2,1,0:T(8,128)(2,1)} %legendre_table.3.table_ref.refs_0_, bf16[2,384]{1,0:T(2,128)(2,1)} %constant.142.lanes_ref, bf16[400,384]{1,0:T(8,128)(2,1)} %get-tuple-element.108.refs_0_, ...), custom_call_target="tpu_custom_call" | custom-call | flops 10000000000 | bytes 1000 | tf_op jit(solution)/shard_map/synthesise/pallas_call | solution.py:542
  214.6 3.9 %all-to-all-start.5 = ((bf16[8,8,48,384]{3,2,1,0:T(8,128)(2,1)}), bf16[8,8,48,384]{3,2,1,0:T(8,128)(2,1)S(1)}, u32[]{:S(2)}, u32[]{:S(2)}) async-start(bf16[8,8,48,384]{3,2,1,0:T(8,128)(2,1)} %synthesise.5.refs_5_), calls=%async_computation.5 | async-start | bytes 4718592 | tf_op jit(solution)/shard_map/all_to_all | solution.py:623
  226.0 4.0 %mix.7 = (bf16[304,384]{1,0:T(8,128)(2,1)}, bf16[304,384]{1,0:T(8,128)(2,1)}, bf16[304,384]{1,0:T(8,128)(2,1)}, bf16[304,384]{1,0:T(8,128)(2,1)}) custom-call(s32[1]{0:T(128)} %bitcast.5.chan_ref, bf16[304,384]{1,0:T(8,128)(2,1)} %get-tuple-element.117.refs_4_.refs_0_, bf16[304,384]{1,0:T(8,128)(2,1)} %copy-done.15, bf16[304,384]{1,0:T(8,128)(2,1)} %copy-done.14, ...), custom_call_target="tpu_custom_call" | custom-call | flops 10000000000 | bytes 1000 | tf_op jit(solution)/shard_map/mix/pallas_call | solution.py:338
  231.5 3.9 %collective-permute-start.21 = (bf16[304,384]{1,0:T(8,128)(2,1)}, bf16[304,384]{1,0:T(8,128)(2,1)S(1)}, u32[]{:S(2)}, u32[]{:S(2)}) collective-permute-start(bf16[304,384]{1,0:T(8,128)(2,1)} %get-tuple-element.139), channel_id=1, source_target_pairs={{0,1},{1,2},{2,3},{3,0},{4,5},{5,6},{6,7},{7,4},{8,9},{9,10},{10,1... | collective-permute-start | bytes 700424 | tf_op jit(solution)/shard_map/ppermute | solution.py:599
  235.4 4.2 %collective-permute-start.22 = (bf16[304,384]{1,0:T(8,128)(2,1)}, bf16[304,384]{1,0:T(8,128)(2,1)S(1)}, u32[]{:S(2)}, u32[]{:S(2)}) collective-permute-start(bf16[304,384]{1,0:T(8,128)(2,1)} %get-tuple-element.141), channel_id=1, source_target_pairs={{0,2},{1,3},{2,0},{3,1},{4,6},{5,7},{6,4},{7,5},{8,10},{9,11},{10,... | collective-permute-start | bytes 700424 | tf_op jit(solution)/shard_map/ppermute | solution.py:599
  240.3 7.7 %synthesise.6.refs_4_ = bf16[8,8,48,384]{3,2,1,0:T(8,128)(2,1)} custom-call(s32[2,8]{1,0:T(2,128)} %constant.139.clone.count_ref, s32[1]{0:T(128)} %bitcast.5.chan_ref, bf16[16,256,768]{2,1,0:T(8,128)(2,1)} %legendre_table.3.table_ref.refs_0_, bf16[2,384]{1,0:T(2,128)(2,1)} %constant.142.lanes_ref, bf16[144,384]{1,0:T(8,128)(2,1)} %get-tuple-element.123.refs_5_.refs_0_, ...), custom_call_target="tpu_custom_call" | custom-call | flops 10000000000 | bytes 1000 | tf_op jit(solution)/shard_map/synthesise/pallas_call | solution.py:542
  249.4 4.4 %all-to-all-start.6 = ((bf16[8,8,48,384]{3,2,1,0:T(8,128)(2,1)}), bf16[8,8,48,384]{3,2,1,0:T(8,128)(2,1)}, u32[]{:S(2)}, u32[]{:S(2)}) async-start(bf16[8,8,48,384]{3,2,1,0:T(8,128)(2,1)} %synthesise.6.refs_4_), calls=%async_computation.6 | async-start | bytes 4718592 | tf_op jit(solution)/shard_map/all_to_all | solution.py:623
  255.6 3.7 %collective-permute-done.23.refs_3_ = bf16[304,384]{1,0:T(8,128)(2,1)S(1)} collective-permute-done((bf16[304,384]{1,0:T(8,128)(2,1)}, bf16[304,384]{1,0:T(8,128)(2,1)S(1)}, u32[]{:S(2)}, u32[]{:S(2)}) %collective-permute-start.23) | collective-permute-done | bytes 233504 | tf_op jit(solution)/shard_map/ppermute | solution.py:599
  260.0 5.6 %synthesise.7 = bf16[8,4,48,384]{3,2,1,0:T(8,128)(2,1)} custom-call(s32[2,4]{1,0:T(2,128)} %constant.140.clone.count_ref, s32[1]{0:T(128)} %bitcast.5.chan_ref, bf16[8,384,768]{2,1,0:T(8,128)(2,1)} %legendre_table.2.table_ref.refs_0_, bf16[2,384]{1,0:T(2,128)(2,1)} %constant.142.lanes_ref, bf16[304,384]{1,0:T(8,128)(2,1)} %get-tuple-element.136.refs_4_.refs_0_, ...), custom_call_target="tpu_custom_call" | custom-call | flops 199999995904 | bytes 1000 | tf_op jit(solution)/shard_map/synthesise/pallas_call | solution.py:542
  265.6 17.6 %all-to-all-done.6.refs_2_ = bf16[8,8,48,384]{3,2,1,0:T(8,128)(2,1)} async-done(((bf16[8,8,48,384]{3,2,1,0:T(8,128)(2,1)}), bf16[8,8,48,384]{3,2,1,0:T(8,128)(2,1)}, u32[]{:S(2)}, u32[]{:S(2)}) %all-to-all-start.6) | async-done | bytes 2359328 | tf_op jit(solution)/shard_map/all_to_all | solution.py:623
  291.5 10.5 %early_rows.1.early_ref = bf16[48,96,640]{2,1,0:T(8,128)(2,1)} custom-call(bf16[256,256]{1,0:T(8,128)(2,1)} %constant.141.swap_ref, bf16[8,4,48,384]{3,2,1,0:T(8,128)(2,1)} %copy-done.2, bf16[8,8,48,384]{3,2,1,0:T(8,128)(2,1)} %copy-done.1, bf16[8,8,48,384]{3,2,1,0:T(8,128)(2,1)} %all-to-all-done.6.refs_2_), custom_call_target="tpu_custom_call" | custom-call | flops 1000 | bytes 1000 | tf_op jit(solution)/shard_map/early_rows/pallas_call | solution.py:437
  304.6 21.6 %inverse_rows.1 = bf16[48,96,1440]{2,1,0:T(8,128)(2,1)} custom-call(bf16[768,1440]{1,0:T(8,128)(2,1)} %pad_maximum_fusion.1.synth_ref, bf16[256,256]{1,0:T(8,128)(2,1)} %constant.141.swap_ref, bf16[48,96,640]{2,1,0:T(8,128)(2,1)} %early_rows.1.early_ref, bf16[8,4,48,384]{3,2,1,0:T(8,128)(2,1)} %copy-done.4), custom_call_target="tpu_custom_call" | custom-call | flops 1000 | bytes 1000 | tf_op jit(solution)/shard_map/inverse_rows/pallas_call | solution.py:474
  (144 shorter events, 71.7 us)
Async XLA Ops:
  23.7 24.8 %all-to-all-start = ((bf16[8,4,48,384]{3,2,1,0:T(8,128)(2,1)}), bf16[8,4,48,384]{3,2,1,0:T(8,128)(2,1)S(1)}, u32[]{:S(2)}, u32[]{:S(2)}) async-start(bf16[8,4,48,384]{3,2,1,0:T(8,128)(2,1)} %get-tuple-element.79.refs_0_), calls=%async_computation | async-start | bytes 2359296 | tf_op jit(solution)/shard_map/all_to_all | solution.py:623
  56.0 28.9 %collective-permute-start = (bf16[368,384]{1,0:T(8,128)(2,1)}, bf16[368,384]{1,0:T(8,128)(2,1)}, u32[]{:S(2)}, u32[]{:S(2)}) collective-permute-start(bf16[368,384]{1,0:T(8,128)(2,1)} %get-tuple-element.83), channel_id=1, source_target_pairs={{0,1},{1,2},{2,3},{3,0},{4,5},{5,6},{6,7},{7,4},{8,9},{9,10},{10,1... | collective-permute-start | bytes 847880 | tf_op jit(solution)/shard_map/ppermute | solution.py:599
  57.6 27.3 %collective-permute-start.1 = (bf16[368,384]{1,0:T(8,128)(2,1)}, bf16[368,384]{1,0:T(8,128)(2,1)}, u32[]{:S(2)}, u32[]{:S(2)}) collective-permute-start(bf16[368,384]{1,0:T(8,128)(2,1)} %get-tuple-element.84), channel_id=1, source_target_pairs={{0,2},{1,3},{2,0},{3,1},{4,6},{5,7},{6,4},{7,5},{8,10},{9,11},{10,... | collective-permute-start | bytes 847880 | tf_op jit(solution)/shard_map/ppermute | solution.py:599
  58.5 26.4 %collective-permute-start.2 = (bf16[368,384]{1,0:T(8,128)(2,1)}, bf16[368,384]{1,0:T(8,128)(2,1)}, u32[]{:S(2)}, u32[]{:S(2)}) collective-permute-start(bf16[368,384]{1,0:T(8,128)(2,1)} %get-tuple-element.85), channel_id=1, source_target_pairs={{0,3},{1,0},{2,1},{3,2},{4,7},{5,4},{6,5},{7,6},{8,11},{9,8},{10,9... | collective-permute-start | bytes 847880 | tf_op jit(solution)/shard_map/ppermute | solution.py:599
  64.0 42.3 %all-to-all-start.1 = ((bf16[8,8,48,384]{3,2,1,0:T(8,128)(2,1)}), bf16[8,8,48,384]{3,2,1,0:T(8,128)(2,1)}, u32[]{:S(2)}, u32[]{:S(2)}) async-start(bf16[8,8,48,384]{3,2,1,0:T(8,128)(2,1)} %get-tuple-element.95), calls=%async_computation.1 | async-start | bytes 4718592 | tf_op jit(solution)/shard_map/all_to_all | solution.py:623
  89.1 35.4 %collective-permute-start.5 = (bf16[368,384]{1,0:T(8,128)(2,1)}, bf16[368,384]{1,0:T(8,128)(2,1)}, u32[]{:S(2)}, u32[]{:S(2)}) collective-permute-start(bf16[368,384]{1,0:T(8,128)(2,1)} %get-tuple-element.93), channel_id=1, source_target_pairs={{0,3},{1,0},{2,1},{3,2},{4,7},{5,4},{6,5},{7,6},{8,11},{9,8},{10,9... | collective-permute-start | bytes 847880 | tf_op jit(solution)/shard_map/ppermute | solution.py:599
  90.8 29.1 %collective-permute-start.4 = (bf16[368,384]{1,0:T(8,128)(2,1)}, bf16[368,384]{1,0:T(8,128)(2,1)}, u32[]{:S(2)}, u32[]{:S(2)}) collective-permute-start(bf16[368,384]{1,0:T(8,128)(2,1)} %get-tuple-element.91), channel_id=1, source_target_pairs={{0,2},{1,3},{2,0},{3,1},{4,6},{5,7},{6,4},{7,5},{8,10},{9,11},{10,... | collective-permute-start | bytes 847880 | tf_op jit(solution)/shard_map/ppermute | solution.py:599
  90.9 33.7 %collective-permute-start.3 = (bf16[368,384]{1,0:T(8,128)(2,1)}, bf16[368,384]{1,0:T(8,128)(2,1)}, u32[]{:S(2)}, u32[]{:S(2)}) collective-permute-start(bf16[368,384]{1,0:T(8,128)(2,1)} %get-tuple-element.89), channel_id=1, source_target_pairs={{0,1},{1,2},{2,3},{3,0},{4,5},{5,6},{6,7},{7,4},{8,9},{9,10},{10,1... | collective-permute-start | bytes 847880 | tf_op jit(solution)/shard_map/ppermute | solution.py:599
  106.3 33.8 %all-to-all-start.2 = ((bf16[8,8,48,384]{3,2,1,0:T(8,128)(2,1)}), bf16[8,8,48,384]{3,2,1,0:T(8,128)(2,1)}, u32[]{:S(2)}, u32[]{:S(2)}) async-start(bf16[8,8,48,384]{3,2,1,0:T(8,128)(2,1)} %get-tuple-element.98.refs_5_), calls=%async_computation.2 | async-start | bytes 4718592 | tf_op jit(solution)/shard_map/all_to_all | solution.py:623
  119.9 34.4 %collective-permute-start.8 = (bf16[400,384]{1,0:T(8,128)(2,1)}, bf16[400,384]{1,0:T(8,128)(2,1)}, u32[]{:S(2)}, u32[]{:S(2)}) collective-permute-start(bf16[400,384]{1,0:T(8,128)(2,1)} %get-tuple-element.106), channel_id=1, source_target_pairs={{0,3},{1,0},{2,1},{3,2},{4,7},{5,4},{6,5},{7,6},{8,11},{9,8},{10,9... | collective-permute-start | bytes 921608 | tf_op jit(solution)/shard_map/ppermute | solution.py:599
  119.9 32.5 %collective-permute-start.7 = (bf16[400,384]{1,0:T(8,128)(2,1)}, bf16[400,384]{1,0:T(8,128)(2,1)}, u32[]{:S(2)}, u32[]{:S(2)}) collective-permute-start(bf16[400,384]{1,0:T(8,128)(2,1)} %get-tuple-element.104), channel_id=1, source_target_pairs={{0,2},{1,3},{2,0},{3,1},{4,6},{5,7},{6,4},{7,5},{8,10},{9,11},{10,... | collective-permute-start | bytes 921608 | tf_op jit(solution)/shard_map/ppermute | solution.py:599
  122.4 31.9 %collective-permute-start.6 = (bf16[400,384]{1,0:T(8,128)(2,1)}, bf16[400,384]{1,0:T(8,128)(2,1)}, u32[]{:S(2)}, u32[]{:S(2)}) collective-permute-start(bf16[400,384]{1,0:T(8,128)(2,1)} %get-tuple-element.102), channel_id=1, source_target_pairs={{0,1},{1,2},{2,3},{3,0},{4,5},{5,6},{6,7},{7,4},{8,9},{9,10},{10,1... | collective-permute-start | bytes 921608 | tf_op jit(solution)/shard_map/ppermute | solution.py:599
  140.2 25.1 %all-to-all-start.3 = ((bf16[8,4,48,384]{3,2,1,0:T(8,128)(2,1)}), bf16[8,4,48,384]{3,2,1,0:T(8,128)(2,1)}, u32[]{:S(2)}, u32[]{:S(2)}) async-start(bf16[8,4,48,384]{3,2,1,0:T(8,128)(2,1)} %get-tuple-element.99), calls=%async_computation.3 | async-start | bytes 2359296 | tf_op jit(solution)/shard_map/all_to_all | solution.py:623
  152.5 7.3 %collective-permute-start.9 = (bf16[144,384]{1,0:T(8,128)(2,1)}, bf16[144,384]{1,0:T(8,128)(2,1)}, u32[]{:S(2)}, u32[]{:S(2)}) collective-permute-start(bf16[144,384]{1,0:T(8,128)(2,1)} %get-tuple-element.111), channel_id=1, source_target_pairs={{0,2},{1,3},{2,0},{3,1},{4,6},{5,7},{6,4},{7,5},{8,10},{9,11},{10,... | collective-permute-start | bytes 331784 | tf_op jit(solution)/shard_map/ppermute | solution.py:599
  159.8 22.3 %collective-permute-start.11 = (bf16[400,384]{1,0:T(8,128)(2,1)}, bf16[400,384]{1,0:T(8,128)(2,1)S(1)}, u32[]{:S(2)}, u32[]{:S(2)}) collective-permute-start(bf16[400,384]{1,0:T(8,128)(2,1)} %get-tuple-element.114), channel_id=1, source_target_pairs={{0,2},{1,3},{2,0},{3,1},{4,6},{5,7},{6,4},{7,5},{8,10},{9,11},{10,... | collective-permute-start | bytes 921608 | tf_op jit(solution)/shard_map/ppermute | solution.py:599
  163.2 39.8 %collective-permute-start.12 = (bf16[400,384]{1,0:T(8,128)(2,1)}, bf16[400,384]{1,0:T(8,128)(2,1)S(1)}, u32[]{:S(2)}, u32[]{:S(2)}) collective-permute-start(bf16[400,384]{1,0:T(8,128)(2,1)} %get-tuple-element.116), channel_id=1, source_target_pairs={{0,3},{1,0},{2,1},{3,2},{4,7},{5,4},{6,5},{7,6},{8,11},{9,8},{10,9... | collective-permute-start | bytes 921608 | tf_op jit(solution)/shard_map/ppermute | solution.py:599
  163.2 39.8 %collective-permute-start.10 = (bf16[400,384]{1,0:T(8,128)(2,1)}, bf16[400,384]{1,0:T(8,128)(2,1)S(1)}, u32[]{:S(2)}, u32[]{:S(2)}) collective-permute-start(bf16[400,384]{1,0:T(8,128)(2,1)} %get-tuple-element.112), channel_id=1, source_target_pairs={{0,1},{1,2},{2,3},{3,0},{4,5},{5,6},{6,7},{7,4},{8,9},{9,10},{10,1... | collective-permute-start | bytes 921608 | tf_op jit(solution)/shard_map/ppermute | solution.py:599
  165.2 48.3 %all-to-all-start.4 = ((bf16[8,4,48,384]{3,2,1,0:T(8,128)(2,1)}), bf16[8,4,48,384]{3,2,1,0:T(8,128)(2,1)S(1)}, u32[]{:S(2)}, u32[]{:S(2)}) async-start(bf16[8,4,48,384]{3,2,1,0:T(8,128)(2,1)} %synthesise.4.refs_0_), calls=%async_computation.4 | async-start | bytes 2359296 | tf_op jit(solution)/shard_map/all_to_all | solution.py:623
  169.1 49.4 %collective-permute-start.14 = (bf16[144,384]{1,0:T(8,128)(2,1)S(1)}, bf16[144,384]{1,0:T(8,128)(2,1)S(1)}, u32[]{:S(2)}, u32[]{:S(2)}) collective-permute-start(bf16[144,384]{1,0:T(8,128)(2,1)S(1)} %copy-done.21), channel_id=1, source_target_pairs={{0,3},{1,0},{2,1},{3,2},{4,7},{5,4},{6,5},{7,6},{8,11},{9,8},{10,9... | collective-permute-start | bytes 331784 | tf_op jit(solution)/shard_map/ppermute | solution.py:599
  169.2 49.4 %collective-permute-start.13 = (bf16[144,384]{1,0:T(8,128)(2,1)S(1)}, bf16[144,384]{1,0:T(8,128)(2,1)S(1)}, u32[]{:S(2)}, u32[]{:S(2)}) collective-permute-start(bf16[144,384]{1,0:T(8,128)(2,1)S(1)} %copy-done.20), channel_id=1, source_target_pairs={{0,1},{1,2},{2,3},{3,0},{4,5},{5,6},{6,7},{7,4},{8,9},{9,10},{10,1... | collective-permute-start | bytes 331784 | tf_op jit(solution)/shard_map/ppermute | solution.py:599
  182.1 40.8 %collective-permute-start.15 = (bf16[304,384]{1,0:T(8,128)(2,1)}, bf16[304,384]{1,0:T(8,128)(2,1)S(1)}, u32[]{:S(2)}, u32[]{:S(2)}) collective-permute-start(bf16[304,384]{1,0:T(8,128)(2,1)} %get-tuple-element.126), channel_id=1, source_target_pairs={{0,2},{1,3},{2,0},{3,1},{4,6},{5,7},{6,4},{7,5},{8,10},{9,11},{10,... | collective-permute-start | bytes 700424 | tf_op jit(solution)/shard_map/ppermute | solution.py:599
  202.9 22.3 %collective-permute-start.19 = (bf16[304,384]{1,0:T(8,128)(2,1)}, bf16[304,384]{1,0:T(8,128)(2,1)S(1)}, u32[]{:S(2)}, u32[]{:S(2)}) collective-permute-start(bf16[304,384]{1,0:T(8,128)(2,1)} %get-tuple-element.133), channel_id=1, source_target_pairs={{0,1},{1,2},{2,3},{3,0},{4,5},{5,6},{6,7},{7,4},{8,9},{9,10},{10,1... | collective-permute-start | bytes 700424 | tf_op jit(solution)/shard_map/ppermute | solution.py:599
  203.0 22.3 %collective-permute-start.20 = (bf16[304,384]{1,0:T(8,128)(2,1)}, bf16[304,384]{1,0:T(8,128)(2,1)S(1)}, u32[]{:S(2)}, u32[]{:S(2)}) collective-permute-start(bf16[304,384]{1,0:T(8,128)(2,1)} %get-tuple-element.135), channel_id=1, source_target_pairs={{0,3},{1,0},{2,1},{3,2},{4,7},{5,4},{6,5},{7,6},{8,11},{9,8},{10,9... | collective-permute-start | bytes 700424 | tf_op jit(solution)/shard_map/ppermute | solution.py:599
  214.6 33.3 %all-to-all-start.5 = ((bf16[8,8,48,384]{3,2,1,0:T(8,128)(2,1)}), bf16[8,8,48,384]{3,2,1,0:T(8,128)(2,1)S(1)}, u32[]{:S(2)}, u32[]{:S(2)}) async-start(bf16[8,8,48,384]{3,2,1,0:T(8,128)(2,1)} %synthesise.5.refs_5_), calls=%async_computation.5 | async-start | bytes 4718592 | tf_op jit(solution)/shard_map/all_to_all | solution.py:623
  222.9 16.7 %collective-permute-start.18 = (bf16[144,384]{1,0:T(8,128)(2,1)}, bf16[144,384]{1,0:T(8,128)(2,1)S(1)}, u32[]{:S(2)}, u32[]{:S(2)}) collective-permute-start(bf16[144,384]{1,0:T(8,128)(2,1)} %get-tuple-element.131), channel_id=1, source_target_pairs={{0,3},{1,0},{2,1},{3,2},{4,7},{5,4},{6,5},{7,6},{8,11},{9,8},{10,9... | collective-permute-start | bytes 331784 | tf_op jit(solution)/shard_map/ppermute | solution.py:599
  223.7 7.8 %collective-permute-start.17 = (bf16[144,384]{1,0:T(8,128)(2,1)}, bf16[144,384]{1,0:T(8,128)(2,1)S(1)}, u32[]{:S(2)}, u32[]{:S(2)}) collective-permute-start(bf16[144,384]{1,0:T(8,128)(2,1)} %get-tuple-element.129), channel_id=1, source_target_pairs={{0,2},{1,3},{2,0},{3,1},{4,6},{5,7},{6,4},{7,5},{8,10},{9,11},{10,... | collective-permute-start | bytes 331784 | tf_op jit(solution)/shard_map/ppermute | solution.py:599
  224.5 15.1 %collective-permute-start.16 = (bf16[144,384]{1,0:T(8,128)(2,1)}, bf16[144,384]{1,0:T(8,128)(2,1)S(1)}, u32[]{:S(2)}, u32[]{:S(2)}) collective-permute-start(bf16[144,384]{1,0:T(8,128)(2,1)} %get-tuple-element.127), channel_id=1, source_target_pairs={{0,1},{1,2},{2,3},{3,0},{4,5},{5,6},{6,7},{7,4},{8,9},{9,10},{10,1... | collective-permute-start | bytes 331784 | tf_op jit(solution)/shard_map/ppermute | solution.py:599
  231.5 22.3 %collective-permute-start.21 = (bf16[304,384]{1,0:T(8,128)(2,1)}, bf16[304,384]{1,0:T(8,128)(2,1)S(1)}, u32[]{:S(2)}, u32[]{:S(2)}) collective-permute-start(bf16[304,384]{1,0:T(8,128)(2,1)} %get-tuple-element.139), channel_id=1, source_target_pairs={{0,1},{1,2},{2,3},{3,0},{4,5},{5,6},{6,7},{7,4},{8,9},{9,10},{10,1... | collective-permute-start | bytes 700424 | tf_op jit(solution)/shard_map/ppermute | solution.py:599
  235.4 20.2 %collective-permute-start.22 = (bf16[304,384]{1,0:T(8,128)(2,1)}, bf16[304,384]{1,0:T(8,128)(2,1)S(1)}, u32[]{:S(2)}, u32[]{:S(2)}) collective-permute-start(bf16[304,384]{1,0:T(8,128)(2,1)} %get-tuple-element.141), channel_id=1, source_target_pairs={{0,2},{1,3},{2,0},{3,1},{4,6},{5,7},{6,4},{7,5},{8,10},{9,11},{10,... | collective-permute-start | bytes 700424 | tf_op jit(solution)/shard_map/ppermute | solution.py:599
  239.6 19.7 %collective-permute-start.23 = (bf16[304,384]{1,0:T(8,128)(2,1)}, bf16[304,384]{1,0:T(8,128)(2,1)S(1)}, u32[]{:S(2)}, u32[]{:S(2)}) collective-permute-start(bf16[304,384]{1,0:T(8,128)(2,1)} %get-tuple-element.143), channel_id=1, source_target_pairs={{0,3},{1,0},{2,1},{3,2},{4,7},{5,4},{6,5},{7,6},{8,11},{9,8},{10,9... | collective-permute-start | bytes 700424 | tf_op jit(solution)/shard_map/ppermute | solution.py:599
  249.4 33.8 %all-to-all-start.6 = ((bf16[8,8,48,384]{3,2,1,0:T(8,128)(2,1)}), bf16[8,8,48,384]{3,2,1,0:T(8,128)(2,1)}, u32[]{:S(2)}, u32[]{:S(2)}) async-start(bf16[8,8,48,384]{3,2,1,0:T(8,128)(2,1)} %synthesise.6.refs_4_), calls=%async_computation.6 | async-start | bytes 4718592 | tf_op jit(solution)/shard_map/all_to_all | solution.py:623
  283.2 20.3 %all-to-all-start.7 = ((bf16[8,4,48,384]{3,2,1,0:T(8,128)(2,1)}), bf16[8,4,48,384]{3,2,1,0:T(8,128)(2,1)S(1)}, u32[]{:S(2)}, u32[]{:S(2)}) async-start(bf16[8,4,48,384]{3,2,1,0:T(8,128)(2,1)} %synthesise.7), calls=%async_computation.7 | async-start | bytes 2359296 | tf_op jit(solution)/shard_map/all_to_all | solution.py:623
  (27 other events, 141.6 us)
